TPU v7x, 256 devices: a whole 4x4x8 slice. The times are simulated.
256 devices in a mesh: atoms: 32 (over z, x), aux: 8 (over y, core).
Axes of the slice: x: 4, y: 4, z: 8, core: 2. Of those that a mesh axis runs over, the one named last changes fastest.
Arguments:
- factors: bfloat16 [32, 48, 512, 512], P('atoms', 'aux'), may hold values from -0.25 to 0.25
- density: bfloat16 [32, 2, 512, 512], P('atoms'), may hold values from -2 to 2
- screen: int32 [32, 2], P('atoms'), may hold values from 0 to 1, as said below
Outputs:
- exchange: float32 [32, 4, 512, 512], P('atoms', None, 'aux')
Inputs may be any that keep to these rules, and one draw needn't show every extreme that they name: `screen`: entry [a, o] is 1 where the pair of atom blocks a and a + o + 1 survives screening and 0 where a + o + 1 >= 32; atom block 2 keeps all its pairs with blocks 0 to 4.
All inputs are finite; a program needn't handle non-finite values.
Results may differ from a plain program's by a relative error of at most 0.0029.
Values may be sent and summed in bfloat16 or wider, within the bound.
No kernel may reach another device: no remote copies, remote signals or barrier semaphores. Data moves between devices by JAX's collectives and lax.ppermute only.
A program may use at most 64 MiB of HBM per device.

v0:
```python
import jax
import jax.numpy as jnp
from jax import lax
from jax.experimental import pallas as pl
from jax.experimental.pallas import tpu as pltpu
from jax.sharding import PartitionSpec as P


F32, BF16 = jnp.float32, jnp.bfloat16
VMEM = pl.BlockSpec(memory_space=pltpu.VMEM)
SMEM = pl.BlockSpec(memory_space=pltpu.SMEM)
LANES = 128
ROWS, PARTS = 64, 8
CHUNKS = ((0, 16), (32, 32), (16, 16))
EARLY, LATE = 384, 128
EARLY_U1, EARLY_U2, EARLY_ALL = 192, 144, 672
LATE_U1, LATE_U2, LATE_ALL = 64, 112, 352


def params(limit=20):
    return pltpu.CompilerParams(vmem_limit_bytes=limit * 1024 * 1024)


def cost(flops, size):
    return pl.CostEstimate(flops=flops, bytes_accessed=size, transcendentals=0)


def shift(value, axis, steps):
    count = lax.axis_size(axis)
    return lax.ppermute(value, axis, [(i, i + steps) for i in range(count) if 0 <= i + steps < count])


def swap_core(value):
    return lax.ppermute(value, "aux", [(i, i ^ 1) for i in range(lax.axis_size("aux"))])


def shift_y(value, steps):
    count = lax.axis_size("aux")
    return lax.ppermute(value, "aux", [(i, (i + 2 * steps) % count) for i in range(count)])


def split(factors, density, screen, start, size):
    count, width = factors.shape[0], factors.shape[-1]
    height = PARTS * size

    def kernel(flag, left, right, piece, far):
        value = left[0].reshape(height, width)
        piece[...] = value
        product = jnp.dot(value, right[0], preferred_element_type=F32).astype(BF16)
        far[...] = product * flag[0, 1].astype(F32).astype(BF16)

    return pl.pallas_call(
        kernel,
        grid=(count,),
        in_specs=[
            SMEM,
            pl.BlockSpec((1, PARTS, size, width), lambda i: (i, 0, start // size, 0)),
            pl.BlockSpec((1, width, width), lambda i: (1, 0, 0)),
        ],
        out_specs=[pl.BlockSpec((height, width), lambda i: (0, i))] * 2,
        out_shape=[jax.ShapeDtypeStruct((height, count * width), BF16)] * 2,
        cost_estimate=cost(2 * height * count * width**2, 6 * height * count * width),
    )(screen, factors, density)


def transform(factors, density, screen):
    count, width = factors.shape[0], factors.shape[-1]

    def kernel(flag, left, right, out):
        product = jnp.dot(left[0].reshape(width, width), right[0], preferred_element_type=F32).astype(BF16)
        out[...] = product * flag[0, 0].astype(F32).astype(BF16)

    return pl.pallas_call(
        kernel,
        grid=(count,),
        in_specs=[
            SMEM,
            pl.BlockSpec((1, PARTS, ROWS, width), lambda i: (i, 0, 0, 0)),
            pl.BlockSpec((1, width, width), lambda i: (0, 0, 0)),
        ],
        out_specs=pl.BlockSpec((width, width), lambda i: (0, i)),
        out_shape=jax.ShapeDtypeStruct((width, count * width), BF16),
        compiler_params=params(),
        cost_estimate=cost(2 * count * width**3, 4 * count * width**2),
    )(screen, factors, density)


def contract(left, right):
    return lax.dot_general(left, right, (((1,), (1,)), ((), ())), preferred_element_type=F32)


def early_rows(ref, part, columns):
    low = ref[pl.ds(pl.multiple_of(16 * part, 16), 16), columns]
    high = ref[pl.ds(pl.multiple_of(128 + 32 * part, 32), 32), columns]
    return low, high


def late_rows(ref, part, columns):
    return ref[pl.ds(pl.multiple_of(16 * part, 16), 16), columns]


def put(out, y, offset, values):
    for value in values:
        out[y, pl.ds(offset, value.shape[0]), :] = value.astype(out.dtype)
        offset += value.shape[0]
    return offset


def lanes(index):
    return pl.ds(index * LANES, LANES)


def pack_early(place, near, ahead, behind):
    width = near.shape[0]
    places = PARTS // 2

    def kernel(place, near, ahead0, ahead1, behind0, behind1, kept, sent, upper, lower, upper_far, lower_far):
        offset = 0
        for right in (ahead0, ahead1):
            columns = pl.ds(offset, right.shape[0])
            value = contract(near[...], right[...])
            upper[:, columns] = value
            lower[columns, :] = value.T
            row = 0
            for left in (behind0, behind1):
                value = contract(left[...], right[...])
                upper_far[pl.ds(row, left.shape[0]), columns] = value
                lower_far[columns, pl.ds(row, left.shape[0])] = value.T
                row += left.shape[0]
            offset += right.shape[0]
        for y in range(places):
            for out, core in ((sent, 1 - place[0]), (kept, place[0])):
                part = 2 * y + core
                own = pl.ds(pl.multiple_of(ROWS * part, ROWS), ROWS)
                at = put(out, y, 0, [upper[own, lanes(t)] for t in range(3)])
                for t in range(3):
                    at = put(out, y, at, early_rows(upper_far, part, lanes(t)))
                for t in range(4):
                    at = put(out, y, at, early_rows(lower, part, lanes(t)))
                for t in range(3):
                    at = put(out, y, at, early_rows(lower_far, part, lanes(t)))

    shape = (places, EARLY_ALL, LANES)
    return pl.pallas_call(
        kernel,
        in_specs=[SMEM] + [VMEM] * 5,
        out_specs=[VMEM] * 2,
        out_shape=[jax.ShapeDtypeStruct(shape, F32), jax.ShapeDtypeStruct(shape, BF16)],
        scratch_shapes=[
            pltpu.VMEM((width, EARLY), F32),
            pltpu.VMEM((EARLY, width), F32),
            pltpu.VMEM((EARLY, EARLY), F32),
            pltpu.VMEM((EARLY, EARLY), F32),
        ],
        compiler_params=params(),
        cost_estimate=cost(2 * near.size * EARLY * 2, near.size * 4),
    )(place, near, *ahead, *behind)


def pack_late(place, near, ahead, behind):
    width = near.shape[0]
    places = PARTS // 2

    def kernel(place, near, ahead0, ahead1, ahead2, behind0, behind1, behind2, kept, sent, upper, lower, tall, wide, tall_t, wide_t):
        value = contract(near[...], ahead2[...])
        upper[...] = value
        lower[...] = value.T
        offset = 0
        for left, right in ((behind0, ahead0), (behind1, ahead1)):
            span = pl.ds(offset, left.shape[0])
            value = contract(left[...], ahead2[...])
            tall[span, :] = value
            wide_t[:, span] = value.T
            value = contract(behind2[...], right[...])
            wide[:, span] = value
            tall_t[span, :] = value.T
            offset += left.shape[0]
        value = contract(behind2[...], ahead2[...])
        wide[:, pl.ds(EARLY, LATE)] = value
        wide_t[:, pl.ds(EARLY, LATE)] = value.T
        for y in range(places):
            for out, core in ((sent, 1 - place[0]), (kept, place[0])):
                part = 2 * y + core
                own = pl.ds(pl.multiple_of(ROWS * part, ROWS), ROWS)
                at = put(out, y, 0, [upper[own, :]])
                at = put(out, y, at, early_rows(tall, part, lanes(0)))
                at = put(out, y, at, [late_rows(wide, part, lanes(t)) for t in range(4)])
                at = put(out, y, at, [late_rows(lower, part, lanes(t)) for t in range(4)])
                at = put(out, y, at, early_rows(tall_t, part, lanes(0)))
                at = put(out, y, at, [late_rows(wide_t, part, lanes(t)) for t in range(4)])

    shape = (places, LATE_ALL, LANES)
    return pl.pallas_call(
        kernel,
        in_specs=[SMEM] + [VMEM] * 7,
        out_specs=[VMEM] * 2,
        out_shape=[jax.ShapeDtypeStruct(shape, F32), jax.ShapeDtypeStruct(shape, BF16)],
        scratch_shapes=[
            pltpu.VMEM((width, LATE), F32),
            pltpu.VMEM((LATE, width), F32),
            pltpu.VMEM((EARLY, LATE), F32),
            pltpu.VMEM((LATE, width), F32),
            pltpu.VMEM((EARLY, LATE), F32),
            pltpu.VMEM((LATE, width), F32),
        ],
        compiler_params=params(),
        cost_estimate=cost(2 * near.size * LATE * 3, near.size * 6),
    )(place, near, *ahead, *behind)


def join_core(place, kept, received):
    places, rows, width = kept.shape

    def kernel(place, kept, received, total, *pieces):
        y = place[1]
        total[...] = kept[y] + received[y].astype(F32)
        for steps in range(1, places):
            target = lax.rem(y + steps, places)
            pieces[steps - 1][...] = (kept[target] + received[target].astype(F32)).astype(BF16)

    shape = (rows, width)
    return pl.pallas_call(
        kernel,
        in_specs=[SMEM, VMEM, VMEM],
        out_specs=[VMEM] * places,
        out_shape=[jax.ShapeDtypeStruct(shape, F32)] + [jax.ShapeDtypeStruct(shape, BF16)] * (places - 1),
        compiler_params=params(),
        cost_estimate=cost(kept.size, 8 * kept.size),
    )(place, kept, received)


def join_places(total, received, first, second):
    rows, width = total.shape
    sizes = (first, second, rows - first - second)

    def kernel(total, one, two, three, *outs):
        offset = 0
        for out, size in zip(outs, sizes):
            span = pl.ds(offset, size)
            value = total[span, :] + one[span, :].astype(F32) + two[span, :].astype(F32) + three[span, :].astype(F32)
            out[...] = value.astype(out.dtype)
            offset += size

    return pl.pallas_call(
        kernel,
        in_specs=[VMEM] * 4,
        out_specs=[VMEM] * 3,
        out_shape=[jax.ShapeDtypeStruct((size, width), dtype) for size, dtype in zip(sizes, (F32, BF16, BF16))],
        compiler_params=params(),
        cost_estimate=cost(total.size * 3, 12 * total.size),
    )(total, *received)


def after(value, *others):
    return lax.optimization_barrier((value, *others))[0]


def send_places(pieces):
    received = []
    for steps in (2, 1, 3):
        received.append(shift_y(pieces[steps - 1], steps))
    return received


def hop(upper, upper_far, lower):
    return upper, shift(upper_far, "atoms", -1), shift(lower, "atoms", 1)


def assemble(order, early, late):
    width = order.shape[0]

    def far(early, late, base, late_base):
        chunks = []
        blocks = [early[pl.ds(base + 48 * t, 48), :] for t in range(3)]
        blocks.append(late[pl.ds(late_base, 48), :])
        body = jnp.concatenate(blocks, axis=1)
        last = jnp.concatenate([late[pl.ds(late_base + 48 + 16 * t, 16), :] for t in range(4)], axis=1)
        chunks = [body[:16], last, body[16:]]
        return jnp.concatenate(chunks, axis=0)

    def kernel(order, upper0, far0, lower0, upper1, far1, lower1, out):
        exact = order[...]
        blocks = [upper0[pl.ds(ROWS * t, ROWS), :] for t in range(3)] + [upper1[...]]
        value = jnp.concatenate(blocks, axis=1)
        out[0, 0] = jnp.dot(value, exact.astype(F32), preferred_element_type=F32, precision=lax.Precision.HIGHEST)
        out[0, 1] = jnp.dot(far(far0, far1, 0, 0), exact, preferred_element_type=F32)
        for t in range(4):
            out[0, 2, pl.ds(0, 16), lanes(t)] = lower0[pl.ds(48 * t, 16), :].astype(F32)
            out[0, 2, pl.ds(16, 16), lanes(t)] = lower1[pl.ds(16 * t, 16), :].astype(F32)
            out[0, 2, pl.ds(32, 32), lanes(t)] = lower0[pl.ds(48 * t + 16, 32), :].astype(F32)
        out[0, 3] = jnp.dot(far(lower0, lower1, 192, 64), exact, preferred_element_type=F32)

    return pl.pallas_call(
        kernel,
        in_specs=[VMEM] * 7,
        out_specs=VMEM,
        out_shape=jax.ShapeDtypeStruct((1, 4, ROWS, width), F32),
        compiler_params=params(),
        cost_estimate=cost(2 * 8 * ROWS * width**2, 4 * ROWS * width * 8),
    )(order, *early, *late)


def natural_order(width):
    index = jnp.arange(width)
    low = ROWS * (index // 16) + index % 16
    high = ROWS * ((index - 128) // 32) + 32 + index % 32
    last = ROWS * ((index - EARLY) // 16) + 16 + index % 16
    place = jnp.where(index < 128, low, jnp.where(index < EARLY, high, last))
    return (place[:, None] == jnp.arange(width)[None, :]).astype(BF16)


def body(factors, density, screen):
    count, width = factors.shape[1], factors.shape[2]
    owned, blocks = factors[0].reshape(count, PARTS, ROWS, width), density[0]
    position = lax.axis_index("aux")
    place = jnp.stack([position % 2, position // 2]).astype(jnp.int32)
    ahead, behind = [], []
    source = owned
    for start, size in CHUNKS:
        piece, far = split(source, blocks, screen, start, size)
        source = after(owned, piece)
        ahead.append(shift(piece, "atoms", -1))
        behind.append(shift(far, "atoms", 1))
    near = transform(source, blocks, screen)
    kept, sent = pack_early(place, near, ahead[:2], behind[:2])
    total, *pieces = join_core(place, kept, swap_core(sent))
    received = send_places(pieces)
    kept, sent = pack_late(after(place, *pieces), near, ahead, behind)
    late_total, *late_pieces = join_core(place, kept, swap_core(sent))
    late_received = send_places(late_pieces)
    early = hop(*join_places(after(total, *late_pieces), received, EARLY_U1, EARLY_U2))
    late = hop(*join_places(late_total, late_received, LATE_U1, LATE_U2))
    return assemble(natural_order(width), early, late)


def solution(mesh):
    in_specs = (P("atoms", "aux", None, None), P("atoms", None, None, None), P("atoms", None))
    out_specs = P("atoms", None, "aux", None)
    return jax.shard_map(body, mesh=mesh, in_specs=in_specs, out_specs=out_specs, check_vma=False)
```

profile of v0, /device:TPU:102, one launch (start us, length us, event | category | flops | bytes accessed | tf_op | source)
XLA Modules:
  0.0 137.3 jit_solution(13217044066302821712)
XLA Ops:
  0.0 5.1 %shard_map.37 = (bf16[128,3072]{1,0:T(8,128)(2,1)}, bf16[128,3072]{1,0:T(8,128)(2,1)}) custom-call(s32[1,2]{1,0:T(1,128)} %flag.7, bf16[6,8,64,512]{3,2,1,0:T(8,128)(2,1)} %bitcast.4, bf16[2,512,512]{2,1,0:T(8,128)(2,1)} %bitcast.8), custom_call_target="tpu_custom_call" | custom-call | flops 402653184 | bytes 2359296 | tf_op jit(solution)/shard_map/pallas_call | solution.py:52
  5.1 5.7 %shard_map.38 = (bf16[256,3072]{1,0:T(8,128)(2,1)}, bf16[256,3072]{1,0:T(8,128)(2,1)}) custom-call(s32[1,2]{1,0:T(1,128)} %flag.7, bf16[6,8,64,512]{3,2,1,0:T(8,128)(2,1)} %bitcast.5, bf16[2,512,512]{2,1,0:T(8,128)(2,1)} %bitcast.9), custom_call_target="tpu_custom_call" | custom-call | flops 805306368 | bytes 4718592 | tf_op jit(solution)/shard_map/pallas_call | solution.py:52
  10.9 2.7 %collective-permute-start.1 = (bf16[256,3072]{1,0:T(8,128)(2,1)}, bf16[256,3072]{1,0:T(8,128)(2,1)}, u32[]{:S(2)}, u32[]{:S(2)}) collective-permute-start(bf16[256,3072]{1,0:T(8,128)(2,1)} %get-tuple-element.36), channel_id=1, source_target_pairs={{8,0},{16,8},{24,16},{32,24},{40,32},{48,40},{56,48},{64,56},{72,6... | collective-permute-start | bytes 4718600 | tf_op jit(solution)/shard_map/ppermute | solution.py:30
  13.6 6.4 %collective-permute-start.3 = (bf16[256,3072]{1,0:T(8,128)(2,1)}, bf16[256,3072]{1,0:T(8,128)(2,1)}, u32[]{:S(2)}, u32[]{:S(2)}) collective-permute-start(bf16[256,3072]{1,0:T(8,128)(2,1)} %get-tuple-element.41), channel_id=1, source_target_pairs={{0,8},{8,16},{16,24},{24,32},{32,40},{40,48},{48,56},{56,64},{64,7... | collective-permute-start | bytes 4718600 | tf_op jit(solution)/shard_map/ppermute | solution.py:30
  20.0 1.9 %collective-permute-start = (bf16[128,3072]{1,0:T(8,128)(2,1)}, bf16[128,3072]{1,0:T(8,128)(2,1)}, u32[]{:S(2)}, u32[]{:S(2)}) collective-permute-start(bf16[128,3072]{1,0:T(8,128)(2,1)} %get-tuple-element.34), channel_id=1, source_target_pairs={{8,0},{16,8},{24,16},{32,24},{40,32},{48,40},{56,48},{64,56},{72,6... | collective-permute-start | bytes 2359304 | tf_op jit(solution)/shard_map/ppermute | solution.py:30
  22.0 7.5 %collective-permute-start.2 = (bf16[128,3072]{1,0:T(8,128)(2,1)}, bf16[128,3072]{1,0:T(8,128)(2,1)}, u32[]{:S(2)}, u32[]{:S(2)}) collective-permute-start(bf16[128,3072]{1,0:T(8,128)(2,1)} %get-tuple-element.40), channel_id=1, source_target_pairs={{0,8},{8,16},{16,24},{24,32},{32,40},{40,48},{48,56},{56,64},{64,7... | collective-permute-start | bytes 2359304 | tf_op jit(solution)/shard_map/ppermute | solution.py:30
  29.5 5.2 %shard_map.39 = (bf16[128,3072]{1,0:T(8,128)(2,1)}, bf16[128,3072]{1,0:T(8,128)(2,1)}) custom-call(s32[1,2]{1,0:T(1,128)} %flag.7, bf16[6,8,64,512]{3,2,1,0:T(8,128)(2,1)} %bitcast.6, bf16[2,512,512]{2,1,0:T(8,128)(2,1)} %bitcast.10), custom_call_target="tpu_custom_call" | custom-call | flops 402653184 | bytes 2359296 | tf_op jit(solution)/shard_map/pallas_call | solution.py:52
  34.7 1.9 %collective-permute-start.5 = (bf16[128,3072]{1,0:T(8,128)(2,1)}, bf16[128,3072]{1,0:T(8,128)(2,1)}, u32[]{:S(2)}, u32[]{:S(2)}) collective-permute-start(bf16[128,3072]{1,0:T(8,128)(2,1)} %get-tuple-element.38), channel_id=1, source_target_pairs={{8,0},{16,8},{24,16},{32,24},{40,32},{48,40},{56,48},{64,56},{72,6... | collective-permute-start | bytes 2359304 | tf_op jit(solution)/shard_map/ppermute | solution.py:30
  37.9 3.5 %shard_map.40.near = bf16[512,3072]{1,0:T(8,128)(2,1)S(1)} custom-call(s32[1,2]{1,0:T(1,128)S(1)} %copy-done.2, bf16[6,8,64,512]{3,2,1,0:T(8,128)(2,1)S(1)} %bitcast.7, bf16[2,512,512]{2,1,0:T(8,128)(2,1)S(1)} %bitcast.11), custom_call_target="tpu_custom_call" | custom-call | flops 1610612736 | bytes 6291456 | tf_op jit(solution)/shard_map/pallas_call | solution.py:73
  41.4 29.1 %collective-permute-done.ahead0 = bf16[128,3072]{1,0:T(8,128)(2,1)} collective-permute-done((bf16[128,3072]{1,0:T(8,128)(2,1)}, bf16[128,3072]{1,0:T(8,128)(2,1)}, u32[]{:S(2)}, u32[]{:S(2)}) %collective-permute-start) | collective-permute-done | bytes 786464 | tf_op jit(solution)/shard_map/ppermute | solution.py:30
  72.5 5.9 %shard_map.41 = (f32[4,672,128]{2,1,0:T(8,128)S(1)}, bf16[4,672,128]{2,1,0:T(8,128)(2,1)S(1)}) custom-call(s32[2]{0:T(128)S(1)} %pad_add_fusion.place, bf16[512,3072]{1,0:T(8,128)(2,1)S(1)} %shard_map.40.near, bf16[128,3072]{1,0:T(8,128)(2,1)} %collective-permute-done.ahead0, bf16[256,3072]{1,0:T(8,128)(2,1)} %collective-permute-done.1.ahead1, ...), custom_call_target="tpu_custom_call" | custom-call | flops 2415919104 | bytes 6291456 | tf_op jit(solution)/shard_map/pallas_call | solution.py:144
  78.4 2.1 %collective-permute-done.4.received = bf16[4,672,128]{2,1,0:T(8,128)(2,1)S(1)} collective-permute-done((bf16[4,672,128]{2,1,0:T(8,128)(2,1)S(1)}, bf16[4,672,128]{2,1,0:T(8,128)(2,1)S(1)}, u32[]{:S(2)}, u32[]{:S(2)}) %collective-permute-start.4) | collective-permute-done | bytes 688160 | tf_op jit(solution)/shard_map/ppermute | solution.py:34
  81.2 5.0 %collective-permute-done.5.ahead2 = bf16[128,3072]{1,0:T(8,128)(2,1)} collective-permute-done((bf16[128,3072]{1,0:T(8,128)(2,1)}, bf16[128,3072]{1,0:T(8,128)(2,1)}, u32[]{:S(2)}, u32[]{:S(2)}) %collective-permute-start.5) | collective-permute-done | bytes 786464 | tf_op jit(solution)/shard_map/ppermute | solution.py:30
  86.2 3.5 %collective-permute-done.6.behind2 = bf16[128,3072]{1,0:T(8,128)(2,1)S(1)} collective-permute-done((bf16[128,3072]{1,0:T(8,128)(2,1)S(1)}, bf16[128,3072]{1,0:T(8,128)(2,1)S(1)}, u32[]{:S(2)}, u32[]{:S(2)}) %collective-permute-start.6) | collective-permute-done | bytes 786464 | tf_op jit(solution)/shard_map/ppermute | solution.py:30
  89.7 5.1 %shard_map.43 = (f32[4,352,128]{2,1,0:T(8,128)S(1)}, bf16[4,352,128]{2,1,0:T(8,128)(2,1)S(1)}) custom-call(s32[2]{0:T(128)S(1)} %pad_add_fusion.place, bf16[512,3072]{1,0:T(8,128)(2,1)S(1)} %shard_map.40.near, bf16[128,3072]{1,0:T(8,128)(2,1)} %collective-permute-done.ahead0, bf16[256,3072]{1,0:T(8,128)(2,1)} %collective-permute-done.1.ahead1, ...), custom_call_target="tpu_custom_call" | custom-call | flops 1207959552 | bytes 9437184 | tf_op jit(solution)/shard_map/pallas_call | solution.py:193
  94.9 3.1 %collective-permute-start.10 = (bf16[672,128]{1,0:T(8,128)(2,1)S(1)}, bf16[672,128]{1,0:T(8,128)(2,1)S(1)}, u32[]{:S(2)}, u32[]{:S(2)}) collective-permute-start(bf16[672,128]{1,0:T(8,128)(2,1)S(1)} %get-tuple-element.47), channel_id=1, source_target_pairs={{0,6},{1,7},{2,0},{3,1},{4,2},{5,3},{6,4},{7,5},{8,14},{9,15},{10,... | collective-permute-start | bytes 516104 | tf_op jit(solution)/shard_map/ppermute | solution.py:39
  100.3 2.0 %collective-permute-start.13 = (bf16[352,128]{1,0:T(8,128)(2,1)S(1)}, bf16[352,128]{1,0:T(8,128)(2,1)S(1)}, u32[]{:S(2)}, u32[]{:S(2)}) collective-permute-start(bf16[352,128]{1,0:T(8,128)(2,1)S(1)} %get-tuple-element.53), channel_id=1, source_target_pairs={{0,4},{1,5},{2,6},{3,7},{4,0},{5,1},{6,2},{7,3},{8,12},{9,13},{10,... | collective-permute-start | bytes 270344 | tf_op jit(solution)/shard_map/ppermute | solution.py:39
  103.5 4.4 %collective-permute-done.10.three = bf16[672,128]{1,0:T(8,128)(2,1)S(1)} collective-permute-done((bf16[672,128]{1,0:T(8,128)(2,1)S(1)}, bf16[672,128]{1,0:T(8,128)(2,1)S(1)}, u32[]{:S(2)}, u32[]{:S(2)}) %collective-permute-start.10) | collective-permute-done | bytes 172064 | tf_op jit(solution)/shard_map/ppermute | solution.py:39
  107.9 3.7 %collective-permute-start.15 = (bf16[352,128]{1,0:T(8,128)(2,1)S(1)}, bf16[352,128]{1,0:T(8,128)(2,1)S(1)}, u32[]{:S(2)}, u32[]{:S(2)}) collective-permute-start(bf16[352,128]{1,0:T(8,128)(2,1)S(1)} %get-tuple-element.54), channel_id=1, source_target_pairs={{0,6},{1,7},{2,0},{3,1},{4,2},{5,3},{6,4},{7,5},{8,14},{9,15},{10,... | collective-permute-start | bytes 270344 | tf_op jit(solution)/shard_map/ppermute | solution.py:39
  111.7 5.5 %collective-permute-start.12 = (bf16[336,128]{1,0:T(8,128)(2,1)S(1)}, bf16[336,128]{1,0:T(8,128)(2,1)S(1)}, u32[]{:S(2)}, u32[]{:S(2)}) collective-permute-start(bf16[336,128]{1,0:T(8,128)(2,1)S(1)} %get-tuple-element.58), channel_id=1, source_target_pairs={{0,8},{8,16},{16,24},{24,32},{32,40},{40,48},{48,56},{56,64},{64,7... | collective-permute-start | bytes 258056 | tf_op jit(solution)/shard_map/ppermute | solution.py:30
  117.2 1.9 %collective-permute-start.11 = (bf16[144,128]{1,0:T(8,128)(2,1)S(1)}, bf16[144,128]{1,0:T(8,128)(2,1)S(1)}, u32[]{:S(2)}, u32[]{:S(2)}) collective-permute-start(bf16[144,128]{1,0:T(8,128)(2,1)S(1)} %get-tuple-element.57), channel_id=1, source_target_pairs={{8,0},{16,8},{24,16},{32,24},{40,32},{48,40},{56,48},{64,56},{72,6... | collective-permute-start | bytes 110600 | tf_op jit(solution)/shard_map/ppermute | solution.py:30
  119.2 7.2 %collective-permute-start.17 = (bf16[176,128]{1,0:T(8,128)(2,1)S(1)}, bf16[176,128]{1,0:T(8,128)(2,1)S(1)}, u32[]{:S(2)}, u32[]{:S(2)}) collective-permute-start(bf16[176,128]{1,0:T(8,128)(2,1)S(1)} %get-tuple-element.62), channel_id=1, source_target_pairs={{0,8},{8,16},{16,24},{24,32},{32,40},{40,48},{48,56},{56,64},{64,7... | collective-permute-start | bytes 135176 | tf_op jit(solution)/shard_map/ppermute | solution.py:30
  126.5 1.9 %collective-permute-start.16 = (bf16[112,128]{1,0:T(8,128)(2,1)S(1)}, bf16[112,128]{1,0:T(8,128)(2,1)S(1)}, u32[]{:S(2)}, u32[]{:S(2)}) collective-permute-start(bf16[112,128]{1,0:T(8,128)(2,1)S(1)} %get-tuple-element.61), channel_id=1, source_target_pairs={{8,0},{16,8},{24,16},{32,24},{40,32},{48,40},{56,48},{64,56},{72,6... | collective-permute-start | bytes 86024 | tf_op jit(solution)/shard_map/ppermute | solution.py:30
  128.6 7.0 %collective-permute-done.16.far1 = bf16[112,128]{1,0:T(8,128)(2,1)S(1)} collective-permute-done((bf16[112,128]{1,0:T(8,128)(2,1)S(1)}, bf16[112,128]{1,0:T(8,128)(2,1)S(1)}, u32[]{:S(2)}, u32[]{:S(2)}) %collective-permute-start.16) | collective-permute-done | bytes 28704 | tf_op jit(solution)/shard_map/ppermute | solution.py:30
  (34 shorter events, 9.5 us)
Async XLA Ops:
  10.9 61.6 %collective-permute-start.1 = (bf16[256,3072]{1,0:T(8,128)(2,1)}, bf16[256,3072]{1,0:T(8,128)(2,1)}, u32[]{:S(2)}, u32[]{:S(2)}) collective-permute-start(bf16[256,3072]{1,0:T(8,128)(2,1)} %get-tuple-element.36), channel_id=1, source_target_pairs={{8,0},{16,8},{24,16},{32,24},{40,32},{48,40},{56,48},{64,56},{72,6... | collective-permute-start | bytes 4718600 | tf_op jit(solution)/shard_map/ppermute | solution.py:30
  13.6 58.8 %collective-permute-start.3 = (bf16[256,3072]{1,0:T(8,128)(2,1)}, bf16[256,3072]{1,0:T(8,128)(2,1)}, u32[]{:S(2)}, u32[]{:S(2)}) collective-permute-start(bf16[256,3072]{1,0:T(8,128)(2,1)} %get-tuple-element.41), channel_id=1, source_target_pairs={{0,8},{8,16},{16,24},{24,32},{32,40},{40,48},{48,56},{56,64},{64,7... | collective-permute-start | bytes 4718600 | tf_op jit(solution)/shard_map/ppermute | solution.py:30
  20.0 50.5 %collective-permute-start = (bf16[128,3072]{1,0:T(8,128)(2,1)}, bf16[128,3072]{1,0:T(8,128)(2,1)}, u32[]{:S(2)}, u32[]{:S(2)}) collective-permute-start(bf16[128,3072]{1,0:T(8,128)(2,1)} %get-tuple-element.34), channel_id=1, source_target_pairs={{8,0},{16,8},{24,16},{32,24},{40,32},{48,40},{56,48},{64,56},{72,6... | collective-permute-start | bytes 2359304 | tf_op jit(solution)/shard_map/ppermute | solution.py:30
  22.0 14.7 %copy-start = (bf16[1,6,512,512]{3,2,1,0:T(8,128)(2,1)S(1)}, bf16[1,6,512,512]{3,2,1,0:T(8,128)(2,1)}, u32[]{:S(2)}) copy-start(bf16[1,6,512,512]{3,2,1,0:T(8,128)(2,1)} %param.3) | copy-start | bytes 9437188
  22.0 14.7 %copy-start.2 = (s32[1,2]{1,0:T(1,128)S(1)}, s32[1,2]{1,0:T(1,128)}, u32[]{:S(2)}) copy-start(s32[1,2]{1,0:T(1,128)} %flag.7) | copy-start | bytes 28
  22.0 50.4 %collective-permute-start.2 = (bf16[128,3072]{1,0:T(8,128)(2,1)}, bf16[128,3072]{1,0:T(8,128)(2,1)}, u32[]{:S(2)}, u32[]{:S(2)}) collective-permute-start(bf16[128,3072]{1,0:T(8,128)(2,1)} %get-tuple-element.40), channel_id=1, source_target_pairs={{0,8},{8,16},{16,24},{24,32},{32,40},{40,48},{48,56},{56,64},{64,7... | collective-permute-start | bytes 2359304 | tf_op jit(solution)/shard_map/ppermute | solution.py:30
  34.7 51.5 %collective-permute-start.5 = (bf16[128,3072]{1,0:T(8,128)(2,1)}, bf16[128,3072]{1,0:T(8,128)(2,1)}, u32[]{:S(2)}, u32[]{:S(2)}) collective-permute-start(bf16[128,3072]{1,0:T(8,128)(2,1)} %get-tuple-element.38), channel_id=1, source_target_pairs={{8,0},{16,8},{24,16},{32,24},{40,32},{48,40},{56,48},{64,56},{72,6... | collective-permute-start | bytes 2359304 | tf_op jit(solution)/shard_map/ppermute | solution.py:30
  36.7 1.2 copy-start.1
  37.9 32.6 %copy-start.3 = (bf16[128,3072]{1,0:T(8,128)(2,1)S(1)}, bf16[128,3072]{1,0:T(8,128)(2,1)}, u32[]{:S(2)}) copy-start(bf16[128,3072]{1,0:T(8,128)(2,1)} %get-tuple-element.49) | copy-start | bytes 2359300
  70.5 19.2 %collective-permute-start.6 = (bf16[128,3072]{1,0:T(8,128)(2,1)S(1)}, bf16[128,3072]{1,0:T(8,128)(2,1)S(1)}, u32[]{:S(2)}, u32[]{:S(2)}) collective-permute-start(bf16[128,3072]{1,0:T(8,128)(2,1)S(1)} %copy-done.3), channel_id=1, source_target_pairs={{0,8},{8,16},{16,24},{24,32},{32,40},{40,48},{48,56},{56,64},{64,7... | collective-permute-start | bytes 2359304 | tf_op jit(solution)/shard_map/ppermute | solution.py:30
  78.3 2.2 %collective-permute-start.4 = (bf16[4,672,128]{2,1,0:T(8,128)(2,1)S(1)}, bf16[4,672,128]{2,1,0:T(8,128)(2,1)S(1)}, u32[]{:S(2)}, u32[]{:S(2)}) collective-permute-start(bf16[4,672,128]{2,1,0:T(8,128)(2,1)S(1)} %get-tuple-element.43), channel_id=1, source_target_pairs={{0,1},{1,0},{2,3},{3,2},{4,5},{5,4},{6,7},{7,6},{8,9},{9,8},{10,11... | collective-permute-start | bytes 2064392 | tf_op jit(solution)/shard_map/ppermute | solution.py:34
  94.8 4.8 %collective-permute-start.7 = (bf16[4,352,128]{2,1,0:T(8,128)(2,1)S(1)}, bf16[4,352,128]{2,1,0:T(8,128)(2,1)S(1)}, u32[]{:S(2)}, u32[]{:S(2)}) collective-permute-start(bf16[4,352,128]{2,1,0:T(8,128)(2,1)S(1)} %get-tuple-element.51), channel_id=1, source_target_pairs={{0,1},{1,0},{2,3},{3,2},{4,5},{5,4},{6,7},{7,6},{8,9},{9,8},{10,11... | collective-permute-start | bytes 1081352 | tf_op jit(solution)/shard_map/ppermute | solution.py:34
  94.9 12.9 %collective-permute-start.10 = (bf16[672,128]{1,0:T(8,128)(2,1)S(1)}, bf16[672,128]{1,0:T(8,128)(2,1)S(1)}, u32[]{:S(2)}, u32[]{:S(2)}) collective-permute-start(bf16[672,128]{1,0:T(8,128)(2,1)S(1)} %get-tuple-element.47), channel_id=1, source_target_pairs={{0,6},{1,7},{2,0},{3,1},{4,2},{5,3},{6,4},{7,5},{8,14},{9,15},{10,... | collective-permute-start | bytes 516104 | tf_op jit(solution)/shard_map/ppermute | solution.py:39
  98.0 13.5 %collective-permute-start.8 = (bf16[672,128]{1,0:T(8,128)(2,1)S(1)}, bf16[672,128]{1,0:T(8,128)(2,1)S(1)}, u32[]{:S(2)}, u32[]{:S(2)}) collective-permute-start(bf16[672,128]{1,0:T(8,128)(2,1)S(1)} %get-tuple-element.46), channel_id=1, source_target_pairs={{0,4},{1,5},{2,6},{3,7},{4,0},{5,1},{6,2},{7,3},{8,12},{9,13},{10,... | collective-permute-start | bytes 516104 | tf_op jit(solution)/shard_map/ppermute | solution.py:39
  98.7 12.9 %collective-permute-start.9 = (bf16[672,128]{1,0:T(8,128)(2,1)S(1)}, bf16[672,128]{1,0:T(8,128)(2,1)S(1)}, u32[]{:S(2)}, u32[]{:S(2)}) collective-permute-start(bf16[672,128]{1,0:T(8,128)(2,1)S(1)} %get-tuple-element.45), channel_id=1, source_target_pairs={{0,2},{1,3},{2,4},{3,5},{4,6},{5,7},{6,0},{7,1},{8,10},{9,11},{10,... | collective-permute-start | bytes 516104 | tf_op jit(solution)/shard_map/ppermute | solution.py:39
  100.3 18.9 %collective-permute-start.13 = (bf16[352,128]{1,0:T(8,128)(2,1)S(1)}, bf16[352,128]{1,0:T(8,128)(2,1)S(1)}, u32[]{:S(2)}, u32[]{:S(2)}) collective-permute-start(bf16[352,128]{1,0:T(8,128)(2,1)S(1)} %get-tuple-element.53), channel_id=1, source_target_pairs={{0,4},{1,5},{2,6},{3,7},{4,0},{5,1},{6,2},{7,3},{8,12},{9,13},{10,... | collective-permute-start | bytes 270344 | tf_op jit(solution)/shard_map/ppermute | solution.py:39
  102.3 16.9 %collective-permute-start.14 = (bf16[352,128]{1,0:T(8,128)(2,1)S(1)}, bf16[352,128]{1,0:T(8,128)(2,1)S(1)}, u32[]{:S(2)}, u32[]{:S(2)}) collective-permute-start(bf16[352,128]{1,0:T(8,128)(2,1)S(1)} %get-tuple-element.52), channel_id=1, source_target_pairs={{0,2},{1,3},{2,4},{3,5},{4,6},{5,7},{6,0},{7,1},{8,10},{9,11},{10,... | collective-permute-start | bytes 270344 | tf_op jit(solution)/shard_map/ppermute | solution.py:39
  107.9 11.3 %collective-permute-start.15 = (bf16[352,128]{1,0:T(8,128)(2,1)S(1)}, bf16[352,128]{1,0:T(8,128)(2,1)S(1)}, u32[]{:S(2)}, u32[]{:S(2)}) collective-permute-start(bf16[352,128]{1,0:T(8,128)(2,1)S(1)} %get-tuple-element.54), channel_id=1, source_target_pairs={{0,6},{1,7},{2,0},{3,1},{4,2},{5,3},{6,4},{7,5},{8,14},{9,15},{10,... | collective-permute-start | bytes 270344 | tf_op jit(solution)/shard_map/ppermute | solution.py:39
  111.7 16.9 %collective-permute-start.12 = (bf16[336,128]{1,0:T(8,128)(2,1)S(1)}, bf16[336,128]{1,0:T(8,128)(2,1)S(1)}, u32[]{:S(2)}, u32[]{:S(2)}) collective-permute-start(bf16[336,128]{1,0:T(8,128)(2,1)S(1)} %get-tuple-element.58), channel_id=1, source_target_pairs={{0,8},{8,16},{16,24},{24,32},{32,40},{40,48},{48,56},{56,64},{64,7... | collective-permute-start | bytes 258056 | tf_op jit(solution)/shard_map/ppermute | solution.py:30
  117.2 11.4 %collective-permute-start.11 = (bf16[144,128]{1,0:T(8,128)(2,1)S(1)}, bf16[144,128]{1,0:T(8,128)(2,1)S(1)}, u32[]{:S(2)}, u32[]{:S(2)}) collective-permute-start(bf16[144,128]{1,0:T(8,128)(2,1)S(1)} %get-tuple-element.57), channel_id=1, source_target_pairs={{8,0},{16,8},{24,16},{32,24},{40,32},{48,40},{56,48},{64,56},{72,6... | collective-permute-start | bytes 110600 | tf_op jit(solution)/shard_map/ppermute | solution.py:30
  119.2 16.3 %collective-permute-start.17 = (bf16[176,128]{1,0:T(8,128)(2,1)S(1)}, bf16[176,128]{1,0:T(8,128)(2,1)S(1)}, u32[]{:S(2)}, u32[]{:S(2)}) collective-permute-start(bf16[176,128]{1,0:T(8,128)(2,1)S(1)} %get-tuple-element.62), channel_id=1, source_target_pairs={{0,8},{8,16},{16,24},{24,32},{32,40},{40,48},{48,56},{56,64},{64,7... | collective-permute-start | bytes 135176 | tf_op jit(solution)/shard_map/ppermute | solution.py:30
  126.5 9.1 %collective-permute-start.16 = (bf16[112,128]{1,0:T(8,128)(2,1)S(1)}, bf16[112,128]{1,0:T(8,128)(2,1)S(1)}, u32[]{:S(2)}, u32[]{:S(2)}) collective-permute-start(bf16[112,128]{1,0:T(8,128)(2,1)S(1)} %get-tuple-element.61), channel_id=1, source_target_pairs={{8,0},{16,8},{24,16},{32,24},{40,32},{48,40},{56,48},{64,56},{72,6... | collective-permute-start | bytes 86024 | tf_op jit(solution)/shard_map/ppermute | solution.py:30
where the time goes:
time: 138 us; the launch traced here: 137 us
  waiting for transfers between devices  51.1 us (37%)
  starting transfers between devices  50.8 us (37%)
  Pallas kernels  33.6 us (24%)
    ppermute x10, waiting for transfers between devices, shift(): lax.ppermute(value, axis, [(i, i + steps) for i in range(count) if 0 <= i...  44.5 us
    ppermute x10, starting transfers between devices, shift(): lax.ppermute(value, axis, [(i, i + steps) for i in range(count) if 0 <= i...  39 us
    pallas_call x3, Pallas kernels, split(): pl.pallas_call(kernel, grid=(count,), in_specs=[SMEM, pl.BlockSpec((1, PA...  16.1 us
    ppermute x6, starting transfers between devices, shift_y(): lax.ppermute(value, 'aux', [(i, (i + 2 * steps) % count) for i in range(c...  11.6 us
    pallas_call x1, Pallas kernels, pack_early(): pl.pallas_call(kernel, in_specs=[SMEM] + [VMEM] * 5, out_specs=[VMEM] * 2...  5.85 us
    pallas_call x1, Pallas kernels, pack_late(): pl.pallas_call(kernel, in_specs=[SMEM] + [VMEM] * 7, out_specs=[VMEM] * 2...  5.14 us
    ppermute x6, waiting for transfers between devices, shift_y(): lax.ppermute(value, 'aux', [(i, (i + 2 * steps) % count) for i in range(c...  4.4 us
    pallas_call x1, Pallas kernels, transform(): pl.pallas_call(kernel, grid=(count,), in_specs=[SMEM, pl.BlockSpec((1, PA...  3.47 us
  transfers between devices with their start and end apart: 18, of which 6 were waited for; matrix products, arithmetic and copies ran while one was open for 0% of the time, Pallas kernels for 12%

commit v1 on v0

v1 whole, which is shorter than its diff:
```python
import jax
import jax.numpy as jnp
from jax import lax
from jax.experimental import pallas as pl
from jax.experimental.pallas import tpu as pltpu
from jax.sharding import PartitionSpec as P


F32, BF16 = jnp.float32, jnp.bfloat16
VMEM = pl.BlockSpec(memory_space=pltpu.VMEM)
SMEM = pl.BlockSpec(memory_space=pltpu.SMEM)
LANES = 128
ROWS, PARTS, STEP = 64, 8, 3
CHUNKS = ((0, 16), (32, 32), (16, 16))
EARLY, LATE = 384, 128
EARLY_U1, EARLY_U2, EARLY_ALL = 192, 144, 672
LATE_U1, LATE_U2, LATE_ALL = 64, 112, 352


def params(limit=20):
    return pltpu.CompilerParams(vmem_limit_bytes=limit * 1024 * 1024)


def cost(flops, size):
    return pl.CostEstimate(flops=flops, bytes_accessed=size, transcendentals=0)


def swap_atoms(value, first):
    count = lax.axis_size("atoms")
    pairs = [(i, i + 1) for i in range(first, count - 1, 2)]
    return lax.ppermute(value, "atoms", pairs + [(j, i) for i, j in pairs])


def swap_core(value):
    return lax.ppermute(value, "aux", [(i, i ^ 1) for i in range(lax.axis_size("aux"))])


def shift_y(value, steps):
    count = lax.axis_size("aux")
    return lax.ppermute(value, "aux", [(i, (i + 2 * steps) % count) for i in range(count)])


def split(place, factors, density, screen, start, size):
    count, width = factors.shape[0], factors.shape[-1]
    height = PARTS * size

    def kernel(place, flag, left, right, first, second):
        scale = flag[0, 1].astype(F32).astype(BF16)
        even = place[2] == 0
        for step in range(STEP):
            columns = pl.ds(step * width, width)
            piece = left[step].reshape(height, width)
            far = jnp.dot(piece, right[0], preferred_element_type=F32).astype(BF16) * scale
            first[:, columns] = jnp.where(even, far, piece)
            second[:, columns] = jnp.where(even, piece, far)

    return pl.pallas_call(
        kernel,
        grid=(count // STEP,),
        in_specs=[
            SMEM,
            SMEM,
            pl.BlockSpec((STEP, PARTS, size, width), lambda i: (i, 0, start // size, 0)),
            pl.BlockSpec((1, width, width), lambda i: (1, 0, 0)),
        ],
        out_specs=[pl.BlockSpec((height, STEP * width), lambda i: (0, i))] * 2,
        out_shape=[jax.ShapeDtypeStruct((height, count * width), BF16)] * 2,
        cost_estimate=cost(2 * height * count * width**2, 6 * height * count * width),
    )(place, screen, factors, density)


def transform(factors, density, screen):
    count, width = factors.shape[0], factors.shape[-1]

    def kernel(flag, left, right, out):
        scale = flag[0, 0].astype(F32).astype(BF16)
        for step in range(STEP):
            piece = left[step].reshape(width, width)
            product = jnp.dot(piece, right[0], preferred_element_type=F32).astype(BF16)
            out[:, pl.ds(step * width, width)] = product * scale

    return pl.pallas_call(
        kernel,
        grid=(count // STEP,),
        in_specs=[
            SMEM,
            pl.BlockSpec((STEP, PARTS, ROWS, width), lambda i: (i, 0, 0, 0)),
            pl.BlockSpec((1, width, width), lambda i: (0, 0, 0)),
        ],
        out_specs=pl.BlockSpec((width, STEP * width), lambda i: (0, i)),
        out_shape=jax.ShapeDtypeStruct((width, count * width), BF16),
        compiler_params=params(),
        cost_estimate=cost(2 * count * width**3, 4 * count * width**2),
    )(screen, factors, density)


def contract(left, right):
    return lax.dot_general(left, right, (((1,), (1,)), ((), ())), preferred_element_type=F32)


def early_rows(ref, part, columns):
    low = ref[pl.ds(pl.multiple_of(16 * part, 16), 16), columns]
    high = ref[pl.ds(pl.multiple_of(128 + 32 * part, 32), 32), columns]
    return low, high


def late_rows(ref, part, columns):
    return ref[pl.ds(pl.multiple_of(16 * part, 16), 16), columns]


def put(out, y, offset, values):
    for value in values:
        out[y, pl.ds(offset, value.shape[0]), :] = value.astype(out.dtype)
        offset += value.shape[0]
    return offset


def lanes(index):
    return pl.ds(index * LANES, LANES)


def pick(place, first, second):
    even = place[2] == 0
    first, second = first[...], second[...]
    return jnp.where(even, first, second), jnp.where(even, second, first)


def pack_early(place, near, first, second):
    width, depth = near.shape
    places = PARTS // 2

    def kernel(place, near, first0, second0, first1, second1, kept, sent, ahead, behind, upper, lower, upper_far, lower_far):
        low, high = pl.ds(0, 128), pl.ds(128, 256)
        ahead[low, :], behind[low, :] = pick(place, first0, second0)
        ahead[high, :], behind[high, :] = pick(place, first1, second1)
        value = contract(near[...], ahead[...])
        upper[...] = value
        lower[...] = value.T
        value = contract(behind[...], ahead[...])
        upper_far[...] = value
        lower_far[...] = value.T
        for y in range(places):
            for out, core in ((sent, 1 - place[0]), (kept, place[0])):
                part = 2 * y + core
                own = pl.ds(pl.multiple_of(ROWS * part, ROWS), ROWS)
                at = put(out, y, 0, [upper[own, lanes(t)] for t in range(3)])
                for t in range(3):
                    at = put(out, y, at, early_rows(upper_far, part, lanes(t)))
                for t in range(4):
                    at = put(out, y, at, early_rows(lower, part, lanes(t)))
                for t in range(3):
                    at = put(out, y, at, early_rows(lower_far, part, lanes(t)))

    shape = (places, EARLY_ALL, LANES)
    return pl.pallas_call(
        kernel,
        in_specs=[SMEM] + [VMEM] * 5,
        out_specs=[VMEM] * 4,
        out_shape=[
            jax.ShapeDtypeStruct(shape, F32),
            jax.ShapeDtypeStruct(shape, BF16),
            jax.ShapeDtypeStruct((EARLY, depth), BF16),
            jax.ShapeDtypeStruct((EARLY, depth), BF16),
        ],
        scratch_shapes=[
            pltpu.VMEM((width, EARLY), F32),
            pltpu.VMEM((EARLY, width), F32),
            pltpu.VMEM((EARLY, EARLY), F32),
            pltpu.VMEM((EARLY, EARLY), F32),
        ],
        compiler_params=params(),
        cost_estimate=cost(2 * near.size * EARLY * 2, near.size * 4),
    )(place, near, first[0], second[0], first[1], second[1])


def pack_late(place, near, ahead, behind, first, second):
    width = near.shape[0]
    places = PARTS // 2

    def kernel(place, near, ahead, behind, first, second, kept, sent, upper, lower, tall, wide, tall_t, wide_t):
        last, prior = pick(place, first, second)
        value = contract(near[...], last)
        upper[...] = value
        lower[...] = value.T
        value = contract(behind[...], last)
        tall[...] = value
        wide_t[:, pl.ds(0, EARLY)] = value.T
        value = contract(ahead[...], prior)
        tall_t[...] = value
        wide[:, pl.ds(0, EARLY)] = value.T
        value = contract(prior, last)
        wide[:, pl.ds(EARLY, LATE)] = value
        wide_t[:, pl.ds(EARLY, LATE)] = value.T
        for y in range(places):
            for out, core in ((sent, 1 - place[0]), (kept, place[0])):
                part = 2 * y + core
                own = pl.ds(pl.multiple_of(ROWS * part, ROWS), ROWS)
                at = put(out, y, 0, [upper[own, :]])
                at = put(out, y, at, early_rows(tall, part, lanes(0)))
                at = put(out, y, at, [late_rows(wide, part, lanes(t)) for t in range(4)])
                at = put(out, y, at, [late_rows(lower, part, lanes(t)) for t in range(4)])
                at = put(out, y, at, early_rows(tall_t, part, lanes(0)))
                at = put(out, y, at, [late_rows(wide_t, part, lanes(t)) for t in range(4)])

    shape = (places, LATE_ALL, LANES)
    return pl.pallas_call(
        kernel,
        in_specs=[SMEM] + [VMEM] * 5,
        out_specs=[VMEM] * 2,
        out_shape=[jax.ShapeDtypeStruct(shape, F32), jax.ShapeDtypeStruct(shape, BF16)],
        scratch_shapes=[
            pltpu.VMEM((width, LATE), F32),
            pltpu.VMEM((LATE, width), F32),
            pltpu.VMEM((EARLY, LATE), F32),
            pltpu.VMEM((LATE, width), F32),
            pltpu.VMEM((EARLY, LATE), F32),
            pltpu.VMEM((LATE, width), F32),
        ],
        compiler_params=params(),
        cost_estimate=cost(2 * near.size * LATE * 3, near.size * 6),
    )(place, near, ahead, behind, first, second)


def join_core(place, kept, received):
    places, rows, width = kept.shape

    def kernel(place, kept, received, total, *pieces):
        y = place[1]
        total[...] = kept[y] + received[y].astype(F32)
        for steps in range(1, places):
            target = lax.rem(y + steps, places)
            pieces[steps - 1][...] = (kept[target] + received[target].astype(F32)).astype(BF16)

    shape = (rows, width)
    return pl.pallas_call(
        kernel,
        in_specs=[SMEM, VMEM, VMEM],
        out_specs=[VMEM] * places,
        out_shape=[jax.ShapeDtypeStruct(shape, F32)] + [jax.ShapeDtypeStruct(shape, BF16)] * (places - 1),
        compiler_params=params(),
        cost_estimate=cost(kept.size, 8 * kept.size),
    )(place, kept, received)


def after(value, *others):
    return lax.optimization_barrier((value, *others))[0]


def send_places(pieces):
    received = []
    for steps in (2, 1, 3):
        received.append(shift_y(pieces[steps - 1], steps))
    return received


def gather(refs, span):
    total, *received = refs
    value = total[span, :]
    for piece in received:
        value = value + piece[span, :].astype(F32)
    return value


def join_early(total, received):
    rows, width = total.shape

    def kernel(total, one, two, three, upper, rest):
        refs = (total, one, two, three)
        upper[...] = gather(refs, pl.ds(0, EARLY_U1))
        rest[...] = gather(refs, pl.ds(EARLY_U1, rows - EARLY_U1)).astype(BF16)

    return pl.pallas_call(
        kernel,
        in_specs=[VMEM] * 4,
        out_specs=[VMEM] * 2,
        out_shape=[
            jax.ShapeDtypeStruct((EARLY_U1, width), F32),
            jax.ShapeDtypeStruct((rows - EARLY_U1, width), BF16),
        ],
        compiler_params=params(),
        cost_estimate=cost(total.size * 3, 12 * total.size),
    )(total, *received)


def join_late(place, rest, total, received):
    rows, width = total.shape
    far = EARLY_U2 + LATE_U2
    low = rest.shape[0] - EARLY_U2
    height = low + rows - LATE_U1 - LATE_U2

    def kernel(place, rest, total, one, two, three, upper, first, second):
        refs = (total, one, two, three)
        even = place[2] == 0
        upper[...] = gather(refs, pl.ds(0, LATE_U1))
        late_far = gather(refs, pl.ds(LATE_U1, LATE_U2)).astype(BF16)
        late_low = gather(refs, pl.ds(LATE_U1 + LATE_U2, rows - LATE_U1 - LATE_U2)).astype(BF16)

        def write(lower, upper_far):
            lower[pl.ds(0, low), :] = rest[pl.ds(EARLY_U2, low), :]
            lower[pl.ds(low, late_low.shape[0]), :] = late_low
            upper_far[pl.ds(0, EARLY_U2), :] = rest[pl.ds(0, EARLY_U2), :]
            upper_far[pl.ds(EARLY_U2, LATE_U2), :] = late_far
            upper_far[pl.ds(far, height - far), :] = jnp.zeros((height - far, width), BF16)

        pl.when(even)(lambda: write(first, second))
        pl.when(jnp.logical_not(even))(lambda: write(second, first))

    return pl.pallas_call(
        kernel,
        in_specs=[SMEM] + [VMEM] * 5,
        out_specs=[VMEM] * 3,
        out_shape=[
            jax.ShapeDtypeStruct((LATE_U1, width), F32),
            jax.ShapeDtypeStruct((height, width), BF16),
            jax.ShapeDtypeStruct((height, width), BF16),
        ],
        compiler_params=params(),
        cost_estimate=cost(total.size * 3, 12 * total.size),
    )(place, rest, total, *received)


def restore(order, early, late):
    width = order.shape[0]

    def kernel(order, early, late, out):
        blocks = [early[pl.ds(ROWS * t, ROWS), :] for t in range(3)] + [late[...]]
        value = jnp.concatenate(blocks, axis=1)
        exact = order[...].astype(F32)
        out[...] = jnp.dot(value, exact, preferred_element_type=F32, precision=lax.Precision.HIGHEST)

    return pl.pallas_call(
        kernel,
        in_specs=[VMEM] * 3,
        out_specs=VMEM,
        out_shape=jax.ShapeDtypeStruct((ROWS, width), F32),
        compiler_params=params(),
        cost_estimate=cost(2 * 6 * ROWS * width**2, 4 * width**2),
    )(order, early, late)


def assemble(place, order, upper, first, second):
    width = order.shape[0]
    late_low = 3 * 144 - 96

    def rows(ref, base, late):
        body = jnp.concatenate(
            [ref[pl.ds(base + 48 * t, 48), :] for t in range(3)] + [ref[pl.ds(late, 48), :]], axis=1
        )
        last = jnp.concatenate([ref[pl.ds(late + 48 + 16 * t, 16), :] for t in range(4)], axis=1)
        return jnp.concatenate([body[:16], last, body[16:]], axis=0)

    def kernel(place, order, upper, first, second, out):
        out[0, 0] = upper[...]

        def write(far, low):
            exact = order[...]
            out[0, 1] = jnp.dot(rows(far, 0, EARLY_U2), exact, preferred_element_type=F32)
            for t in range(4):
                out[0, 2, pl.ds(0, 16), lanes(t)] = low[pl.ds(48 * t, 16), :].astype(F32)
                out[0, 2, pl.ds(16, 16), lanes(t)] = low[pl.ds(late_low + 16 * t, 16), :].astype(F32)
                out[0, 2, pl.ds(32, 32), lanes(t)] = low[pl.ds(48 * t + 16, 32), :].astype(F32)
            out[0, 3] = jnp.dot(rows(low, 192, late_low + 64), exact, preferred_element_type=F32)

        pl.when(place[2] == 0)(lambda: write(first, second))
        pl.when(place[2] != 0)(lambda: write(second, first))

    return pl.pallas_call(
        kernel,
        in_specs=[SMEM] + [VMEM] * 4,
        out_specs=VMEM,
        out_shape=jax.ShapeDtypeStruct((1, 4, ROWS, width), F32),
        compiler_params=params(),
        cost_estimate=cost(2 * 2 * ROWS * width**2, 4 * ROWS * width * 8),
    )(place, order, upper, first, second)


def natural_order(width):
    index = jnp.arange(width)
    low = ROWS * (index // 16) + index % 16
    high = ROWS * ((index - 128) // 32) + 32 + index % 32
    last = ROWS * ((index - EARLY) // 16) + 16 + index % 16
    place = jnp.where(index < 128, low, jnp.where(index < EARLY, high, last))
    return (place[:, None] == jnp.arange(width)[None, :]).astype(BF16)


def body(factors, density, screen):
    count, width = factors.shape[1], factors.shape[2]
    owned, blocks = factors[0].reshape(count, PARTS, ROWS, width), density[0]
    position = lax.axis_index("aux")
    place = jnp.stack([position % 2, position // 2, lax.axis_index("atoms") % 2]).astype(jnp.int32)
    first, second = [], []
    source = owned
    for start, size in CHUNKS:
        one, two = split(place, source, blocks, screen, start, size)
        source = after(owned, one)
        first.append(swap_atoms(one, 0))
        second.append(swap_atoms(two, 1))
    near = transform(source, blocks, screen)
    kept, sent, ahead, behind = pack_early(place, near, first[:2], second[:2])
    total, *pieces = join_core(place, kept, swap_core(sent))
    received = send_places(pieces)
    kept, sent = pack_late(after(place, *pieces), near, ahead, behind, first[2], second[2])
    late_total, *late_pieces = join_core(place, kept, swap_core(sent))
    late_received = send_places(late_pieces)
    upper, rest = join_early(after(total, *late_pieces), received)
    late_upper, one, two = join_late(place, rest, late_total, late_received)
    one = swap_atoms(one, 0)
    two = swap_atoms(two, 1)
    order = natural_order(width)
    upper = restore(order, upper, late_upper)
    return assemble(place, order, upper, one, two)


def solution(mesh):
    in_specs = (P("atoms", "aux", None, None), P("atoms", None, None, None), P("atoms", None))
    out_specs = P("atoms", None, "aux", None)
    return jax.shard_map(body, mesh=mesh, in_specs=in_specs, out_specs=out_specs, check_vma=False)
```

time: 138 us -> 120 us (0.87)
  the two profiles are of different devices: /device:TPU:102 before, /device:TPU:126 now
where the time goes in v1:
time: 120 us; the launch traced here: 119 us
  waiting for transfers between devices  63 us (52%)
  starting transfers between devices  28.6 us (24%)
  Pallas kernels  25.4 us (21%)
  local copies, waits for them, and re-layouts  1.24 us (1%)
    ppermute x8, waiting for transfers between devices, swap_atoms(): return lax.ppermute(value, 'atoms', pairs + [(j, i) for i, j in pairs])  49.4 us
    ppermute x8, starting transfers between devices, swap_atoms(): return lax.ppermute(value, 'atoms', pairs + [(j, i) for i, j in pairs])  21.3 us
    ppermute x6, waiting for transfers between devices, shift_y(): lax.ppermute(value, 'aux', [(i, (i + 2 * steps) % count) for i in range(c...  11.5 us
    pallas_call x3, Pallas kernels, split(): pl.pallas_call(kernel, grid=(count // STEP,), in_specs=[SMEM, SMEM, pl.Bl...  9.59 us
    ppermute x6, starting transfers between devices, shift_y(): lax.ppermute(value, 'aux', [(i, (i + 2 * steps) % count) for i in range(c...  7.11 us
    pallas_call x1, Pallas kernels, pack_early(): pl.pallas_call(kernel, in_specs=[SMEM] + [VMEM] * 5, out_specs=[VMEM] * 4...  5.68 us
    pallas_call x1, Pallas kernels, pack_late(): pl.pallas_call(kernel, in_specs=[SMEM] + [VMEM] * 5, out_specs=[VMEM] * 2...  3.08 us
    pallas_call x1, Pallas kernels, transform(): pl.pallas_call(kernel, grid=(count // STEP,), in_specs=[SMEM, pl.BlockSpe...  2.74 us
  transfers between devices with their start and end apart: 16, of which 8 were waited for; matrix products, arithmetic and copies ran while one was open for 0% of the time, Pallas kernels for 11%

profile of v1, /device:TPU:126, one launch (start us, length us, event | category | flops | bytes accessed | tf_op | source)
XLA Modules:
  0.0 119.3 jit_solution(3962407160114362128)
XLA Ops:
  0.6 3.0 %shard_map.37 = (bf16[128,3072]{1,0:T(8,128)(2,1)}, bf16[128,3072]{1,0:T(8,128)(2,1)}) custom-call(s32[3]{0:T(128)} %pad_add_fusion.place, s32[1,2]{1,0:T(1,128)} %flag.7, bf16[6,8,64,512]{3,2,1,0:T(8,128)(2,1)} %bitcast.5, bf16[2,512,512]{2,1,0:T(8,128)(2,1)} %bitcast.9), custom_call_target="tpu_custom_call" | custom-call | flops 402653184 | bytes 2359296 | tf_op jit(solution)/shard_map/pallas_call | solution.py:57
  3.6 3.7 %shard_map.38 = (bf16[256,3072]{1,0:T(8,128)(2,1)}, bf16[256,3072]{1,0:T(8,128)(2,1)}) custom-call(s32[3]{0:T(128)} %pad_add_fusion.place, s32[1,2]{1,0:T(1,128)} %flag.7, bf16[6,8,64,512]{3,2,1,0:T(8,128)(2,1)} %bitcast.6, bf16[2,512,512]{2,1,0:T(8,128)(2,1)} %bitcast.10), custom_call_target="tpu_custom_call" | custom-call | flops 805306368 | bytes 4718592 | tf_op jit(solution)/shard_map/pallas_call | solution.py:57
  7.3 0.8 collective-permute-start.2
  8.1 5.6 %collective-permute-start.3 = (bf16[256,3072]{1,0:T(8,128)(2,1)}, bf16[256,3072]{1,0:T(8,128)(2,1)}, u32[]{:S(2)}, u32[]{:S(2)}) collective-permute-start(bf16[256,3072]{1,0:T(8,128)(2,1)} %get-tuple-element.42), channel_id=1, source_target_pairs={{8,16},{24,32},{40,48},{56,64},{72,80},{88,96},{104,112},{120,128}... | collective-permute-start | bytes 4718600 | tf_op jit(solution)/shard_map/ppermute | solution.py:31
  13.8 4.8 %collective-permute-start.1 = (bf16[128,3072]{1,0:T(8,128)(2,1)}, bf16[128,3072]{1,0:T(8,128)(2,1)}, u32[]{:S(2)}, u32[]{:S(2)}) collective-permute-start(bf16[128,3072]{1,0:T(8,128)(2,1)} %get-tuple-element.41), channel_id=1, source_target_pairs={{8,16},{24,32},{40,48},{56,64},{72,80},{88,96},{104,112},{120,128}... | collective-permute-start | bytes 2359304 | tf_op jit(solution)/shard_map/ppermute | solution.py:31
  18.7 2.9 %shard_map.39 = (bf16[128,3072]{1,0:T(8,128)(2,1)}, bf16[128,3072]{1,0:T(8,128)(2,1)}) custom-call(s32[3]{0:T(128)} %pad_add_fusion.place, s32[1,2]{1,0:T(1,128)} %flag.7, bf16[6,8,64,512]{3,2,1,0:T(8,128)(2,1)} %bitcast.7, bf16[2,512,512]{2,1,0:T(8,128)(2,1)} %bitcast.11), custom_call_target="tpu_custom_call" | custom-call | flops 402653184 | bytes 2359296 | tf_op jit(solution)/shard_map/pallas_call | solution.py:57
  21.6 1.2 %copy-done.1 = bf16[1,2,512,512]{3,2,1,0:T(8,128)(2,1)S(1)} copy-done((bf16[1,2,512,512]{3,2,1,0:T(8,128)(2,1)S(1)}, bf16[1,2,512,512]{3,2,1,0:T(8,128)(2,1)}, u32[]{:S(2)}) %copy-start.1) | copy-done | bytes 1048600
  22.8 2.7 %shard_map.40.near = bf16[512,3072]{1,0:T(8,128)(2,1)S(1)} custom-call(s32[1,2]{1,0:T(1,128)S(1)} %copy-done.3, bf16[6,8,64,512]{3,2,1,0:T(8,128)(2,1)S(1)} %bitcast.8, bf16[2,512,512]{2,1,0:T(8,128)(2,1)S(1)} %bitcast.12), custom_call_target="tpu_custom_call" | custom-call | flops 1610612736 | bytes 6291456 | tf_op jit(solution)/shard_map/pallas_call | solution.py:82
  25.6 36.1 %collective-permute-done.first0 = bf16[128,3072]{1,0:T(8,128)(2,1)} collective-permute-done((bf16[128,3072]{1,0:T(8,128)(2,1)}, bf16[128,3072]{1,0:T(8,128)(2,1)}, u32[]{:S(2)}, u32[]{:S(2)}) %collective-permute-start) | collective-permute-done | bytes 786464 | tf_op jit(solution)/shard_map/ppermute | solution.py:31
  61.7 4.9 %collective-permute-start.6 = (bf16[128,3072]{1,0:T(8,128)(2,1)S(1)}, bf16[128,3072]{1,0:T(8,128)(2,1)S(1)}, u32[]{:S(2)}, u32[]{:S(2)}) collective-permute-start(bf16[128,3072]{1,0:T(8,128)(2,1)S(1)} %copy-done.4), channel_id=1, source_target_pairs={{8,16},{24,32},{40,48},{56,64},{72,80},{88,96},{104,112},{120,128}... | collective-permute-start | bytes 2359304 | tf_op jit(solution)/shard_map/ppermute | solution.py:31
  66.7 5.7 %shard_map.41 = (f32[4,672,128]{2,1,0:T(8,128)S(1)}, bf16[4,672,128]{2,1,0:T(8,128)(2,1)S(1)}, bf16[384,3072]{1,0:T(8,128)(2,1)S(1)}, bf16[384,3072]{1,0:T(8,128)(2,1)S(1)}) custom-call(s32[3]{0:T(128)S(1)} %copy-done.2, bf16[512,3072]{1,0:T(8,128)(2,1)S(1)} %shard_map.40.near, bf16[128,3072]{1,0:T(8,128)(2,1)} %collective-permute-done.first0, ...), custom_call_target="tpu_custom_call" | custom-call | flops 2415919104 | bytes 6291456 | tf_op jit(solution)/shard_map/pallas_call | solution.py:155
  72.5 2.1 %collective-permute-done.4.received = bf16[4,672,128]{2,1,0:T(8,128)(2,1)S(1)} collective-permute-done((bf16[4,672,128]{2,1,0:T(8,128)(2,1)S(1)}, bf16[4,672,128]{2,1,0:T(8,128)(2,1)S(1)}, u32[]{:S(2)}, u32[]{:S(2)}) %collective-permute-start.4) | collective-permute-done | bytes 688160 | tf_op jit(solution)/shard_map/ppermute | solution.py:35
  75.3 2.0 %collective-permute-done.5.first = bf16[128,3072]{1,0:T(8,128)(2,1)S(1)} collective-permute-done((bf16[128,3072]{1,0:T(8,128)(2,1)}, bf16[128,3072]{1,0:T(8,128)(2,1)S(1)}, u32[]{:S(2)}, u32[]{:S(2)}) %collective-permute-start.5) | collective-permute-done | bytes 786464 | tf_op jit(solution)/shard_map/ppermute | solution.py:31
  77.3 6.9 %collective-permute-done.6.second = bf16[128,3072]{1,0:T(8,128)(2,1)S(1)} collective-permute-done((bf16[128,3072]{1,0:T(8,128)(2,1)S(1)}, bf16[128,3072]{1,0:T(8,128)(2,1)S(1)}, u32[]{:S(2)}, u32[]{:S(2)}) %collective-permute-start.6) | collective-permute-done | bytes 786464 | tf_op jit(solution)/shard_map/ppermute | solution.py:31
  84.2 3.1 %shard_map.43 = (f32[4,352,128]{2,1,0:T(8,128)S(1)}, bf16[4,352,128]{2,1,0:T(8,128)(2,1)S(1)}) custom-call(s32[3]{0:T(128)S(1)} %copy-done.2, bf16[512,3072]{1,0:T(8,128)(2,1)S(1)} %shard_map.40.near, bf16[384,3072]{1,0:T(8,128)(2,1)S(1)} %get-tuple-element.50.ahead, bf16[384,3072]{1,0:T(8,128)(2,1)S(1)} %get-tuple-element.51.behind, ...), custom_call_target="tpu_custom_call" | custom-call | flops 1207959552 | bytes 9437184 | tf_op jit(solution)/shard_map/pallas_call | solution.py:206
  88.2 0.9 collective-permute-start.8
  89.2 2.2 %collective-permute-start.9 = (bf16[672,128]{1,0:T(8,128)(2,1)S(1)}, bf16[672,128]{1,0:T(8,128)(2,1)S(1)}, u32[]{:S(2)}, u32[]{:S(2)}) collective-permute-start(bf16[672,128]{1,0:T(8,128)(2,1)S(1)} %get-tuple-element.46), channel_id=1, source_target_pairs={{0,2},{1,3},{2,4},{3,5},{4,6},{5,7},{6,0},{7,1},{8,10},{9,11},{10,... | collective-permute-start | bytes 516104 | tf_op jit(solution)/shard_map/ppermute | solution.py:40
  92.0 2.6 %collective-permute-start.11 = (bf16[352,128]{1,0:T(8,128)(2,1)S(1)}, bf16[352,128]{1,0:T(8,128)(2,1)S(1)}, u32[]{:S(2)}, u32[]{:S(2)}) collective-permute-start(bf16[352,128]{1,0:T(8,128)(2,1)S(1)} %get-tuple-element.56), channel_id=1, source_target_pairs={{0,4},{1,5},{2,6},{3,7},{4,0},{5,1},{6,2},{7,3},{8,12},{9,13},{10,... | collective-permute-start | bytes 270344 | tf_op jit(solution)/shard_map/ppermute | solution.py:40
  95.1 5.9 %collective-permute-done.10.three = bf16[672,128]{1,0:T(8,128)(2,1)S(1)} collective-permute-done((bf16[672,128]{1,0:T(8,128)(2,1)S(1)}, bf16[672,128]{1,0:T(8,128)(2,1)S(1)}, u32[]{:S(2)}, u32[]{:S(2)}) %collective-permute-start.10) | collective-permute-done | bytes 172064 | tf_op jit(solution)/shard_map/ppermute | solution.py:40
  101.1 2.4 %collective-permute-done.12.two = bf16[352,128]{1,0:T(8,128)(2,1)S(1)} collective-permute-done((bf16[352,128]{1,0:T(8,128)(2,1)S(1)}, bf16[352,128]{1,0:T(8,128)(2,1)S(1)}, u32[]{:S(2)}, u32[]{:S(2)}) %collective-permute-start.12) | collective-permute-done | bytes 90144 | tf_op jit(solution)/shard_map/ppermute | solution.py:40
  103.6 3.2 %collective-permute-done.13.three = bf16[352,128]{1,0:T(8,128)(2,1)S(1)} collective-permute-done((bf16[352,128]{1,0:T(8,128)(2,1)S(1)}, bf16[352,128]{1,0:T(8,128)(2,1)S(1)}, u32[]{:S(2)}, u32[]{:S(2)}) %collective-permute-start.13) | collective-permute-done | bytes 90144 | tf_op jit(solution)/shard_map/ppermute | solution.py:40
  107.4 5.0 %collective-permute-start.15 = (bf16[512,128]{1,0:T(8,128)(2,1)S(1)}, bf16[512,128]{1,0:T(8,128)(2,1)S(1)}, u32[]{:S(2)}, u32[]{:S(2)}) collective-permute-start(bf16[512,128]{1,0:T(8,128)(2,1)S(1)} %get-tuple-element.64), channel_id=1, source_target_pairs={{8,16},{24,32},{40,48},{56,64},{72,80},{88,96},{104,112},{120,128}... | collective-permute-start | bytes 393224 | tf_op jit(solution)/shard_map/ppermute | solution.py:31
  113.3 4.3 %collective-permute-done.15.second = bf16[512,128]{1,0:T(8,128)(2,1)S(1)} collective-permute-done((bf16[512,128]{1,0:T(8,128)(2,1)S(1)}, bf16[512,128]{1,0:T(8,128)(2,1)S(1)}, u32[]{:S(2)}, u32[]{:S(2)}) %collective-permute-start.15) | collective-permute-done | bytes 131104 | tf_op jit(solution)/shard_map/ppermute | solution.py:31
  117.6 1.6 %shard_map.48 = f32[1,4,64,512]{3,2,1,0:T(8,128)} custom-call(s32[3]{0:T(128)S(1)} %copy-done.2, bf16[512,512]{1,0:T(8,128)(2,1)S(1)} %fusion.order, f32[64,512]{1,0:T(8,128)S(1)} %shard_map.47.upper, bf16[512,128]{1,0:T(8,128)(2,1)S(1)} %collective-permute-done.14.first, bf16[512,128]{1,0:T(8,128)(2,1)S(1)} %collective-permute-done.15.second), custom_call_target="tpu_custom_call" | custom-call | flops 67108864 | bytes 1048576 | tf_op jit(solution)/shard_map/pallas_call | solution.py:367
  (33 shorter events, 5.3 us)
Async XLA Ops:
  7.3 59.4 %collective-permute-start.2 = (bf16[256,3072]{1,0:T(8,128)(2,1)}, bf16[256,3072]{1,0:T(8,128)(2,1)}, u32[]{:S(2)}, u32[]{:S(2)}) collective-permute-start(bf16[256,3072]{1,0:T(8,128)(2,1)} %get-tuple-element.37), channel_id=1, source_target_pairs={{0,8},{16,24},{32,40},{48,56},{64,72},{80,88},{96,104},{112,120},{... | collective-permute-start | bytes 4718600 | tf_op jit(solution)/shard_map/ppermute | solution.py:31
  8.1 58.6 %collective-permute-start.3 = (bf16[256,3072]{1,0:T(8,128)(2,1)}, bf16[256,3072]{1,0:T(8,128)(2,1)}, u32[]{:S(2)}, u32[]{:S(2)}) collective-permute-start(bf16[256,3072]{1,0:T(8,128)(2,1)} %get-tuple-element.42), channel_id=1, source_target_pairs={{8,16},{24,32},{40,48},{56,64},{72,80},{88,96},{104,112},{120,128}... | collective-permute-start | bytes 4718600 | tf_op jit(solution)/shard_map/ppermute | solution.py:31
  13.7 48.0 %collective-permute-start = (bf16[128,3072]{1,0:T(8,128)(2,1)}, bf16[128,3072]{1,0:T(8,128)(2,1)}, u32[]{:S(2)}, u32[]{:S(2)}) collective-permute-start(bf16[128,3072]{1,0:T(8,128)(2,1)} %get-tuple-element.35), channel_id=1, source_target_pairs={{0,8},{16,24},{32,40},{48,56},{64,72},{80,88},{96,104},{112,120},{... | collective-permute-start | bytes 2359304 | tf_op jit(solution)/shard_map/ppermute | solution.py:31
  13.8 7.8 %copy-start = (bf16[1,6,512,512]{3,2,1,0:T(8,128)(2,1)S(1)}, bf16[1,6,512,512]{3,2,1,0:T(8,128)(2,1)}, u32[]{:S(2)}) copy-start(bf16[1,6,512,512]{3,2,1,0:T(8,128)(2,1)} %param.3) | copy-start | bytes 9437188
  13.8 7.8 %copy-start.3 = (s32[1,2]{1,0:T(1,128)S(1)}, s32[1,2]{1,0:T(1,128)}, u32[]{:S(2)}) copy-start(s32[1,2]{1,0:T(1,128)} %flag.7) | copy-start | bytes 28
  13.8 52.8 %collective-permute-start.1 = (bf16[128,3072]{1,0:T(8,128)(2,1)}, bf16[128,3072]{1,0:T(8,128)(2,1)}, u32[]{:S(2)}, u32[]{:S(2)}) collective-permute-start(bf16[128,3072]{1,0:T(8,128)(2,1)} %get-tuple-element.41), channel_id=1, source_target_pairs={{8,16},{24,32},{40,48},{56,64},{72,80},{88,96},{104,112},{120,128}... | collective-permute-start | bytes 2359304 | tf_op jit(solution)/shard_map/ppermute | solution.py:31
  21.6 55.7 %collective-permute-start.5 = (bf16[128,3072]{1,0:T(8,128)(2,1)}, bf16[128,3072]{1,0:T(8,128)(2,1)S(1)}, u32[]{:S(2)}, u32[]{:S(2)}) collective-permute-start(bf16[128,3072]{1,0:T(8,128)(2,1)} %get-tuple-element.39), channel_id=1, source_target_pairs={{0,8},{16,24},{32,40},{48,56},{64,72},{80,88},{96,104},{112,120},{... | collective-permute-start | bytes 2359304 | tf_op jit(solution)/shard_map/ppermute | solution.py:31
  21.6 1.2 %copy-start.1 = (bf16[1,2,512,512]{3,2,1,0:T(8,128)(2,1)S(1)}, bf16[1,2,512,512]{3,2,1,0:T(8,128)(2,1)}, u32[]{:S(2)}) copy-start(bf16[1,2,512,512]{3,2,1,0:T(8,128)(2,1)} %param.4) | copy-start | bytes 3145732
  22.8 38.9 %copy-start.4 = (bf16[128,3072]{1,0:T(8,128)(2,1)S(1)}, bf16[128,3072]{1,0:T(8,128)(2,1)}, u32[]{:S(2)}) copy-start(bf16[128,3072]{1,0:T(8,128)(2,1)} %get-tuple-element.52) | copy-start | bytes 2359300
  22.8 43.9 %copy-start.2 = (s32[3]{0:T(128)S(1)}, s32[3]{0:T(128)}, u32[]{:S(2)}) copy-start(s32[3]{0:T(128)} %pad_add_fusion.place) | copy-start | bytes 40
  61.7 22.5 %collective-permute-start.6 = (bf16[128,3072]{1,0:T(8,128)(2,1)S(1)}, bf16[128,3072]{1,0:T(8,128)(2,1)S(1)}, u32[]{:S(2)}, u32[]{:S(2)}) collective-permute-start(bf16[128,3072]{1,0:T(8,128)(2,1)S(1)} %copy-done.4), channel_id=1, source_target_pairs={{8,16},{24,32},{40,48},{56,64},{72,80},{88,96},{104,112},{120,128}... | collective-permute-start | bytes 2359304 | tf_op jit(solution)/shard_map/ppermute | solution.py:31
  72.4 2.2 %collective-permute-start.4 = (bf16[4,672,128]{2,1,0:T(8,128)(2,1)S(1)}, bf16[4,672,128]{2,1,0:T(8,128)(2,1)S(1)}, u32[]{:S(2)}, u32[]{:S(2)}) collective-permute-start(bf16[4,672,128]{2,1,0:T(8,128)(2,1)S(1)} %get-tuple-element.44), channel_id=1, source_target_pairs={{0,1},{1,0},{2,3},{3,2},{4,5},{5,4},{6,7},{7,6},{8,9},{9,8},{10,11... | collective-permute-start | bytes 2064392 | tf_op jit(solution)/shard_map/ppermute | solution.py:35
  87.3 4.0 %collective-permute-start.7 = (bf16[4,352,128]{2,1,0:T(8,128)(2,1)S(1)}, bf16[4,352,128]{2,1,0:T(8,128)(2,1)S(1)}, u32[]{:S(2)}, u32[]{:S(2)}) collective-permute-start(bf16[4,352,128]{2,1,0:T(8,128)(2,1)S(1)} %get-tuple-element.54), channel_id=1, source_target_pairs={{0,1},{1,0},{2,3},{3,2},{4,5},{5,4},{6,7},{7,6},{8,9},{9,8},{10,11... | collective-permute-start | bytes 1081352 | tf_op jit(solution)/shard_map/ppermute | solution.py:35
  87.4 13.6 %collective-permute-start.10 = (bf16[672,128]{1,0:T(8,128)(2,1)S(1)}, bf16[672,128]{1,0:T(8,128)(2,1)S(1)}, u32[]{:S(2)}, u32[]{:S(2)}) collective-permute-start(bf16[672,128]{1,0:T(8,128)(2,1)S(1)} %get-tuple-element.48), channel_id=1, source_target_pairs={{0,6},{1,7},{2,0},{3,1},{4,2},{5,3},{6,4},{7,5},{8,14},{9,15},{10,... | collective-permute-start | bytes 516104 | tf_op jit(solution)/shard_map/ppermute | solution.py:40
  88.2 12.8 %collective-permute-start.8 = (bf16[672,128]{1,0:T(8,128)(2,1)S(1)}, bf16[672,128]{1,0:T(8,128)(2,1)S(1)}, u32[]{:S(2)}, u32[]{:S(2)}) collective-permute-start(bf16[672,128]{1,0:T(8,128)(2,1)S(1)} %get-tuple-element.47), channel_id=1, source_target_pairs={{0,4},{1,5},{2,6},{3,7},{4,0},{5,1},{6,2},{7,3},{8,12},{9,13},{10,... | collective-permute-start | bytes 516104 | tf_op jit(solution)/shard_map/ppermute | solution.py:40
  89.2 11.9 %collective-permute-start.9 = (bf16[672,128]{1,0:T(8,128)(2,1)S(1)}, bf16[672,128]{1,0:T(8,128)(2,1)S(1)}, u32[]{:S(2)}, u32[]{:S(2)}) collective-permute-start(bf16[672,128]{1,0:T(8,128)(2,1)S(1)} %get-tuple-element.46), channel_id=1, source_target_pairs={{0,2},{1,3},{2,4},{3,5},{4,6},{5,7},{6,0},{7,1},{8,10},{9,11},{10,... | collective-permute-start | bytes 516104 | tf_op jit(solution)/shard_map/ppermute | solution.py:40
  92.0 9.2 %collective-permute-start.11 = (bf16[352,128]{1,0:T(8,128)(2,1)S(1)}, bf16[352,128]{1,0:T(8,128)(2,1)S(1)}, u32[]{:S(2)}, u32[]{:S(2)}) collective-permute-start(bf16[352,128]{1,0:T(8,128)(2,1)S(1)} %get-tuple-element.56), channel_id=1, source_target_pairs={{0,4},{1,5},{2,6},{3,7},{4,0},{5,1},{6,2},{7,3},{8,12},{9,13},{10,... | collective-permute-start | bytes 270344 | tf_op jit(solution)/shard_map/ppermute | solution.py:40
  94.5 9.0 %collective-permute-start.12 = (bf16[352,128]{1,0:T(8,128)(2,1)S(1)}, bf16[352,128]{1,0:T(8,128)(2,1)S(1)}, u32[]{:S(2)}, u32[]{:S(2)}) collective-permute-start(bf16[352,128]{1,0:T(8,128)(2,1)S(1)} %get-tuple-element.55), channel_id=1, source_target_pairs={{0,2},{1,3},{2,4},{3,5},{4,6},{5,7},{6,0},{7,1},{8,10},{9,11},{10,... | collective-permute-start | bytes 270344 | tf_op jit(solution)/shard_map/ppermute | solution.py:40
  101.0 5.7 %collective-permute-start.13 = (bf16[352,128]{1,0:T(8,128)(2,1)S(1)}, bf16[352,128]{1,0:T(8,128)(2,1)S(1)}, u32[]{:S(2)}, u32[]{:S(2)}) collective-permute-start(bf16[352,128]{1,0:T(8,128)(2,1)S(1)} %get-tuple-element.57), channel_id=1, source_target_pairs={{0,6},{1,7},{2,0},{3,1},{4,2},{5,3},{6,4},{7,5},{8,14},{9,15},{10,... | collective-permute-start | bytes 270344 | tf_op jit(solution)/shard_map/ppermute | solution.py:40
  107.3 6.0 %collective-permute-start.14 = (bf16[512,128]{1,0:T(8,128)(2,1)S(1)}, bf16[512,128]{1,0:T(8,128)(2,1)S(1)}, u32[]{:S(2)}, u32[]{:S(2)}) collective-permute-start(bf16[512,128]{1,0:T(8,128)(2,1)S(1)} %get-tuple-element.63), channel_id=1, source_target_pairs={{0,8},{16,24},{32,40},{48,56},{64,72},{80,88},{96,104},{112,120},{... | collective-permute-start | bytes 393224 | tf_op jit(solution)/shard_map/ppermute | solution.py:31
  107.4 10.2 %collective-permute-start.15 = (bf16[512,128]{1,0:T(8,128)(2,1)S(1)}, bf16[512,128]{1,0:T(8,128)(2,1)S(1)}, u32[]{:S(2)}, u32[]{:S(2)}) collective-permute-start(bf16[512,128]{1,0:T(8,128)(2,1)S(1)} %get-tuple-element.64), channel_id=1, source_target_pairs={{8,16},{24,32},{40,48},{56,64},{72,80},{88,96},{104,112},{120,128}... | collective-permute-start | bytes 393224 | tf_op jit(solution)/shard_map/ppermute | solution.py:31

commit v2 on v1

--- a/solution.py
+++ b/solution.py
@@ -11,7 +11,7 @@
 SMEM = pl.BlockSpec(memory_space=pltpu.SMEM)
 LANES = 128
 ROWS, PARTS, STEP = 64, 8, 3
-CHUNKS = ((0, 16), (32, 32), (16, 16))
+CHUNKS = ((0, 16, 0, 6), (32, 32, 0, 6), (16, 16, 0, 3), (16, 16, 3, 3))
 EARLY, LATE = 384, 128
 EARLY_U1, EARLY_U2, EARLY_ALL = 192, 144, 672
 LATE_U1, LATE_U2, LATE_ALL = 64, 112, 352
@@ -40,13 +40,22 @@
     return lax.ppermute(value, "aux", [(i, (i + 2 * steps) % count) for i in range(count)])
 
 
-def split(place, factors, density, screen, start, size):
-    count, width = factors.shape[0], factors.shape[-1]
+def spot():
+    aux = lax.axis_index("aux")
+    return lax.rem(aux, 2), lax.div(aux, 2)
+
+
+def on_even():
+    return lax.rem(lax.axis_index("atoms"), 2) == 0
+
+
+def split(factors, density, screen, start, size, begin, count):
+    width = factors.shape[-1]
     height = PARTS * size
 
-    def kernel(place, flag, left, right, first, second):
+    def kernel(flag, left, right, first, second):
         scale = flag[0, 1].astype(F32).astype(BF16)
-        even = place[2] == 0
+        even = on_even()
         for step in range(STEP):
             columns = pl.ds(step * width, width)
             piece = left[step].reshape(height, width)
@@ -59,14 +68,13 @@
         grid=(count // STEP,),
         in_specs=[
             SMEM,
-            SMEM,
-            pl.BlockSpec((STEP, PARTS, size, width), lambda i: (i, 0, start // size, 0)),
+            pl.BlockSpec((STEP, PARTS, size, width), lambda i: (begin // STEP + i, 0, start // size, 0)),
             pl.BlockSpec((1, width, width), lambda i: (1, 0, 0)),
         ],
         out_specs=[pl.BlockSpec((height, STEP * width), lambda i: (0, i))] * 2,
         out_shape=[jax.ShapeDtypeStruct((height, count * width), BF16)] * 2,
         cost_estimate=cost(2 * height * count * width**2, 6 * height * count * width),
-    )(place, screen, factors, density)
+    )(screen, factors, density)
 
 
 def transform(factors, density, screen):
@@ -119,28 +127,29 @@
     return pl.ds(index * LANES, LANES)
 
 
-def pick(place, first, second):
-    even = place[2] == 0
+def pick(first, second):
+    even = on_even()
     first, second = first[...], second[...]
     return jnp.where(even, first, second), jnp.where(even, second, first)
 
 
-def pack_early(place, near, first, second):
+def pack_early(near, first, second):
     width, depth = near.shape
     places = PARTS // 2
 
-    def kernel(place, near, first0, second0, first1, second1, kept, sent, ahead, behind, upper, lower, upper_far, lower_far):
+    def kernel(near, first0, second0, first1, second1, kept, sent, ahead, behind, upper, lower, upper_far, lower_far):
         low, high = pl.ds(0, 128), pl.ds(128, 256)
-        ahead[low, :], behind[low, :] = pick(place, first0, second0)
-        ahead[high, :], behind[high, :] = pick(place, first1, second1)
+        ahead[low, :], behind[low, :] = pick(first0, second0)
+        ahead[high, :], behind[high, :] = pick(first1, second1)
         value = contract(near[...], ahead[...])
         upper[...] = value
         lower[...] = value.T
         value = contract(behind[...], ahead[...])
         upper_far[...] = value
         lower_far[...] = value.T
+        mine = spot()[0]
         for y in range(places):
-            for out, core in ((sent, 1 - place[0]), (kept, place[0])):
+            for out, core in ((sent, 1 - mine), (kept, mine)):
                 part = 2 * y + core
                 own = pl.ds(pl.multiple_of(ROWS * part, ROWS), ROWS)
                 at = put(out, y, 0, [upper[own, lanes(t)] for t in range(3)])
@@ -154,7 +163,7 @@
     shape = (places, EARLY_ALL, LANES)
     return pl.pallas_call(
         kernel,
-        in_specs=[SMEM] + [VMEM] * 5,
+        in_specs=[VMEM] * 5,
         out_specs=[VMEM] * 4,
         out_shape=[
             jax.ShapeDtypeStruct(shape, F32),
@@ -170,29 +179,54 @@
         ],
         compiler_params=params(),
         cost_estimate=cost(2 * near.size * EARLY * 2, near.size * 4),
-    )(place, near, first[0], second[0], first[1], second[1])
-
-
-def pack_late(place, near, ahead, behind, first, second):
+    )(near, first[0], second[0], first[1], second[1])
+
+
+def pack_middle(near, ahead, behind, first, second):
+    width = near.shape[0]
+    depth = first.shape[1]
+
+    def kernel(near, ahead, behind, first, second, upper, tall, tall_t, corner):
+        last, prior = pick(first, second)
+        columns = pl.ds(0, depth)
+        upper[...] = contract(near[:, columns], last)
+        tall[...] = contract(behind[:, columns], last)
+        tall_t[...] = contract(ahead[:, columns], prior)
+        corner[...] = contract(prior, last)
+
+    return pl.pallas_call(
+        kernel,
+        in_specs=[VMEM] * 5,
+        out_specs=[VMEM] * 4,
+        out_shape=[jax.ShapeDtypeStruct((height, LATE), F32) for height in (width, EARLY, EARLY, LATE)],
+        compiler_params=params(),
+        cost_estimate=cost(near.size * LATE * 3, near.size * 6),
+    )(near, ahead, behind, first, second)
+
+
+def pack_late(near, ahead, behind, middle, first, second):
     width = near.shape[0]
     places = PARTS // 2
-
-    def kernel(place, near, ahead, behind, first, second, kept, sent, upper, lower, tall, wide, tall_t, wide_t):
-        last, prior = pick(place, first, second)
-        value = contract(near[...], last)
+    depth = first.shape[1]
+
+    def kernel(near, ahead, behind, upper0, tall0, tall_t0, corner0, first, second, kept, sent, upper, lower, tall, wide, tall_t, wide_t):
+        last, prior = pick(first, second)
+        columns = pl.ds(near.shape[1] - depth, depth)
+        value = upper0[...] + contract(near[:, columns], last)
         upper[...] = value
         lower[...] = value.T
-        value = contract(behind[...], last)
+        value = tall0[...] + contract(behind[:, columns], last)
         tall[...] = value
         wide_t[:, pl.ds(0, EARLY)] = value.T
-        value = contract(ahead[...], prior)
+        value = tall_t0[...] + contract(ahead[:, columns], prior)
         tall_t[...] = value
         wide[:, pl.ds(0, EARLY)] = value.T
-        value = contract(prior, last)
+        value = corner0[...] + contract(prior, last)
         wide[:, pl.ds(EARLY, LATE)] = value
         wide_t[:, pl.ds(EARLY, LATE)] = value.T
+        mine = spot()[0]
         for y in range(places):
-            for out, core in ((sent, 1 - place[0]), (kept, place[0])):
+            for out, core in ((sent, 1 - mine), (kept, mine)):
                 part = 2 * y + core
                 own = pl.ds(pl.multiple_of(ROWS * part, ROWS), ROWS)
                 at = put(out, y, 0, [upper[own, :]])
@@ -205,7 +239,7 @@
     shape = (places, LATE_ALL, LANES)
     return pl.pallas_call(
         kernel,
-        in_specs=[SMEM] + [VMEM] * 5,
+        in_specs=[VMEM] * 9,
         out_specs=[VMEM] * 2,
         out_shape=[jax.ShapeDtypeStruct(shape, F32), jax.ShapeDtypeStruct(shape, BF16)],
         scratch_shapes=[
@@ -217,15 +251,15 @@
             pltpu.VMEM((LATE, width), F32),
         ],
         compiler_params=params(),
-        cost_estimate=cost(2 * near.size * LATE * 3, near.size * 6),
-    )(place, near, ahead, behind, first, second)
-
-
-def join_core(place, kept, received):
+        cost_estimate=cost(near.size * LATE * 3, near.size * 6),
+    )(near, ahead, behind, *middle, first, second)
+
+
+def join_core(kept, received):
     places, rows, width = kept.shape
 
-    def kernel(place, kept, received, total, *pieces):
-        y = place[1]
+    def kernel(kept, received, total, *pieces):
+        y = spot()[1]
         total[...] = kept[y] + received[y].astype(F32)
         for steps in range(1, places):
             target = lax.rem(y + steps, places)
@@ -234,12 +268,12 @@
     shape = (rows, width)
     return pl.pallas_call(
         kernel,
-        in_specs=[SMEM, VMEM, VMEM],
+        in_specs=[VMEM, VMEM],
         out_specs=[VMEM] * places,
         out_shape=[jax.ShapeDtypeStruct(shape, F32)] + [jax.ShapeDtypeStruct(shape, BF16)] * (places - 1),
         compiler_params=params(),
         cost_estimate=cost(kept.size, 8 * kept.size),
-    )(place, kept, received)
+    )(kept, received)
 
 
 def after(value, *others):
@@ -282,15 +316,15 @@
     )(total, *received)
 
 
-def join_late(place, rest, total, received):
+def join_late(rest, total, received):
     rows, width = total.shape
     far = EARLY_U2 + LATE_U2
     low = rest.shape[0] - EARLY_U2
     height = low + rows - LATE_U1 - LATE_U2
 
-    def kernel(place, rest, total, one, two, three, upper, first, second):
+    def kernel(rest, total, one, two, three, upper, first, second):
         refs = (total, one, two, three)
-        even = place[2] == 0
+        even = on_even()
         upper[...] = gather(refs, pl.ds(0, LATE_U1))
         late_far = gather(refs, pl.ds(LATE_U1, LATE_U2)).astype(BF16)
         late_low = gather(refs, pl.ds(LATE_U1 + LATE_U2, rows - LATE_U1 - LATE_U2)).astype(BF16)
@@ -307,7 +341,7 @@
 
     return pl.pallas_call(
         kernel,
-        in_specs=[SMEM] + [VMEM] * 5,
+        in_specs=[VMEM] * 5,
         out_specs=[VMEM] * 3,
         out_shape=[
             jax.ShapeDtypeStruct((LATE_U1, width), F32),
@@ -316,7 +350,7 @@
         ],
         compiler_params=params(),
         cost_estimate=cost(total.size * 3, 12 * total.size),
-    )(place, rest, total, *received)
+    )(rest, total, *received)
 
 
 def restore(order, early, late):
@@ -338,7 +372,7 @@
     )(order, early, late)
 
 
-def assemble(place, order, upper, first, second):
+def assemble(order, upper, first, second):
     width = order.shape[0]
     late_low = 3 * 144 - 96
 
@@ -349,7 +383,8 @@
         last = jnp.concatenate([ref[pl.ds(late + 48 + 16 * t, 16), :] for t in range(4)], axis=1)
         return jnp.concatenate([body[:16], last, body[16:]], axis=0)
 
-    def kernel(place, order, upper, first, second, out):
+    def kernel(order, upper, first, second, out):
+        even = on_even()
         out[0, 0] = upper[...]
 
         def write(far, low):
@@ -361,17 +396,17 @@
                 out[0, 2, pl.ds(32, 32), lanes(t)] = low[pl.ds(48 * t + 16, 32), :].astype(F32)
             out[0, 3] = jnp.dot(rows(low, 192, late_low + 64), exact, preferred_element_type=F32)
 
-        pl.when(place[2] == 0)(lambda: write(first, second))
-        pl.when(place[2] != 0)(lambda: write(second, first))
-
-    return pl.pallas_call(
-        kernel,
-        in_specs=[SMEM] + [VMEM] * 4,
+        pl.when(even)(lambda: write(first, second))
+        pl.when(jnp.logical_not(even))(lambda: write(second, first))
+
+    return pl.pallas_call(
+        kernel,
+        in_specs=[VMEM] * 4,
         out_specs=VMEM,
         out_shape=jax.ShapeDtypeStruct((1, 4, ROWS, width), F32),
         compiler_params=params(),
         cost_estimate=cost(2 * 2 * ROWS * width**2, 4 * ROWS * width * 8),
-    )(place, order, upper, first, second)
+    )(order, upper, first, second)
 
 
 def natural_order(width):
@@ -386,29 +421,28 @@
 def body(factors, density, screen):
     count, width = factors.shape[1], factors.shape[2]
     owned, blocks = factors[0].reshape(count, PARTS, ROWS, width), density[0]
-    position = lax.axis_index("aux")
-    place = jnp.stack([position % 2, position // 2, lax.axis_index("atoms") % 2]).astype(jnp.int32)
     first, second = [], []
     source = owned
-    for start, size in CHUNKS:
-        one, two = split(place, source, blocks, screen, start, size)
+    for chunk in CHUNKS:
+        one, two = split(source, blocks, screen, *chunk)
         source = after(owned, one)
+        second.append(swap_atoms(two, 1))
         first.append(swap_atoms(one, 0))
-        second.append(swap_atoms(two, 1))
     near = transform(source, blocks, screen)
-    kept, sent, ahead, behind = pack_early(place, near, first[:2], second[:2])
-    total, *pieces = join_core(place, kept, swap_core(sent))
+    kept, sent, ahead, behind = pack_early(near, first[:2], second[:2])
+    total, *pieces = join_core(kept, swap_core(sent))
     received = send_places(pieces)
-    kept, sent = pack_late(after(place, *pieces), near, ahead, behind, first[2], second[2])
-    late_total, *late_pieces = join_core(place, kept, swap_core(sent))
+    middle = pack_middle(near, ahead, behind, first[2], second[2])
+    kept, sent = pack_late(near, ahead, behind, middle, first[3], second[3])
+    late_total, *late_pieces = join_core(kept, swap_core(sent))
     late_received = send_places(late_pieces)
     upper, rest = join_early(after(total, *late_pieces), received)
-    late_upper, one, two = join_late(place, rest, late_total, late_received)
+    late_upper, one, two = join_late(rest, late_total, late_received)
+    two = swap_atoms(two, 1)
     one = swap_atoms(one, 0)
-    two = swap_atoms(two, 1)
     order = natural_order(width)
     upper = restore(order, upper, late_upper)
-    return assemble(place, order, upper, one, two)
+    return assemble(order, upper, one, two)
 
 
 def solution(mesh):

time: 120 us -> 119 us (level)
  the two profiles are of different devices: /device:TPU:126 before, /device:TPU:136 now
where the time goes in v2:
time: 119 us
  waiting for transfers between devices  59.4 us (50%)
  starting transfers between devices  32.4 us (27%)
  Pallas kernels  25.4 us (21%)
  local copies, waits for them, and re-layouts  1.24 us (1%)
    ppermute x10, waiting for transfers between devices, swap_atoms(): return lax.ppermute(value, 'atoms', pairs + [(j, i) for i, j in pairs])  52.4 us
    ppermute x10, starting transfers between devices, swap_atoms(): return lax.ppermute(value, 'atoms', pairs + [(j, i) for i, j in pairs])  23.3 us
    pallas_call x4, Pallas kernels, split(): pl.pallas_call(kernel, grid=(count // STEP,), in_specs=[SMEM, pl.BlockSpe...  11.7 us
    ppermute x6, starting transfers between devices, shift_y(): lax.ppermute(value, 'aux', [(i, (i + 2 * steps) % count) for i in range(c...  8.91 us
    ppermute x6, waiting for transfers between devices, shift_y(): lax.ppermute(value, 'aux', [(i, (i + 2 * steps) % count) for i in range(c...  6.97 us
    pallas_call x1, Pallas kernels, pack_early(): pl.pallas_call(kernel, in_specs=[VMEM] * 5, out_specs=[VMEM] * 4, out_sha...  6 us
    pallas_call x1, Pallas kernels, transform(): pl.pallas_call(kernel, grid=(count // STEP,), in_specs=[SMEM, pl.BlockSpe...  2.73 us
  transfers between devices with their start and end apart: 18, of which 10 were waited for; matrix products, arithmetic and copies ran while one was open for 0% of the time, Pallas kernels for 15%

profile of v2, /device:TPU:136, one launch (start us, length us, event | category | flops | bytes accessed | tf_op | source)
XLA Modules:
  0.0 118.8 jit_solution(13018487768455824423)
XLA Ops:
  0.0 2.9 %shard_map.37 = (bf16[128,3072]{1,0:T(8,128)(2,1)}, bf16[128,3072]{1,0:T(8,128)(2,1)}) custom-call(s32[1,2]{1,0:T(1,128)} %flag.9, bf16[6,8,64,512]{3,2,1,0:T(8,128)(2,1)} %bitcast.2, bf16[2,512,512]{2,1,0:T(8,128)(2,1)} %bitcast.7), custom_call_target="tpu_custom_call" | custom-call | flops 402653184 | bytes 2359296 | tf_op jit(solution)/shard_map/pallas_call | solution.py:66
  2.9 3.7 %shard_map.38 = (bf16[256,3072]{1,0:T(8,128)(2,1)}, bf16[256,3072]{1,0:T(8,128)(2,1)}) custom-call(s32[1,2]{1,0:T(1,128)} %flag.9, bf16[6,8,64,512]{3,2,1,0:T(8,128)(2,1)} %bitcast.3, bf16[2,512,512]{2,1,0:T(8,128)(2,1)} %bitcast.8), custom_call_target="tpu_custom_call" | custom-call | flops 805306368 | bytes 4718592 | tf_op jit(solution)/shard_map/pallas_call | solution.py:66
  6.6 1.5 %collective-permute-start.2 = (bf16[256,3072]{1,0:T(8,128)(2,1)}, bf16[256,3072]{1,0:T(8,128)(2,1)}, u32[]{:S(2)}, u32[]{:S(2)}) collective-permute-start(bf16[256,3072]{1,0:T(8,128)(2,1)} %get-tuple-element.43), channel_id=1, source_target_pairs={{0,8},{16,24},{32,40},{48,56},{64,72},{80,88},{96,104},{112,120},{... | collective-permute-start | bytes 4718600 | tf_op jit(solution)/shard_map/ppermute | solution.py:31
  8.1 3.5 %collective-permute-start.3 = (bf16[256,3072]{1,0:T(8,128)(2,1)}, bf16[256,3072]{1,0:T(8,128)(2,1)}, u32[]{:S(2)}, u32[]{:S(2)}) collective-permute-start(bf16[256,3072]{1,0:T(8,128)(2,1)} %get-tuple-element.50), channel_id=1, source_target_pairs={{8,16},{24,32},{40,48},{56,64},{72,80},{88,96},{104,112},{120,128}... | collective-permute-start | bytes 4718600 | tf_op jit(solution)/shard_map/ppermute | solution.py:31
  12.8 4.6 %collective-permute-start.1 = (bf16[128,3072]{1,0:T(8,128)(2,1)}, bf16[128,3072]{1,0:T(8,128)(2,1)}, u32[]{:S(2)}, u32[]{:S(2)}) collective-permute-start(bf16[128,3072]{1,0:T(8,128)(2,1)} %get-tuple-element.49), channel_id=1, source_target_pairs={{8,16},{24,32},{40,48},{56,64},{72,80},{88,96},{104,112},{120,128}... | collective-permute-start | bytes 2359304 | tf_op jit(solution)/shard_map/ppermute | solution.py:31
  17.4 2.4 %shard_map.39 = (bf16[128,1536]{1,0:T(8,128)(2,1)}, bf16[128,1536]{1,0:T(8,128)(2,1)}) custom-call(s32[1,2]{1,0:T(1,128)} %flag.9, bf16[6,8,64,512]{3,2,1,0:T(8,128)(2,1)} %bitcast.4, bf16[2,512,512]{2,1,0:T(8,128)(2,1)} %bitcast.9), custom_call_target="tpu_custom_call" | custom-call | flops 201326592 | bytes 1179648 | tf_op jit(solution)/shard_map/pallas_call | solution.py:66
  19.9 2.6 %shard_map.40 = (bf16[128,1536]{1,0:T(8,128)(2,1)}, bf16[128,1536]{1,0:T(8,128)(2,1)}) custom-call(s32[1,2]{1,0:T(1,128)} %flag.9, bf16[6,8,64,512]{3,2,1,0:T(8,128)(2,1)} %bitcast.5, bf16[2,512,512]{2,1,0:T(8,128)(2,1)} %bitcast.10), custom_call_target="tpu_custom_call" | custom-call | flops 201326592 | bytes 1179648 | tf_op jit(solution)/shard_map/pallas_call | solution.py:66
  23.7 2.7 %shard_map.41.near = bf16[512,3072]{1,0:T(8,128)(2,1)S(1)} custom-call(s32[1,2]{1,0:T(1,128)S(1)} %copy-done.2, bf16[6,8,64,512]{3,2,1,0:T(8,128)(2,1)S(1)} %bitcast.6, bf16[2,512,512]{2,1,0:T(8,128)(2,1)S(1)} %bitcast.11), custom_call_target="tpu_custom_call" | custom-call | flops 1610612736 | bytes 6291456 | tf_op jit(solution)/shard_map/pallas_call | solution.py:90
  26.4 34.6 %collective-permute-done.first0 = bf16[128,3072]{1,0:T(8,128)(2,1)} collective-permute-done((bf16[128,3072]{1,0:T(8,128)(2,1)}, bf16[128,3072]{1,0:T(8,128)(2,1)}, u32[]{:S(2)}, u32[]{:S(2)}) %collective-permute-start) | collective-permute-done | bytes 786464 | tf_op jit(solution)/shard_map/ppermute | solution.py:31
  61.1 4.3 %collective-permute-start.6 = (bf16[128,1536]{1,0:T(8,128)(2,1)S(1)}, bf16[128,1536]{1,0:T(8,128)(2,1)S(1)}, u32[]{:S(2)}, u32[]{:S(2)}) collective-permute-start(bf16[128,1536]{1,0:T(8,128)(2,1)S(1)} %copy-done.5), channel_id=1, source_target_pairs={{8,16},{24,32},{40,48},{56,64},{72,80},{88,96},{104,112},{120,128}... | collective-permute-start | bytes 1179656 | tf_op jit(solution)/shard_map/ppermute | solution.py:31
  66.4 6.0 %shard_map.42 = (f32[4,672,128]{2,1,0:T(8,128)S(1)}, bf16[4,672,128]{2,1,0:T(8,128)(2,1)S(1)}, bf16[384,3072]{1,0:T(8,128)(2,1)S(1)}, bf16[384,3072]{1,0:T(8,128)(2,1)S(1)}) custom-call(bf16[512,3072]{1,0:T(8,128)(2,1)S(1)} %shard_map.41.near, bf16[128,3072]{1,0:T(8,128)(2,1)} %collective-permute-done.first0, ...), custom_call_target="tpu_custom_call" | custom-call | flops 2415919104 | bytes 6291456 | tf_op jit(solution)/shard_map/pallas_call | solution.py:164
  72.6 4.0 %collective-permute-start.8 = (bf16[128,1536]{1,0:T(8,128)(2,1)S(1)}, bf16[128,1536]{1,0:T(8,128)(2,1)S(1)}, u32[]{:S(2)}, u32[]{:S(2)}) collective-permute-start(bf16[128,1536]{1,0:T(8,128)(2,1)S(1)} %copy-done.3), channel_id=1, source_target_pairs={{8,16},{24,32},{40,48},{56,64},{72,80},{88,96},{104,112},{120,128}... | collective-permute-start | bytes 1179656 | tf_op jit(solution)/shard_map/ppermute | solution.py:31
  77.9 6.0 %collective-permute-done.7.first = bf16[128,1536]{1,0:T(8,128)(2,1)S(1)} collective-permute-done((bf16[128,1536]{1,0:T(8,128)(2,1)S(1)}, bf16[128,1536]{1,0:T(8,128)(2,1)S(1)}, u32[]{:S(2)}, u32[]{:S(2)}) %collective-permute-start.7) | collective-permute-done | bytes 393248 | tf_op jit(solution)/shard_map/ppermute | solution.py:31
  84.0 5.2 %collective-permute-done.8.second = bf16[128,1536]{1,0:T(8,128)(2,1)S(1)} collective-permute-done((bf16[128,1536]{1,0:T(8,128)(2,1)S(1)}, bf16[128,1536]{1,0:T(8,128)(2,1)S(1)}, u32[]{:S(2)}, u32[]{:S(2)}) %collective-permute-start.8) | collective-permute-done | bytes 393248 | tf_op jit(solution)/shard_map/ppermute | solution.py:31
  89.2 1.5 %shard_map.45 = (f32[4,352,128]{2,1,0:T(8,128)S(1)}, bf16[4,352,128]{2,1,0:T(8,128)(2,1)S(1)}) custom-call(bf16[512,3072]{1,0:T(8,128)(2,1)S(1)} %shard_map.41.near, bf16[384,3072]{1,0:T(8,128)(2,1)S(1)} %get-tuple-element.54.ahead, bf16[384,3072]{1,0:T(8,128)(2,1)S(1)} %get-tuple-element.55.behind, f32[512,128]{1,0:T(8,128)S(1)} %get-tuple-element.57.upper0, ...), custom_call_target="tpu_custom_call" | custom-call | flops 603979776 | bytes 9437184 | tf_op jit(solution)/shard_map/pallas_call | solution.py:240
  91.0 2.4 %collective-permute-start.10 = (bf16[672,128]{1,0:T(8,128)(2,1)S(1)}, bf16[672,128]{1,0:T(8,128)(2,1)S(1)}, u32[]{:S(2)}, u32[]{:S(2)}) collective-permute-start(bf16[672,128]{1,0:T(8,128)(2,1)S(1)} %get-tuple-element.68), channel_id=1, source_target_pairs={{0,4},{1,5},{2,6},{3,7},{4,0},{5,1},{6,2},{7,3},{8,12},{9,13},{10,... | collective-permute-start | bytes 516104 | tf_op jit(solution)/shard_map/ppermute | solution.py:40
  93.4 2.0 %collective-permute-start.12 = (bf16[672,128]{1,0:T(8,128)(2,1)S(1)}, bf16[672,128]{1,0:T(8,128)(2,1)S(1)}, u32[]{:S(2)}, u32[]{:S(2)}) collective-permute-start(bf16[672,128]{1,0:T(8,128)(2,1)S(1)} %get-tuple-element.70), channel_id=1, source_target_pairs={{0,6},{1,7},{2,0},{3,1},{4,2},{5,3},{6,4},{7,5},{8,14},{9,15},{10,... | collective-permute-start | bytes 516104 | tf_op jit(solution)/shard_map/ppermute | solution.py:40
  95.5 1.5 %collective-permute-start.13 = (bf16[352,128]{1,0:T(8,128)(2,1)S(1)}, bf16[352,128]{1,0:T(8,128)(2,1)S(1)}, u32[]{:S(2)}, u32[]{:S(2)}) collective-permute-start(bf16[352,128]{1,0:T(8,128)(2,1)S(1)} %get-tuple-element.65), channel_id=1, source_target_pairs={{0,4},{1,5},{2,6},{3,7},{4,0},{5,1},{6,2},{7,3},{8,12},{9,13},{10,... | collective-permute-start | bytes 270344 | tf_op jit(solution)/shard_map/ppermute | solution.py:40
  97.0 2.6 %collective-permute-start.14 = (bf16[352,128]{1,0:T(8,128)(2,1)S(1)}, bf16[352,128]{1,0:T(8,128)(2,1)S(1)}, u32[]{:S(2)}, u32[]{:S(2)}) collective-permute-start(bf16[352,128]{1,0:T(8,128)(2,1)S(1)} %get-tuple-element.64), channel_id=1, source_target_pairs={{0,2},{1,3},{2,4},{3,5},{4,6},{5,7},{6,0},{7,1},{8,10},{9,11},{10,... | collective-permute-start | bytes 270344 | tf_op jit(solution)/shard_map/ppermute | solution.py:40
  100.3 3.4 %collective-permute-done.11.two = bf16[672,128]{1,0:T(8,128)(2,1)S(1)} collective-permute-done((bf16[672,128]{1,0:T(8,128)(2,1)S(1)}, bf16[672,128]{1,0:T(8,128)(2,1)S(1)}, u32[]{:S(2)}, u32[]{:S(2)}) %collective-permute-start.11) | collective-permute-done | bytes 172064 | tf_op jit(solution)/shard_map/ppermute | solution.py:40
  103.8 1.8 %collective-permute-done.13.one = bf16[352,128]{1,0:T(8,128)(2,1)S(1)} collective-permute-done((bf16[352,128]{1,0:T(8,128)(2,1)S(1)}, bf16[352,128]{1,0:T(8,128)(2,1)S(1)}, u32[]{:S(2)}, u32[]{:S(2)}) %collective-permute-start.13) | collective-permute-done | bytes 90144 | tf_op jit(solution)/shard_map/ppermute | solution.py:40
  105.5 1.5 %collective-permute-done.14.two = bf16[352,128]{1,0:T(8,128)(2,1)S(1)} collective-permute-done((bf16[352,128]{1,0:T(8,128)(2,1)S(1)}, bf16[352,128]{1,0:T(8,128)(2,1)S(1)}, u32[]{:S(2)}, u32[]{:S(2)}) %collective-permute-start.14) | collective-permute-done | bytes 90144 | tf_op jit(solution)/shard_map/ppermute | solution.py:40
  107.3 4.0 %collective-permute-start.17 = (bf16[512,128]{1,0:T(8,128)(2,1)S(1)}, bf16[512,128]{1,0:T(8,128)(2,1)S(1)}, u32[]{:S(2)}, u32[]{:S(2)}) collective-permute-start(bf16[512,128]{1,0:T(8,128)(2,1)S(1)} %get-tuple-element.76), channel_id=1, source_target_pairs={{8,16},{24,32},{40,48},{56,64},{72,80},{88,96},{104,112},{120,128}... | collective-permute-start | bytes 393224 | tf_op jit(solution)/shard_map/ppermute | solution.py:31
  112.5 5.2 %collective-permute-done.17.second = bf16[512,128]{1,0:T(8,128)(2,1)S(1)} collective-permute-done((bf16[512,128]{1,0:T(8,128)(2,1)S(1)}, bf16[512,128]{1,0:T(8,128)(2,1)S(1)}, u32[]{:S(2)}, u32[]{:S(2)}) %collective-permute-start.17) | collective-permute-done | bytes 131104 | tf_op jit(solution)/shard_map/ppermute | solution.py:31
  (40 shorter events, 8.4 us)
Async XLA Ops:
  6.6 59.7 %collective-permute-start.2 = (bf16[256,3072]{1,0:T(8,128)(2,1)}, bf16[256,3072]{1,0:T(8,128)(2,1)}, u32[]{:S(2)}, u32[]{:S(2)}) collective-permute-start(bf16[256,3072]{1,0:T(8,128)(2,1)} %get-tuple-element.43), channel_id=1, source_target_pairs={{0,8},{16,24},{32,40},{48,56},{64,72},{80,88},{96,104},{112,120},{... | collective-permute-start | bytes 4718600 | tf_op jit(solution)/shard_map/ppermute | solution.py:31
  8.1 58.2 %collective-permute-start.3 = (bf16[256,3072]{1,0:T(8,128)(2,1)}, bf16[256,3072]{1,0:T(8,128)(2,1)}, u32[]{:S(2)}, u32[]{:S(2)}) collective-permute-start(bf16[256,3072]{1,0:T(8,128)(2,1)} %get-tuple-element.50), channel_id=1, source_target_pairs={{8,16},{24,32},{40,48},{56,64},{72,80},{88,96},{104,112},{120,128}... | collective-permute-start | bytes 4718600 | tf_op jit(solution)/shard_map/ppermute | solution.py:31
  11.7 49.4 %collective-permute-start = (bf16[128,3072]{1,0:T(8,128)(2,1)}, bf16[128,3072]{1,0:T(8,128)(2,1)}, u32[]{:S(2)}, u32[]{:S(2)}) collective-permute-start(bf16[128,3072]{1,0:T(8,128)(2,1)} %get-tuple-element.41), channel_id=1, source_target_pairs={{0,8},{16,24},{32,40},{48,56},{64,72},{80,88},{96,104},{112,120},{... | collective-permute-start | bytes 2359304 | tf_op jit(solution)/shard_map/ppermute | solution.py:31
  12.8 53.5 %collective-permute-start.1 = (bf16[128,3072]{1,0:T(8,128)(2,1)}, bf16[128,3072]{1,0:T(8,128)(2,1)}, u32[]{:S(2)}, u32[]{:S(2)}) collective-permute-start(bf16[128,3072]{1,0:T(8,128)(2,1)} %get-tuple-element.49), channel_id=1, source_target_pairs={{8,16},{24,32},{40,48},{56,64},{72,80},{88,96},{104,112},{120,128}... | collective-permute-start | bytes 2359304 | tf_op jit(solution)/shard_map/ppermute | solution.py:31
  19.8 2.6 %copy-start = (bf16[1,6,512,512]{3,2,1,0:T(8,128)(2,1)S(1)}, bf16[1,6,512,512]{3,2,1,0:T(8,128)(2,1)}, u32[]{:S(2)}) copy-start(bf16[1,6,512,512]{3,2,1,0:T(8,128)(2,1)} %param.3) | copy-start | bytes 9437188
  19.8 2.6 %copy-start.2 = (s32[1,2]{1,0:T(1,128)S(1)}, s32[1,2]{1,0:T(1,128)}, u32[]{:S(2)}) copy-start(s32[1,2]{1,0:T(1,128)} %flag.9) | copy-start | bytes 28
  19.8 56.8 %collective-permute-start.5 = (bf16[128,1536]{1,0:T(8,128)(2,1)}, bf16[128,1536]{1,0:T(8,128)(2,1)S(1)}, u32[]{:S(2)}, u32[]{:S(2)}) collective-permute-start(bf16[128,1536]{1,0:T(8,128)(2,1)} %get-tuple-element.45), channel_id=1, source_target_pairs={{0,8},{16,24},{32,40},{48,56},{64,72},{80,88},{96,104},{112,120},{... | collective-permute-start | bytes 1179656 | tf_op jit(solution)/shard_map/ppermute | solution.py:31
  22.5 1.2 %copy-start.1 = (bf16[1,2,512,512]{3,2,1,0:T(8,128)(2,1)S(1)}, bf16[1,2,512,512]{3,2,1,0:T(8,128)(2,1)}, u32[]{:S(2)}) copy-start(bf16[1,2,512,512]{3,2,1,0:T(8,128)(2,1)} %param.4) | copy-start | bytes 3145732
  23.7 37.4 %copy-start.5 = (bf16[128,1536]{1,0:T(8,128)(2,1)S(1)}, bf16[128,1536]{1,0:T(8,128)(2,1)}, u32[]{:S(2)}) copy-start(bf16[128,1536]{1,0:T(8,128)(2,1)} %get-tuple-element.56) | copy-start | bytes 1179652
  61.1 11.4 %copy-start.4 = (bf16[128,1536]{1,0:T(8,128)(2,1)S(1)}, bf16[128,1536]{1,0:T(8,128)(2,1)}, u32[]{:S(2)}) copy-start(bf16[128,1536]{1,0:T(8,128)(2,1)} %get-tuple-element.47) | copy-start | bytes 1179652
  61.1 11.5 %copy-start.3 = (bf16[128,1536]{1,0:T(8,128)(2,1)S(1)}, bf16[128,1536]{1,0:T(8,128)(2,1)}, u32[]{:S(2)}) copy-start(bf16[128,1536]{1,0:T(8,128)(2,1)} %get-tuple-element.61) | copy-start | bytes 1179652
  61.1 15.6 %collective-permute-start.6 = (bf16[128,1536]{1,0:T(8,128)(2,1)S(1)}, bf16[128,1536]{1,0:T(8,128)(2,1)S(1)}, u32[]{:S(2)}, u32[]{:S(2)}) collective-permute-start(bf16[128,1536]{1,0:T(8,128)(2,1)S(1)} %copy-done.5), channel_id=1, source_target_pairs={{8,16},{24,32},{40,48},{56,64},{72,80},{88,96},{104,112},{120,128}... | collective-permute-start | bytes 1179656 | tf_op jit(solution)/shard_map/ppermute | solution.py:31
  72.4 18.5 %collective-permute-start.4 = (bf16[4,672,128]{2,1,0:T(8,128)(2,1)S(1)}, bf16[4,672,128]{2,1,0:T(8,128)(2,1)S(1)}, u32[]{:S(2)}, u32[]{:S(2)}) collective-permute-start(bf16[4,672,128]{2,1,0:T(8,128)(2,1)S(1)} %get-tuple-element.52), channel_id=1, source_target_pairs={{0,1},{1,0},{2,3},{3,2},{4,5},{5,4},{6,7},{7,6},{8,9},{9,8},{10,11... | collective-permute-start | bytes 2064392 | tf_op jit(solution)/shard_map/ppermute | solution.py:35
  72.5 11.5 %collective-permute-start.7 = (bf16[128,1536]{1,0:T(8,128)(2,1)S(1)}, bf16[128,1536]{1,0:T(8,128)(2,1)S(1)}, u32[]{:S(2)}, u32[]{:S(2)}) collective-permute-start(bf16[128,1536]{1,0:T(8,128)(2,1)S(1)} %copy-done.4), channel_id=1, source_target_pairs={{0,8},{16,24},{32,40},{48,56},{64,72},{80,88},{96,104},{112,120},{... | collective-permute-start | bytes 1179656 | tf_op jit(solution)/shard_map/ppermute | solution.py:31
  72.6 16.6 %collective-permute-start.8 = (bf16[128,1536]{1,0:T(8,128)(2,1)S(1)}, bf16[128,1536]{1,0:T(8,128)(2,1)S(1)}, u32[]{:S(2)}, u32[]{:S(2)}) collective-permute-start(bf16[128,1536]{1,0:T(8,128)(2,1)S(1)} %copy-done.3), channel_id=1, source_target_pairs={{8,16},{24,32},{40,48},{56,64},{72,80},{88,96},{104,112},{120,128}... | collective-permute-start | bytes 1179656 | tf_op jit(solution)/shard_map/ppermute | solution.py:31
  90.7 4.7 %collective-permute-start.9 = (bf16[4,352,128]{2,1,0:T(8,128)(2,1)S(1)}, bf16[4,352,128]{2,1,0:T(8,128)(2,1)S(1)}, u32[]{:S(2)}, u32[]{:S(2)}) collective-permute-start(bf16[4,352,128]{2,1,0:T(8,128)(2,1)S(1)} %get-tuple-element.63), channel_id=1, source_target_pairs={{0,1},{1,0},{2,3},{3,2},{4,5},{5,4},{6,7},{7,6},{8,9},{9,8},{10,11... | collective-permute-start | bytes 1081352 | tf_op jit(solution)/shard_map/ppermute | solution.py:35
  91.0 8.9 %collective-permute-start.10 = (bf16[672,128]{1,0:T(8,128)(2,1)S(1)}, bf16[672,128]{1,0:T(8,128)(2,1)S(1)}, u32[]{:S(2)}, u32[]{:S(2)}) collective-permute-start(bf16[672,128]{1,0:T(8,128)(2,1)S(1)} %get-tuple-element.68), channel_id=1, source_target_pairs={{0,4},{1,5},{2,6},{3,7},{4,0},{5,1},{6,2},{7,3},{8,12},{9,13},{10,... | collective-permute-start | bytes 516104 | tf_op jit(solution)/shard_map/ppermute | solution.py:40
  93.4 10.3 %collective-permute-start.11 = (bf16[672,128]{1,0:T(8,128)(2,1)S(1)}, bf16[672,128]{1,0:T(8,128)(2,1)S(1)}, u32[]{:S(2)}, u32[]{:S(2)}) collective-permute-start(bf16[672,128]{1,0:T(8,128)(2,1)S(1)} %get-tuple-element.69), channel_id=1, source_target_pairs={{0,2},{1,3},{2,4},{3,5},{4,6},{5,7},{6,0},{7,1},{8,10},{9,11},{10,... | collective-permute-start | bytes 516104 | tf_op jit(solution)/shard_map/ppermute | solution.py:40
  93.4 10.3 %collective-permute-start.12 = (bf16[672,128]{1,0:T(8,128)(2,1)S(1)}, bf16[672,128]{1,0:T(8,128)(2,1)S(1)}, u32[]{:S(2)}, u32[]{:S(2)}) collective-permute-start(bf16[672,128]{1,0:T(8,128)(2,1)S(1)} %get-tuple-element.70), channel_id=1, source_target_pairs={{0,6},{1,7},{2,0},{3,1},{4,2},{5,3},{6,4},{7,5},{8,14},{9,15},{10,... | collective-permute-start | bytes 516104 | tf_op jit(solution)/shard_map/ppermute | solution.py:40
  95.5 10.0 %collective-permute-start.13 = (bf16[352,128]{1,0:T(8,128)(2,1)S(1)}, bf16[352,128]{1,0:T(8,128)(2,1)S(1)}, u32[]{:S(2)}, u32[]{:S(2)}) collective-permute-start(bf16[352,128]{1,0:T(8,128)(2,1)S(1)} %get-tuple-element.65), channel_id=1, source_target_pairs={{0,4},{1,5},{2,6},{3,7},{4,0},{5,1},{6,2},{7,3},{8,12},{9,13},{10,... | collective-permute-start | bytes 270344 | tf_op jit(solution)/shard_map/ppermute | solution.py:40
  97.0 10.1 %collective-permute-start.14 = (bf16[352,128]{1,0:T(8,128)(2,1)S(1)}, bf16[352,128]{1,0:T(8,128)(2,1)S(1)}, u32[]{:S(2)}, u32[]{:S(2)}) collective-permute-start(bf16[352,128]{1,0:T(8,128)(2,1)S(1)} %get-tuple-element.64), channel_id=1, source_target_pairs={{0,2},{1,3},{2,4},{3,5},{4,6},{5,7},{6,0},{7,1},{8,10},{9,11},{10,... | collective-permute-start | bytes 270344 | tf_op jit(solution)/shard_map/ppermute | solution.py:40
  99.9 7.2 %collective-permute-start.15 = (bf16[352,128]{1,0:T(8,128)(2,1)S(1)}, bf16[352,128]{1,0:T(8,128)(2,1)S(1)}, u32[]{:S(2)}, u32[]{:S(2)}) collective-permute-start(bf16[352,128]{1,0:T(8,128)(2,1)S(1)} %get-tuple-element.66), channel_id=1, source_target_pairs={{0,6},{1,7},{2,0},{3,1},{4,2},{5,3},{6,4},{7,5},{8,14},{9,15},{10,... | collective-permute-start | bytes 270344 | tf_op jit(solution)/shard_map/ppermute | solution.py:40
  107.1 5.4 %collective-permute-start.16 = (bf16[512,128]{1,0:T(8,128)(2,1)S(1)}, bf16[512,128]{1,0:T(8,128)(2,1)S(1)}, u32[]{:S(2)}, u32[]{:S(2)}) collective-permute-start(bf16[512,128]{1,0:T(8,128)(2,1)S(1)} %get-tuple-element.75), channel_id=1, source_target_pairs={{0,8},{16,24},{32,40},{48,56},{64,72},{80,88},{96,104},{112,120},{... | collective-permute-start | bytes 393224 | tf_op jit(solution)/shard_map/ppermute | solution.py:31
  107.3 10.5 %collective-permute-start.17 = (bf16[512,128]{1,0:T(8,128)(2,1)S(1)}, bf16[512,128]{1,0:T(8,128)(2,1)S(1)}, u32[]{:S(2)}, u32[]{:S(2)}) collective-permute-start(bf16[512,128]{1,0:T(8,128)(2,1)S(1)} %get-tuple-element.76), channel_id=1, source_target_pairs={{8,16},{24,32},{40,48},{56,64},{72,80},{88,96},{104,112},{120,128}... | collective-permute-start | bytes 393224 | tf_op jit(solution)/shard_map/ppermute | solution.py:31

commit v3 on v2

--- a/solution.py
+++ b/solution.py
@@ -11,7 +11,7 @@
 SMEM = pl.BlockSpec(memory_space=pltpu.SMEM)
 LANES = 128
 ROWS, PARTS, STEP = 64, 8, 3
-CHUNKS = ((0, 16, 0, 6), (32, 32, 0, 6), (16, 16, 0, 3), (16, 16, 3, 3))
+CHUNKS = ((0, 16, 0, 6), (32, 32, 0, 3), (32, 32, 3, 3), (16, 16, 0, 3), (16, 16, 3, 3))
 EARLY, LATE = 384, 128
 EARLY_U1, EARLY_U2, EARLY_ALL = 192, 144, 672
 LATE_U1, LATE_U2, LATE_ALL = 64, 112, 352
@@ -133,20 +133,64 @@
     return jnp.where(even, first, second), jnp.where(even, second, first)
 
 
-def pack_early(near, first, second):
-    width, depth = near.shape
+def products(kernel, inputs, outputs, flops, scratch=()):
+    return pl.pallas_call(
+        kernel,
+        in_specs=[VMEM] * len(inputs),
+        out_specs=[VMEM] * len(outputs),
+        out_shape=[jax.ShapeDtypeStruct(shape, dtype) for shape, dtype in outputs],
+        scratch_shapes=[pltpu.VMEM(shape, F32) for shape in scratch],
+        compiler_params=params(),
+        cost_estimate=cost(flops, sum(2 * value.size for value in inputs)),
+    )(*inputs)
+
+
+def begin(near, first, second):
+    shape = first.shape
+
+    def kernel(near, first, second, ahead, behind, upper, corner):
+        ahead[...], behind[...] = pick(first, second)
+        upper[...] = contract(near[...], ahead[...])
+        corner[...] = contract(behind[...], ahead[...])
+
+    outputs = [(shape, BF16), (shape, BF16), ((near.shape[0], shape[0]), F32), ((shape[0], shape[0]), F32)]
+    return products(kernel, (near, first, second), outputs, 2 * near.size * shape[0])
+
+
+def advance(near, ahead0, behind0, first, second):
+    height, depth = first.shape
+    columns = pl.ds(0, depth)
+
+    def kernel(near, ahead0, behind0, first, second, ahead, behind, upper, right, below, corner):
+        ahead[...], behind[...] = pick(first, second)
+        upper[...] = contract(near[:, columns], ahead[...])
+        right[...] = contract(behind0[:, columns], ahead[...])
+        below[...] = contract(behind[...], ahead0[:, columns])
+        corner[...] = contract(behind[...], ahead[...])
+
+    low = ahead0.shape[0]
+    outputs = [((height, depth), BF16)] * 2
+    outputs += [(shape, F32) for shape in ((near.shape[0], height), (low, height), (height, low), (height, height))]
+    return products(kernel, (near, ahead0, behind0, first, second), outputs, 2 * near.size * height)
+
+
+def pack_early(near, start, half, first, second):
+    width = near.shape[0]
     places = PARTS // 2
-
-    def kernel(near, first0, second0, first1, second1, kept, sent, ahead, behind, upper, lower, upper_far, lower_far):
-        low, high = pl.ds(0, 128), pl.ds(128, 256)
-        ahead[low, :], behind[low, :] = pick(first0, second0)
-        ahead[high, :], behind[high, :] = pick(first1, second1)
-        value = contract(near[...], ahead[...])
-        upper[...] = value
-        lower[...] = value.T
-        value = contract(behind[...], ahead[...])
-        upper_far[...] = value
-        lower_far[...] = value.T
+    height, depth = first.shape
+    columns = pl.ds(near.shape[1] - depth, depth)
+    low, high = pl.ds(0, EARLY - height), pl.ds(EARLY - height, height)
+
+    def kernel(near, ahead0, behind0, upper0, corner0, upper1, right, below, corner, first, second, kept, sent, ahead, behind, upper, lower, upper_far, lower_far):
+        ahead[...], behind[...] = pick(first, second)
+        upper[:, low] = upper0[...]
+        upper[:, high] = upper1[...] + contract(near[:, columns], ahead[...])
+        lower[...] = upper[...].T
+        upper_far[low, low] = corner0[...]
+        upper_far[low, high] = right[...] + contract(behind0[:, columns], ahead[...])
+        upper_far[high, low] = below[...] + contract(behind[...], ahead0[:, columns])
+        upper_far[high, high] = corner[...] + contract(behind[...], ahead[...])
+        lower_far[...] = upper_far[...].T
         mine = spot()[0]
         for y in range(places):
             for out, core in ((sent, 1 - mine), (kept, mine)):
@@ -161,66 +205,49 @@
                     at = put(out, y, at, early_rows(lower_far, part, lanes(t)))
 
     shape = (places, EARLY_ALL, LANES)
-    return pl.pallas_call(
-        kernel,
-        in_specs=[VMEM] * 5,
-        out_specs=[VMEM] * 4,
-        out_shape=[
-            jax.ShapeDtypeStruct(shape, F32),
-            jax.ShapeDtypeStruct(shape, BF16),
-            jax.ShapeDtypeStruct((EARLY, depth), BF16),
-            jax.ShapeDtypeStruct((EARLY, depth), BF16),
-        ],
-        scratch_shapes=[
-            pltpu.VMEM((width, EARLY), F32),
-            pltpu.VMEM((EARLY, width), F32),
-            pltpu.VMEM((EARLY, EARLY), F32),
-            pltpu.VMEM((EARLY, EARLY), F32),
-        ],
-        compiler_params=params(),
-        cost_estimate=cost(2 * near.size * EARLY * 2, near.size * 4),
-    )(near, first[0], second[0], first[1], second[1])
-
-
-def pack_middle(near, ahead, behind, first, second):
+    outputs = [(shape, F32), (shape, BF16), ((height, depth), BF16), ((height, depth), BF16)]
+    scratch = ((width, EARLY), (EARLY, width), (EARLY, EARLY), (EARLY, EARLY))
+    return products(kernel, (near, *start, *half[2:], first, second), outputs, near.size * EARLY, scratch)
+
+
+def pack_middle(near, ahead0, behind0, ahead1, behind1, first, second):
     width = near.shape[0]
-    depth = first.shape[1]
-
-    def kernel(near, ahead, behind, first, second, upper, tall, tall_t, corner):
+    height, depth = first.shape
+    columns = pl.ds(0, depth)
+    low, high = pl.ds(0, ahead0.shape[0]), pl.ds(ahead0.shape[0], ahead1.shape[0])
+
+    def kernel(near, ahead0, behind0, ahead1, behind1, first, second, upper, tall, tall_t, corner):
         last, prior = pick(first, second)
-        columns = pl.ds(0, depth)
         upper[...] = contract(near[:, columns], last)
-        tall[...] = contract(behind[:, columns], last)
-        tall_t[...] = contract(ahead[:, columns], prior)
+        tall[low, :] = contract(behind0[:, columns], last)
+        tall[high, :] = contract(behind1[...], last)
+        tall_t[low, :] = contract(ahead0[:, columns], prior)
+        tall_t[high, :] = contract(ahead1[...], prior)
         corner[...] = contract(prior, last)
 
-    return pl.pallas_call(
-        kernel,
-        in_specs=[VMEM] * 5,
-        out_specs=[VMEM] * 4,
-        out_shape=[jax.ShapeDtypeStruct((height, LATE), F32) for height in (width, EARLY, EARLY, LATE)],
-        compiler_params=params(),
-        cost_estimate=cost(near.size * LATE * 3, near.size * 6),
-    )(near, ahead, behind, first, second)
-
-
-def pack_late(near, ahead, behind, middle, first, second):
+    outputs = [((rows, height), F32) for rows in (width, EARLY, EARLY, height)]
+    inputs = (near, ahead0, behind0, ahead1, behind1, first, second)
+    return products(kernel, inputs, outputs, 3 * near.size * height)
+
+
+def pack_late(near, ahead0, behind0, ahead1, behind1, middle, first, second):
     width = near.shape[0]
     places = PARTS // 2
     depth = first.shape[1]
-
-    def kernel(near, ahead, behind, upper0, tall0, tall_t0, corner0, first, second, kept, sent, upper, lower, tall, wide, tall_t, wide_t):
+    columns = pl.ds(near.shape[1] - depth, depth)
+    low, high = pl.ds(0, ahead0.shape[0]), pl.ds(ahead0.shape[0], ahead1.shape[0])
+
+    def kernel(near, ahead0, behind0, ahead1, behind1, upper0, tall0, tall_t0, corner0, first, second, kept, sent, upper, lower, tall, wide, tall_t, wide_t):
         last, prior = pick(first, second)
-        columns = pl.ds(near.shape[1] - depth, depth)
         value = upper0[...] + contract(near[:, columns], last)
         upper[...] = value
         lower[...] = value.T
-        value = tall0[...] + contract(behind[:, columns], last)
-        tall[...] = value
-        wide_t[:, pl.ds(0, EARLY)] = value.T
-        value = tall_t0[...] + contract(ahead[:, columns], prior)
-        tall_t[...] = value
-        wide[:, pl.ds(0, EARLY)] = value.T
+        tall[low, :] = tall0[low, :] + contract(behind0[:, columns], last)
+        tall[high, :] = tall0[high, :] + contract(behind1[...], last)
+        wide_t[:, pl.ds(0, EARLY)] = tall[...].T
+        tall_t[low, :] = tall_t0[low, :] + contract(ahead0[:, columns], prior)
+        tall_t[high, :] = tall_t0[high, :] + contract(ahead1[...], prior)
+        wide[:, pl.ds(0, EARLY)] = tall_t[...].T
         value = corner0[...] + contract(prior, last)
         wide[:, pl.ds(EARLY, LATE)] = value
         wide_t[:, pl.ds(EARLY, LATE)] = value.T
@@ -237,22 +264,9 @@
                 at = put(out, y, at, [late_rows(wide_t, part, lanes(t)) for t in range(4)])
 
     shape = (places, LATE_ALL, LANES)
-    return pl.pallas_call(
-        kernel,
-        in_specs=[VMEM] * 9,
-        out_specs=[VMEM] * 2,
-        out_shape=[jax.ShapeDtypeStruct(shape, F32), jax.ShapeDtypeStruct(shape, BF16)],
-        scratch_shapes=[
-            pltpu.VMEM((width, LATE), F32),
-            pltpu.VMEM((LATE, width), F32),
-            pltpu.VMEM((EARLY, LATE), F32),
-            pltpu.VMEM((LATE, width), F32),
-            pltpu.VMEM((EARLY, LATE), F32),
-            pltpu.VMEM((LATE, width), F32),
-        ],
-        compiler_params=params(),
-        cost_estimate=cost(near.size * LATE * 3, near.size * 6),
-    )(near, ahead, behind, *middle, first, second)
+    inputs = (near, ahead0, behind0, ahead1, behind1, *middle, first, second)
+    scratch = ((width, LATE), (LATE, width), (EARLY, LATE), (LATE, width), (EARLY, LATE), (LATE, width))
+    return products(kernel, inputs, [(shape, F32), (shape, BF16)], 3 * near.size * LATE, scratch)
 
 
 def join_core(kept, received):
@@ -429,11 +443,13 @@
         second.append(swap_atoms(two, 1))
         first.append(swap_atoms(one, 0))
     near = transform(source, blocks, screen)
-    kept, sent, ahead, behind = pack_early(near, first[:2], second[:2])
+    start = begin(near, first[0], second[0])
+    half = advance(near, *start[:2], first[1], second[1])
+    kept, sent, ahead, behind = pack_early(near, start, half, first[2], second[2])
     total, *pieces = join_core(kept, swap_core(sent))
     received = send_places(pieces)
-    middle = pack_middle(near, ahead, behind, first[2], second[2])
-    kept, sent = pack_late(near, ahead, behind, middle, first[3], second[3])
+    middle = pack_middle(near, *start[:2], *half[:2], first[3], second[3])
+    kept, sent = pack_late(near, *start[:2], ahead, behind, middle, first[4], second[4])
     late_total, *late_pieces = join_core(kept, swap_core(sent))
     late_received = send_places(late_pieces)
     upper, rest = join_early(after(total, *late_pieces), received)

time: 119 us -> 114 us (0.958)
  waiting for transfers between devices: 59.4 us -> 44.8 us
  Pallas kernels: 25.4 us -> 29.9 us
  starting transfers between devices: 32.4 us -> 36.5 us
    ppermute x10 -> x12, waiting for transfers between devices: 52.4 us -> 37.8 us  [swap_atoms(): return lax.ppermute(value, 'atoms', pairs + [(j, i) for i, j in pairs])]
    ppermute x10 -> x12, starting transfers between devices: 23.3 us -> 27.4 us  [swap_atoms(): return lax.ppermute(value, 'atoms', pairs + [(j, i) for i, j in pairs])]
    pallas_call x4 -> x5, Pallas kernels: 11.7 us -> 14 us  [split(): pl.pallas_call(kernel, grid=(count // STEP,), in_specs=[SMEM, pl.BlockSpe...]
    pallas_call x3 -> x5, Pallas kernels: 8.81 us -> 11 us  [products(): pl.pallas_call(kernel, in_specs=[VMEM] * len(inputs), out_specs=[VMEM] *...]
  transfers between devices with their start and end apart: 18 -> 20, of which waited for: 10 -> 12; matrix products, arithmetic and copies ran while one was open for 0% -> 0% of each run, Pallas kernels for 15% -> 23%
where the time goes in v3:
time: 114 us
  waiting for transfers between devices  44.8 us (39%)
  starting transfers between devices  36.5 us (32%)
  Pallas kernels  29.9 us (26%)
  local copies, waits for them, and re-layouts  2.19 us (2%)
    ppermute x12, waiting for transfers between devices, swap_atoms(): return lax.ppermute(value, 'atoms', pairs + [(j, i) for i, j in pairs])  37.8 us
    ppermute x12, starting transfers between devices, swap_atoms(): return lax.ppermute(value, 'atoms', pairs + [(j, i) for i, j in pairs])  27.4 us
    pallas_call x5, Pallas kernels, split(): pl.pallas_call(kernel, grid=(count // STEP,), in_specs=[SMEM, pl.BlockSpe...  14 us
    pallas_call x5, Pallas kernels, products(): pl.pallas_call(kernel, in_specs=[VMEM] * len(inputs), out_specs=[VMEM] *...  11 us
    ppermute x6, starting transfers between devices, shift_y(): lax.ppermute(value, 'aux', [(i, (i + 2 * steps) % count) for i in range(c...  8.91 us
    ppermute x6, waiting for transfers between devices, shift_y(): lax.ppermute(value, 'aux', [(i, (i + 2 * steps) % count) for i in range(c...  6.99 us
    pallas_call x1, Pallas kernels, transform(): pl.pallas_call(kernel, grid=(count // STEP,), in_specs=[SMEM, pl.BlockSpe...  2.74 us
  transfers between devices with their start and end apart: 20, of which 12 were waited for; matrix products, arithmetic and copies ran while one was open for 0% of the time, Pallas kernels for 23%

profile of v3, /device:TPU:136, one launch (start us, length us, event | category | flops | bytes accessed | tf_op | source)
XLA Modules:
  0.0 113.7 jit_solution(8232172228594782977)
XLA Ops:
  0.0 2.9 %shard_map.37 = (bf16[128,3072]{1,0:T(8,128)(2,1)}, bf16[128,3072]{1,0:T(8,128)(2,1)}) custom-call(s32[1,2]{1,0:T(1,128)} %flag.11, bf16[6,8,64,512]{3,2,1,0:T(8,128)(2,1)} %bitcast.2, bf16[2,512,512]{2,1,0:T(8,128)(2,1)} %bitcast.8), custom_call_target="tpu_custom_call" | custom-call | flops 402653184 | bytes 2359296 | tf_op jit(solution)/shard_map/pallas_call | solution.py:66
  4.4 3.5 %collective-permute-start.1 = (bf16[128,3072]{1,0:T(8,128)(2,1)}, bf16[128,3072]{1,0:T(8,128)(2,1)}, u32[]{:S(2)}, u32[]{:S(2)}) collective-permute-start(bf16[128,3072]{1,0:T(8,128)(2,1)} %get-tuple-element.64), channel_id=1, source_target_pairs={{8,16},{24,32},{40,48},{56,64},{72,80},{88,96},{104,112},{120,128}... | collective-permute-start | bytes 2359304 | tf_op jit(solution)/shard_map/ppermute | solution.py:31
  7.9 3.0 %shard_map.38 = (bf16[256,1536]{1,0:T(8,128)(2,1)}, bf16[256,1536]{1,0:T(8,128)(2,1)}) custom-call(s32[1,2]{1,0:T(1,128)} %flag.11, bf16[6,8,64,512]{3,2,1,0:T(8,128)(2,1)} %bitcast.3, bf16[2,512,512]{2,1,0:T(8,128)(2,1)} %bitcast.9), custom_call_target="tpu_custom_call" | custom-call | flops 402653184 | bytes 2359296 | tf_op jit(solution)/shard_map/pallas_call | solution.py:66
  12.0 4.6 %collective-permute-start.3 = (bf16[256,1536]{1,0:T(8,128)(2,1)}, bf16[256,1536]{1,0:T(8,128)(2,1)}, u32[]{:S(2)}, u32[]{:S(2)}) collective-permute-start(bf16[256,1536]{1,0:T(8,128)(2,1)} %get-tuple-element.69), channel_id=1, source_target_pairs={{8,16},{24,32},{40,48},{56,64},{72,80},{88,96},{104,112},{120,128}... | collective-permute-start | bytes 2359304 | tf_op jit(solution)/shard_map/ppermute | solution.py:31
  16.6 3.0 %shard_map.39 = (bf16[256,1536]{1,0:T(8,128)(2,1)}, bf16[256,1536]{1,0:T(8,128)(2,1)}) custom-call(s32[1,2]{1,0:T(1,128)} %flag.11, bf16[6,8,64,512]{3,2,1,0:T(8,128)(2,1)} %bitcast.4, bf16[2,512,512]{2,1,0:T(8,128)(2,1)} %bitcast.10), custom_call_target="tpu_custom_call" | custom-call | flops 402653184 | bytes 2359296 | tf_op jit(solution)/shard_map/pallas_call | solution.py:66
  19.6 3.9 %collective-permute-done.first = bf16[128,3072]{1,0:T(8,128)(2,1)S(1)} collective-permute-done((bf16[128,3072]{1,0:T(8,128)(2,1)}, bf16[128,3072]{1,0:T(8,128)(2,1)S(1)}, u32[]{:S(2)}, u32[]{:S(2)}) %collective-permute-start) | collective-permute-done | bytes 786464 | tf_op jit(solution)/shard_map/ppermute | solution.py:31
  24.5 4.2 %collective-permute-start.5 = (bf16[256,1536]{1,0:T(8,128)(2,1)}, bf16[256,1536]{1,0:T(8,128)(2,1)}, u32[]{:S(2)}, u32[]{:S(2)}) collective-permute-start(bf16[256,1536]{1,0:T(8,128)(2,1)} %get-tuple-element.74), channel_id=1, source_target_pairs={{8,16},{24,32},{40,48},{56,64},{72,80},{88,96},{104,112},{120,128}... | collective-permute-start | bytes 2359304 | tf_op jit(solution)/shard_map/ppermute | solution.py:31
  28.7 2.4 %shard_map.40 = (bf16[128,1536]{1,0:T(8,128)(2,1)}, bf16[128,1536]{1,0:T(8,128)(2,1)}) custom-call(s32[1,2]{1,0:T(1,128)} %flag.11, bf16[6,8,64,512]{3,2,1,0:T(8,128)(2,1)} %bitcast.5, bf16[2,512,512]{2,1,0:T(8,128)(2,1)} %bitcast.11), custom_call_target="tpu_custom_call" | custom-call | flops 201326592 | bytes 1179648 | tf_op jit(solution)/shard_map/pallas_call | solution.py:66
  31.1 2.6 %shard_map.41 = (bf16[128,1536]{1,0:T(8,128)(2,1)}, bf16[128,1536]{1,0:T(8,128)(2,1)}) custom-call(s32[1,2]{1,0:T(1,128)} %flag.11, bf16[6,8,64,512]{3,2,1,0:T(8,128)(2,1)} %bitcast.6, bf16[2,512,512]{2,1,0:T(8,128)(2,1)} %bitcast.12), custom_call_target="tpu_custom_call" | custom-call | flops 201326592 | bytes 1179648 | tf_op jit(solution)/shard_map/pallas_call | solution.py:66
  34.9 2.7 %shard_map.42.near = bf16[512,3072]{1,0:T(8,128)(2,1)S(1)} custom-call(s32[1,2]{1,0:T(1,128)S(1)} %copy-done.4, bf16[6,8,64,512]{3,2,1,0:T(8,128)(2,1)S(1)} %bitcast.7, bf16[2,512,512]{2,1,0:T(8,128)(2,1)S(1)} %bitcast.13), custom_call_target="tpu_custom_call" | custom-call | flops 1610612736 | bytes 6291456 | tf_op jit(solution)/shard_map/pallas_call | solution.py:90
  38.5 2.3 %shard_map.43 = (bf16[128,3072]{1,0:T(8,128)(2,1)S(1)}, bf16[128,3072]{1,0:T(8,128)(2,1)S(1)}, f32[512,128]{1,0:T(8,128)S(1)}, f32[128,128]{1,0:T(8,128)S(1)}) custom-call(bf16[512,3072]{1,0:T(8,128)(2,1)S(1)} %shard_map.42.near, bf16[128,3072]{1,0:T(8,128)(2,1)S(1)} %copy-done.3, bf16[128,3072]{1,0:T(8,128)(2,1)} %collective-permute-done.1.second), custom_call_target="tpu_custom_call" | custom-call | flops 402653184 | bytes 4718592 | tf_op jit(solution)/shard_map/pallas_call | solution.py:137
  40.8 4.3 %collective-permute-start.8 = (bf16[128,1536]{1,0:T(8,128)(2,1)S(1)}, bf16[128,1536]{1,0:T(8,128)(2,1)S(1)}, u32[]{:S(2)}, u32[]{:S(2)}) collective-permute-start(bf16[128,1536]{1,0:T(8,128)(2,1)S(1)} %copy-done.7), channel_id=1, source_target_pairs={{8,16},{24,32},{40,48},{56,64},{72,80},{88,96},{104,112},{120,128}... | collective-permute-start | bytes 1179656 | tf_op jit(solution)/shard_map/ppermute | solution.py:31
  47.2 2.6 %shard_map.44 = (bf16[256,1536]{1,0:T(8,128)(2,1)S(1)}, bf16[256,1536]{1,0:T(8,128)(2,1)S(1)}, f32[512,256]{1,0:T(8,128)S(1)}, f32[128,256]{1,0:T(8,128)S(1)}, f...) custom-call(bf16[512,3072]{1,0:T(8,128)(2,1)S(1)} %shard_map.42.near, bf16[128,3072]{1,0:T(8,128)(2,1)S(1)} %get-tuple-element.65.ahead0, ...), custom_call_target="tpu_custom_call" | custom-call | flops 805306368 | bytes 6291456 | tf_op jit(solution)/shard_map/pallas_call | solution.py:137
  49.7 7.6 %collective-permute-done.4.first = bf16[256,1536]{1,0:T(8,128)(2,1)} collective-permute-done((bf16[256,1536]{1,0:T(8,128)(2,1)}, bf16[256,1536]{1,0:T(8,128)(2,1)}, u32[]{:S(2)}, u32[]{:S(2)}) %collective-permute-start.4) | collective-permute-done | bytes 786464 | tf_op jit(solution)/shard_map/ppermute | solution.py:31
  57.3 6.7 %collective-permute-done.5.second = bf16[256,1536]{1,0:T(8,128)(2,1)} collective-permute-done((bf16[256,1536]{1,0:T(8,128)(2,1)}, bf16[256,1536]{1,0:T(8,128)(2,1)}, u32[]{:S(2)}, u32[]{:S(2)}) %collective-permute-start.5) | collective-permute-done | bytes 786464 | tf_op jit(solution)/shard_map/ppermute | solution.py:31
  64.0 3.2 %shard_map.45 = (f32[4,672,128]{2,1,0:T(8,128)S(1)}, bf16[4,672,128]{2,1,0:T(8,128)(2,1)S(1)}, bf16[256,1536]{1,0:T(8,128)(2,1)S(1)}, bf16[256,1536]{1,0:T(8,128)(2,1)S(1)}) custom-call(bf16[512,3072]{1,0:T(8,128)(2,1)S(1)} %shard_map.42.near, bf16[128,3072]{1,0:T(8,128)(2,1)S(1)} %get-tuple-element.65.ahead0, ...), custom_call_target="tpu_custom_call" | custom-call | flops 603979776 | bytes 6979584 | tf_op jit(solution)/shard_map/pallas_call | solution.py:137
  67.4 3.7 %collective-permute-start.10 = (bf16[128,1536]{1,0:T(8,128)(2,1)S(1)}, bf16[128,1536]{1,0:T(8,128)(2,1)S(1)}, u32[]{:S(2)}, u32[]{:S(2)}) collective-permute-start(bf16[128,1536]{1,0:T(8,128)(2,1)S(1)} %copy-done.5), channel_id=1, source_target_pairs={{8,16},{24,32},{40,48},{56,64},{72,80},{88,96},{104,112},{120,128}... | collective-permute-start | bytes 1179656 | tf_op jit(solution)/shard_map/ppermute | solution.py:31
  72.5 6.3 %collective-permute-done.9.first = bf16[128,1536]{1,0:T(8,128)(2,1)S(1)} collective-permute-done((bf16[128,1536]{1,0:T(8,128)(2,1)S(1)}, bf16[128,1536]{1,0:T(8,128)(2,1)S(1)}, u32[]{:S(2)}, u32[]{:S(2)}) %collective-permute-start.9) | collective-permute-done | bytes 393248 | tf_op jit(solution)/shard_map/ppermute | solution.py:31
  78.8 5.2 %collective-permute-done.10.second = bf16[128,1536]{1,0:T(8,128)(2,1)S(1)} collective-permute-done((bf16[128,1536]{1,0:T(8,128)(2,1)S(1)}, bf16[128,1536]{1,0:T(8,128)(2,1)S(1)}, u32[]{:S(2)}, u32[]{:S(2)}) %collective-permute-start.10) | collective-permute-done | bytes 393248 | tf_op jit(solution)/shard_map/ppermute | solution.py:31
  85.9 2.4 %collective-permute-start.12 = (bf16[672,128]{1,0:T(8,128)(2,1)S(1)}, bf16[672,128]{1,0:T(8,128)(2,1)S(1)}, u32[]{:S(2)}, u32[]{:S(2)}) collective-permute-start(bf16[672,128]{1,0:T(8,128)(2,1)S(1)} %get-tuple-element.94), channel_id=1, source_target_pairs={{0,4},{1,5},{2,6},{3,7},{4,0},{5,1},{6,2},{7,3},{8,12},{9,13},{10,... | collective-permute-start | bytes 516104 | tf_op jit(solution)/shard_map/ppermute | solution.py:40
  91.9 2.6 %collective-permute-start.16 = (bf16[352,128]{1,0:T(8,128)(2,1)S(1)}, bf16[352,128]{1,0:T(8,128)(2,1)S(1)}, u32[]{:S(2)}, u32[]{:S(2)}) collective-permute-start(bf16[352,128]{1,0:T(8,128)(2,1)S(1)} %get-tuple-element.90), channel_id=1, source_target_pairs={{0,2},{1,3},{2,4},{3,5},{4,6},{5,7},{6,0},{7,1},{8,10},{9,11},{10,... | collective-permute-start | bytes 270344 | tf_op jit(solution)/shard_map/ppermute | solution.py:40
  95.2 3.4 %collective-permute-done.13.two = bf16[672,128]{1,0:T(8,128)(2,1)S(1)} collective-permute-done((bf16[672,128]{1,0:T(8,128)(2,1)S(1)}, bf16[672,128]{1,0:T(8,128)(2,1)S(1)}, u32[]{:S(2)}, u32[]{:S(2)}) %collective-permute-start.13) | collective-permute-done | bytes 172064 | tf_op jit(solution)/shard_map/ppermute | solution.py:40
  102.1 3.6 %collective-permute-start.19 = (bf16[512,128]{1,0:T(8,128)(2,1)S(1)}, bf16[512,128]{1,0:T(8,128)(2,1)S(1)}, u32[]{:S(2)}, u32[]{:S(2)}) collective-permute-start(bf16[512,128]{1,0:T(8,128)(2,1)S(1)} %get-tuple-element.102), channel_id=1, source_target_pairs={{8,16},{24,32},{40,48},{56,64},{72,80},{88,96},{104,112},{120,128}... | collective-permute-start | bytes 393224 | tf_op jit(solution)/shard_map/ppermute | solution.py:31
  107.4 5.2 %collective-permute-done.19.second = bf16[512,128]{1,0:T(8,128)(2,1)S(1)} collective-permute-done((bf16[512,128]{1,0:T(8,128)(2,1)S(1)}, bf16[512,128]{1,0:T(8,128)(2,1)S(1)}, u32[]{:S(2)}, u32[]{:S(2)}) %collective-permute-start.19) | collective-permute-done | bytes 131104 | tf_op jit(solution)/shard_map/ppermute | solution.py:31
  (53 shorter events, 21.4 us)
Async XLA Ops:
  2.9 20.6 %collective-permute-start = (bf16[128,3072]{1,0:T(8,128)(2,1)}, bf16[128,3072]{1,0:T(8,128)(2,1)S(1)}, u32[]{:S(2)}, u32[]{:S(2)}) collective-permute-start(bf16[128,3072]{1,0:T(8,128)(2,1)} %get-tuple-element.54), channel_id=1, source_target_pairs={{0,8},{16,24},{32,40},{48,56},{64,72},{80,88},{96,104},{112,120},{... | collective-permute-start | bytes 2359304 | tf_op jit(solution)/shard_map/ppermute | solution.py:31
  4.4 33.3 %collective-permute-start.1 = (bf16[128,3072]{1,0:T(8,128)(2,1)}, bf16[128,3072]{1,0:T(8,128)(2,1)}, u32[]{:S(2)}, u32[]{:S(2)}) collective-permute-start(bf16[128,3072]{1,0:T(8,128)(2,1)} %get-tuple-element.64), channel_id=1, source_target_pairs={{8,16},{24,32},{40,48},{56,64},{72,80},{88,96},{104,112},{120,128}... | collective-permute-start | bytes 2359304 | tf_op jit(solution)/shard_map/ppermute | solution.py:31
  11.0 29.9 %collective-permute-start.2 = (bf16[256,1536]{1,0:T(8,128)(2,1)}, bf16[256,1536]{1,0:T(8,128)(2,1)}, u32[]{:S(2)}, u32[]{:S(2)}) collective-permute-start(bf16[256,1536]{1,0:T(8,128)(2,1)} %get-tuple-element.56), channel_id=1, source_target_pairs={{0,8},{16,24},{32,40},{48,56},{64,72},{80,88},{96,104},{112,120},{... | collective-permute-start | bytes 2359304 | tf_op jit(solution)/shard_map/ppermute | solution.py:31
  12.0 35.2 %collective-permute-start.3 = (bf16[256,1536]{1,0:T(8,128)(2,1)}, bf16[256,1536]{1,0:T(8,128)(2,1)}, u32[]{:S(2)}, u32[]{:S(2)}) collective-permute-start(bf16[256,1536]{1,0:T(8,128)(2,1)} %get-tuple-element.69), channel_id=1, source_target_pairs={{8,16},{24,32},{40,48},{56,64},{72,80},{88,96},{104,112},{120,128}... | collective-permute-start | bytes 2359304 | tf_op jit(solution)/shard_map/ppermute | solution.py:31
  19.6 37.7 %collective-permute-start.4 = (bf16[256,1536]{1,0:T(8,128)(2,1)}, bf16[256,1536]{1,0:T(8,128)(2,1)}, u32[]{:S(2)}, u32[]{:S(2)}) collective-permute-start(bf16[256,1536]{1,0:T(8,128)(2,1)} %get-tuple-element.58), channel_id=1, source_target_pairs={{0,8},{16,24},{32,40},{48,56},{64,72},{80,88},{96,104},{112,120},{... | collective-permute-start | bytes 2359304 | tf_op jit(solution)/shard_map/ppermute | solution.py:31
  24.5 39.6 %collective-permute-start.5 = (bf16[256,1536]{1,0:T(8,128)(2,1)}, bf16[256,1536]{1,0:T(8,128)(2,1)}, u32[]{:S(2)}, u32[]{:S(2)}) collective-permute-start(bf16[256,1536]{1,0:T(8,128)(2,1)} %get-tuple-element.74), channel_id=1, source_target_pairs={{8,16},{24,32},{40,48},{56,64},{72,80},{88,96},{104,112},{120,128}... | collective-permute-start | bytes 2359304 | tf_op jit(solution)/shard_map/ppermute | solution.py:31
  34.9 3.5 %copy-start.3 = (bf16[128,3072]{1,0:T(8,128)(2,1)S(1)}, bf16[128,3072]{1,0:T(8,128)(2,1)}, u32[]{:S(2)}) copy-start(bf16[128,3072]{1,0:T(8,128)(2,1)} %copy-done.2) | copy-start | bytes 2359300
  37.7 3.2 %copy-start.7 = (bf16[128,1536]{1,0:T(8,128)(2,1)S(1)}, bf16[128,1536]{1,0:T(8,128)(2,1)}, u32[]{:S(2)}) copy-start(bf16[128,1536]{1,0:T(8,128)(2,1)} %get-tuple-element.82) | copy-start | bytes 1179652
  37.7 33.4 %collective-permute-start.7 = (bf16[128,1536]{1,0:T(8,128)(2,1)S(1)}, bf16[128,1536]{1,0:T(8,128)(2,1)S(1)}, u32[]{:S(2)}, u32[]{:S(2)}) collective-permute-start(bf16[128,1536]{1,0:T(8,128)(2,1)S(1)} %copy-done.8), channel_id=1, source_target_pairs={{0,8},{16,24},{32,40},{48,56},{64,72},{80,88},{96,104},{112,120},{... | collective-permute-start | bytes 1179656 | tf_op jit(solution)/shard_map/ppermute | solution.py:31
  40.8 30.3 %collective-permute-start.8 = (bf16[128,1536]{1,0:T(8,128)(2,1)S(1)}, bf16[128,1536]{1,0:T(8,128)(2,1)S(1)}, u32[]{:S(2)}, u32[]{:S(2)}) collective-permute-start(bf16[128,1536]{1,0:T(8,128)(2,1)S(1)} %copy-done.7), channel_id=1, source_target_pairs={{8,16},{24,32},{40,48},{56,64},{72,80},{88,96},{104,112},{120,128}... | collective-permute-start | bytes 1179656 | tf_op jit(solution)/shard_map/ppermute | solution.py:31
  64.0 3.3 %copy-start.6 = (bf16[128,1536]{1,0:T(8,128)(2,1)S(1)}, bf16[128,1536]{1,0:T(8,128)(2,1)}, u32[]{:S(2)}) copy-start(bf16[128,1536]{1,0:T(8,128)(2,1)} %get-tuple-element.62) | copy-start | bytes 1179652
  64.0 3.4 %copy-start.5 = (bf16[128,1536]{1,0:T(8,128)(2,1)S(1)}, bf16[128,1536]{1,0:T(8,128)(2,1)}, u32[]{:S(2)}) copy-start(bf16[128,1536]{1,0:T(8,128)(2,1)} %get-tuple-element.87) | copy-start | bytes 1179652
  67.2 18.5 %collective-permute-start.6 = (bf16[4,672,128]{2,1,0:T(8,128)(2,1)S(1)}, bf16[4,672,128]{2,1,0:T(8,128)(2,1)S(1)}, u32[]{:S(2)}, u32[]{:S(2)}) collective-permute-start(bf16[4,672,128]{2,1,0:T(8,128)(2,1)S(1)} %get-tuple-element.76), channel_id=1, source_target_pairs={{0,1},{1,0},{2,3},{3,2},{4,5},{5,4},{6,7},{7,6},{8,9},{9,8},{10,11... | collective-permute-start | bytes 2064392 | tf_op jit(solution)/shard_map/ppermute | solution.py:35
  67.3 11.5 %collective-permute-start.9 = (bf16[128,1536]{1,0:T(8,128)(2,1)S(1)}, bf16[128,1536]{1,0:T(8,128)(2,1)S(1)}, u32[]{:S(2)}, u32[]{:S(2)}) collective-permute-start(bf16[128,1536]{1,0:T(8,128)(2,1)S(1)} %copy-done.6), channel_id=1, source_target_pairs={{0,8},{16,24},{32,40},{48,56},{64,72},{80,88},{96,104},{112,120},{... | collective-permute-start | bytes 1179656 | tf_op jit(solution)/shard_map/ppermute | solution.py:31
  67.4 16.6 %collective-permute-start.10 = (bf16[128,1536]{1,0:T(8,128)(2,1)S(1)}, bf16[128,1536]{1,0:T(8,128)(2,1)S(1)}, u32[]{:S(2)}, u32[]{:S(2)}) collective-permute-start(bf16[128,1536]{1,0:T(8,128)(2,1)S(1)} %copy-done.5), channel_id=1, source_target_pairs={{8,16},{24,32},{40,48},{56,64},{72,80},{88,96},{104,112},{120,128}... | collective-permute-start | bytes 1179656 | tf_op jit(solution)/shard_map/ppermute | solution.py:31
  85.6 4.7 %collective-permute-start.11 = (bf16[4,352,128]{2,1,0:T(8,128)(2,1)S(1)}, bf16[4,352,128]{2,1,0:T(8,128)(2,1)S(1)}, u32[]{:S(2)}, u32[]{:S(2)}) collective-permute-start(bf16[4,352,128]{2,1,0:T(8,128)(2,1)S(1)} %get-tuple-element.89), channel_id=1, source_target_pairs={{0,1},{1,0},{2,3},{3,2},{4,5},{5,4},{6,7},{7,6},{8,9},{9,8},{10,11... | collective-permute-start | bytes 1081352 | tf_op jit(solution)/shard_map/ppermute | solution.py:35
  85.9 8.9 %collective-permute-start.12 = (bf16[672,128]{1,0:T(8,128)(2,1)S(1)}, bf16[672,128]{1,0:T(8,128)(2,1)S(1)}, u32[]{:S(2)}, u32[]{:S(2)}) collective-permute-start(bf16[672,128]{1,0:T(8,128)(2,1)S(1)} %get-tuple-element.94), channel_id=1, source_target_pairs={{0,4},{1,5},{2,6},{3,7},{4,0},{5,1},{6,2},{7,3},{8,12},{9,13},{10,... | collective-permute-start | bytes 516104 | tf_op jit(solution)/shard_map/ppermute | solution.py:40
  88.3 10.3 %collective-permute-start.13 = (bf16[672,128]{1,0:T(8,128)(2,1)S(1)}, bf16[672,128]{1,0:T(8,128)(2,1)S(1)}, u32[]{:S(2)}, u32[]{:S(2)}) collective-permute-start(bf16[672,128]{1,0:T(8,128)(2,1)S(1)} %get-tuple-element.95), channel_id=1, source_target_pairs={{0,2},{1,3},{2,4},{3,5},{4,6},{5,7},{6,0},{7,1},{8,10},{9,11},{10,... | collective-permute-start | bytes 516104 | tf_op jit(solution)/shard_map/ppermute | solution.py:40
  88.3 10.3 %collective-permute-start.14 = (bf16[672,128]{1,0:T(8,128)(2,1)S(1)}, bf16[672,128]{1,0:T(8,128)(2,1)S(1)}, u32[]{:S(2)}, u32[]{:S(2)}) collective-permute-start(bf16[672,128]{1,0:T(8,128)(2,1)S(1)} %get-tuple-element.96), channel_id=1, source_target_pairs={{0,6},{1,7},{2,0},{3,1},{4,2},{5,3},{6,4},{7,5},{8,14},{9,15},{10,... | collective-permute-start | bytes 516104 | tf_op jit(solution)/shard_map/ppermute | solution.py:40
  90.4 10.0 %collective-permute-start.15 = (bf16[352,128]{1,0:T(8,128)(2,1)S(1)}, bf16[352,128]{1,0:T(8,128)(2,1)S(1)}, u32[]{:S(2)}, u32[]{:S(2)}) collective-permute-start(bf16[352,128]{1,0:T(8,128)(2,1)S(1)} %get-tuple-element.91), channel_id=1, source_target_pairs={{0,4},{1,5},{2,6},{3,7},{4,0},{5,1},{6,2},{7,3},{8,12},{9,13},{10,... | collective-permute-start | bytes 270344 | tf_op jit(solution)/shard_map/ppermute | solution.py:40
  91.9 10.1 %collective-permute-start.16 = (bf16[352,128]{1,0:T(8,128)(2,1)S(1)}, bf16[352,128]{1,0:T(8,128)(2,1)S(1)}, u32[]{:S(2)}, u32[]{:S(2)}) collective-permute-start(bf16[352,128]{1,0:T(8,128)(2,1)S(1)} %get-tuple-element.90), channel_id=1, source_target_pairs={{0,2},{1,3},{2,4},{3,5},{4,6},{5,7},{6,0},{7,1},{8,10},{9,11},{10,... | collective-permute-start | bytes 270344 | tf_op jit(solution)/shard_map/ppermute | solution.py:40
  94.8 7.2 %collective-permute-start.17 = (bf16[352,128]{1,0:T(8,128)(2,1)S(1)}, bf16[352,128]{1,0:T(8,128)(2,1)S(1)}, u32[]{:S(2)}, u32[]{:S(2)}) collective-permute-start(bf16[352,128]{1,0:T(8,128)(2,1)S(1)} %get-tuple-element.92), channel_id=1, source_target_pairs={{0,6},{1,7},{2,0},{3,1},{4,2},{5,3},{6,4},{7,5},{8,14},{9,15},{10,... | collective-permute-start | bytes 270344 | tf_op jit(solution)/shard_map/ppermute | solution.py:40
  102.0 5.3 %collective-permute-start.18 = (bf16[512,128]{1,0:T(8,128)(2,1)S(1)}, bf16[512,128]{1,0:T(8,128)(2,1)S(1)}, u32[]{:S(2)}, u32[]{:S(2)}) collective-permute-start(bf16[512,128]{1,0:T(8,128)(2,1)S(1)} %get-tuple-element.101), channel_id=1, source_target_pairs={{0,8},{16,24},{32,40},{48,56},{64,72},{80,88},{96,104},{112,120},{... | collective-permute-start | bytes 393224 | tf_op jit(solution)/shard_map/ppermute | solution.py:31
  102.1 10.5 %collective-permute-start.19 = (bf16[512,128]{1,0:T(8,128)(2,1)S(1)}, bf16[512,128]{1,0:T(8,128)(2,1)S(1)}, u32[]{:S(2)}, u32[]{:S(2)}) collective-permute-start(bf16[512,128]{1,0:T(8,128)(2,1)S(1)} %get-tuple-element.102), channel_id=1, source_target_pairs={{8,16},{24,32},{40,48},{56,64},{72,80},{88,96},{104,112},{120,128}... | collective-permute-start | bytes 393224 | tf_op jit(solution)/shard_map/ppermute | solution.py:31
  (5 other events, 10.2 us)

commit v4 on v3

--- a/solution.py
+++ b/solution.py
@@ -11,7 +11,7 @@
 SMEM = pl.BlockSpec(memory_space=pltpu.SMEM)
 LANES = 128
 ROWS, PARTS, STEP = 64, 8, 3
-CHUNKS = ((0, 16, 0, 6), (32, 32, 0, 3), (32, 32, 3, 3), (16, 16, 0, 3), (16, 16, 3, 3))
+CHUNKS = ((0, 16, 0, 3), (0, 16, 3, 3), (32, 32, 0, 3), (32, 32, 3, 3), (16, 16, 0, 3), (16, 16, 3, 3))
 EARLY, LATE = 384, 128
 EARLY_U1, EARLY_U2, EARLY_ALL = 192, 144, 672
 LATE_U1, LATE_U2, LATE_ALL = 64, 112, 352
@@ -146,15 +146,18 @@
 
 
 def begin(near, first, second):
-    shape = first.shape
-
-    def kernel(near, first, second, ahead, behind, upper, corner):
-        ahead[...], behind[...] = pick(first, second)
+    height, depth = first[0].shape
+    shape = (height, len(first) * depth)
+
+    def kernel(near, first0, first1, second0, second1, ahead, behind, upper, corner):
+        low, high = pl.ds(0, depth), pl.ds(depth, depth)
+        ahead[:, low], behind[:, low] = pick(first0, second0)
+        ahead[:, high], behind[:, high] = pick(first1, second1)
         upper[...] = contract(near[...], ahead[...])
         corner[...] = contract(behind[...], ahead[...])
 
-    outputs = [(shape, BF16), (shape, BF16), ((near.shape[0], shape[0]), F32), ((shape[0], shape[0]), F32)]
-    return products(kernel, (near, first, second), outputs, 2 * near.size * shape[0])
+    outputs = [(shape, BF16), (shape, BF16), ((near.shape[0], height), F32), ((height, height), F32)]
+    return products(kernel, (near, *first, *second), outputs, 2 * near.size * height)
 
 
 def advance(near, ahead0, behind0, first, second):
@@ -296,7 +299,7 @@
 
 def send_places(pieces):
     received = []
-    for steps in (2, 1, 3):
+    for steps in (1, 2, 3):
         received.append(shift_y(pieces[steps - 1], steps))
     return received
 
@@ -443,13 +446,13 @@
         second.append(swap_atoms(two, 1))
         first.append(swap_atoms(one, 0))
     near = transform(source, blocks, screen)
-    start = begin(near, first[0], second[0])
-    half = advance(near, *start[:2], first[1], second[1])
-    kept, sent, ahead, behind = pack_early(near, start, half, first[2], second[2])
+    start = begin(near, first[:2], second[:2])
+    half = advance(near, *start[:2], first[2], second[2])
+    kept, sent, ahead, behind = pack_early(near, start, half, first[3], second[3])
     total, *pieces = join_core(kept, swap_core(sent))
     received = send_places(pieces)
-    middle = pack_middle(near, *start[:2], *half[:2], first[3], second[3])
-    kept, sent = pack_late(near, *start[:2], ahead, behind, middle, first[4], second[4])
+    middle = pack_middle(near, *start[:2], *half[:2], first[4], second[4])
+    kept, sent = pack_late(near, *start[:2], ahead, behind, middle, first[5], second[5])
     late_total, *late_pieces = join_core(kept, swap_core(sent))
     late_received = send_places(late_pieces)
     upper, rest = join_early(after(total, *late_pieces), received)

time: 114 us -> 125 us (1.096)
  the two profiles are of different devices: /device:TPU:136 before, /device:TPU:128 now
where the time goes in v4:
time: 125 us
  starting transfers between devices  45.4 us (36%)
  waiting for transfers between devices  44.3 us (35%)
  Pallas kernels  31.8 us (25%)
  local copies, waits for them, and re-layouts  2.81 us (2%)
    ppermute x14, waiting for transfers between devices, swap_atoms(): return lax.ppermute(value, 'atoms', pairs + [(j, i) for i, j in pairs])  37.3 us
    ppermute x14, starting transfers between devices, swap_atoms(): return lax.ppermute(value, 'atoms', pairs + [(j, i) for i, j in pairs])  35.5 us
    pallas_call x6, Pallas kernels, split(): pl.pallas_call(kernel, grid=(count // STEP,), in_specs=[SMEM, pl.BlockSpe...  16.1 us
    pallas_call x5, Pallas kernels, products(): pl.pallas_call(kernel, in_specs=[VMEM] * len(inputs), out_specs=[VMEM] *...  10.8 us
    ppermute x6, starting transfers between devices, shift_y(): lax.ppermute(value, 'aux', [(i, (i + 2 * steps) % count) for i in range(c...  9.68 us
    ppermute x6, waiting for transfers between devices, shift_y(): lax.ppermute(value, 'aux', [(i, (i + 2 * steps) % count) for i in range(c...  7.02 us
    unnamed x24, local copies, waits for them, and re-layouts  2.81 us
    pallas_call x1, Pallas kernels, transform(): pl.pallas_call(kernel, grid=(count // STEP,), in_specs=[SMEM, pl.BlockSpe...  2.74 us
  transfers between devices with their start and end apart: 22, of which 8 were waited for; matrix products, arithmetic and copies ran while one was open for 0% of the time, Pallas kernels for 21%

profile of v4, /device:TPU:128, one launch (start us, length us, event | category | flops | bytes accessed | tf_op | source)
XLA Modules:
  0.0 124.8 jit_solution(105272243103762090)
XLA Ops:
  0.0 2.5 %shard_map.37 = (bf16[128,1536]{1,0:T(8,128)(2,1)}, bf16[128,1536]{1,0:T(8,128)(2,1)}) custom-call(s32[1,2]{1,0:T(1,128)} %flag.13, bf16[6,8,64,512]{3,2,1,0:T(8,128)(2,1)} %bitcast.2, bf16[2,512,512]{2,1,0:T(8,128)(2,1)} %bitcast.9), custom_call_target="tpu_custom_call" | custom-call | flops 201326592 | bytes 1179648 | tf_op jit(solution)/shard_map/pallas_call | solution.py:66
  2.5 2.5 %shard_map.38 = (bf16[128,1536]{1,0:T(8,128)(2,1)}, bf16[128,1536]{1,0:T(8,128)(2,1)}) custom-call(s32[1,2]{1,0:T(1,128)} %flag.13, bf16[6,8,64,512]{3,2,1,0:T(8,128)(2,1)} %bitcast.3, bf16[2,512,512]{2,1,0:T(8,128)(2,1)} %bitcast.10), custom_call_target="tpu_custom_call" | custom-call | flops 201326592 | bytes 1179648 | tf_op jit(solution)/shard_map/pallas_call | solution.py:66
  6.4 3.5 %collective-permute-start.3 = (bf16[128,1536]{1,0:T(8,128)(2,1)}, bf16[128,1536]{1,0:T(8,128)(2,1)S(1)}, u32[]{:S(2)}, u32[]{:S(2)}) collective-permute-start(bf16[128,1536]{1,0:T(8,128)(2,1)} %get-tuple-element.70), channel_id=1, source_target_pairs={{8,16},{24,32},{40,48},{56,64},{72,80},{88,96},{104,112},{120,128}... | collective-permute-start | bytes 1179656 | tf_op jit(solution)/shard_map/ppermute | solution.py:31
  11.1 3.0 %shard_map.39 = (bf16[256,1536]{1,0:T(8,128)(2,1)}, bf16[256,1536]{1,0:T(8,128)(2,1)}) custom-call(s32[1,2]{1,0:T(1,128)} %flag.13, bf16[6,8,64,512]{3,2,1,0:T(8,128)(2,1)} %bitcast.4, bf16[2,512,512]{2,1,0:T(8,128)(2,1)} %bitcast.11), custom_call_target="tpu_custom_call" | custom-call | flops 402653184 | bytes 2359296 | tf_op jit(solution)/shard_map/pallas_call | solution.py:66
  15.1 5.6 %collective-permute-start.5 = (bf16[256,1536]{1,0:T(8,128)(2,1)}, bf16[256,1536]{1,0:T(8,128)(2,1)}, u32[]{:S(2)}, u32[]{:S(2)}) collective-permute-start(bf16[256,1536]{1,0:T(8,128)(2,1)} %get-tuple-element.75), channel_id=1, source_target_pairs={{8,16},{24,32},{40,48},{56,64},{72,80},{88,96},{104,112},{120,128}... | collective-permute-start | bytes 2359304 | tf_op jit(solution)/shard_map/ppermute | solution.py:31
  20.7 3.0 %shard_map.40 = (bf16[256,1536]{1,0:T(8,128)(2,1)}, bf16[256,1536]{1,0:T(8,128)(2,1)}) custom-call(s32[1,2]{1,0:T(1,128)} %flag.13, bf16[6,8,64,512]{3,2,1,0:T(8,128)(2,1)} %bitcast.5, bf16[2,512,512]{2,1,0:T(8,128)(2,1)} %bitcast.12), custom_call_target="tpu_custom_call" | custom-call | flops 402653184 | bytes 2359296 | tf_op jit(solution)/shard_map/pallas_call | solution.py:66
  24.6 3.5 %collective-permute-start.7 = (bf16[256,1536]{1,0:T(8,128)(2,1)}, bf16[256,1536]{1,0:T(8,128)(2,1)}, u32[]{:S(2)}, u32[]{:S(2)}) collective-permute-start(bf16[256,1536]{1,0:T(8,128)(2,1)} %get-tuple-element.80), channel_id=1, source_target_pairs={{8,16},{24,32},{40,48},{56,64},{72,80},{88,96},{104,112},{120,128}... | collective-permute-start | bytes 2359304 | tf_op jit(solution)/shard_map/ppermute | solution.py:31
  28.9 5.6 %collective-permute-start.2 = (bf16[128,1536]{1,0:T(8,128)(2,1)}, bf16[128,1536]{1,0:T(8,128)(2,1)}, u32[]{:S(2)}, u32[]{:S(2)}) collective-permute-start(bf16[128,1536]{1,0:T(8,128)(2,1)} %get-tuple-element.69), channel_id=1, source_target_pairs={{8,16},{24,32},{40,48},{56,64},{72,80},{88,96},{104,112},{120,128}... | collective-permute-start | bytes 1179656 | tf_op jit(solution)/shard_map/ppermute | solution.py:31
  34.5 2.5 %shard_map.41 = (bf16[128,1536]{1,0:T(8,128)(2,1)}, bf16[128,1536]{1,0:T(8,128)(2,1)}) custom-call(s32[1,2]{1,0:T(1,128)} %flag.13, bf16[6,8,64,512]{3,2,1,0:T(8,128)(2,1)} %bitcast.6, bf16[2,512,512]{2,1,0:T(8,128)(2,1)} %bitcast.13), custom_call_target="tpu_custom_call" | custom-call | flops 201326592 | bytes 1179648 | tf_op jit(solution)/shard_map/pallas_call | solution.py:66
  37.0 2.6 %shard_map.42 = (bf16[128,1536]{1,0:T(8,128)(2,1)}, bf16[128,1536]{1,0:T(8,128)(2,1)}) custom-call(s32[1,2]{1,0:T(1,128)} %flag.13, bf16[6,8,64,512]{3,2,1,0:T(8,128)(2,1)} %bitcast.7, bf16[2,512,512]{2,1,0:T(8,128)(2,1)} %bitcast.14), custom_call_target="tpu_custom_call" | custom-call | flops 201326592 | bytes 1179648 | tf_op jit(solution)/shard_map/pallas_call | solution.py:66
  40.9 2.7 %shard_map.43.near = bf16[512,3072]{1,0:T(8,128)(2,1)S(1)} custom-call(s32[1,2]{1,0:T(1,128)S(1)} %copy-done.6, bf16[6,8,64,512]{3,2,1,0:T(8,128)(2,1)S(1)} %bitcast.8, bf16[2,512,512]{2,1,0:T(8,128)(2,1)S(1)} %bitcast.15), custom_call_target="tpu_custom_call" | custom-call | flops 1610612736 | bytes 6291456 | tf_op jit(solution)/shard_map/pallas_call | solution.py:90
  43.6 21.1 %collective-permute-done.2.second0 = bf16[128,1536]{1,0:T(8,128)(2,1)} collective-permute-done((bf16[128,1536]{1,0:T(8,128)(2,1)}, bf16[128,1536]{1,0:T(8,128)(2,1)}, u32[]{:S(2)}, u32[]{:S(2)}) %collective-permute-start.2) | collective-permute-done | bytes 393248 | tf_op jit(solution)/shard_map/ppermute | solution.py:31
  64.7 2.2 %shard_map.44 = (bf16[128,3072]{1,0:T(8,128)(2,1)S(1)}, bf16[128,3072]{1,0:T(8,128)(2,1)S(1)}, f32[512,128]{1,0:T(8,128)S(1)}, f32[128,128]{1,0:T(8,128)S(1)}) custom-call(bf16[512,3072]{1,0:T(8,128)(2,1)S(1)} %shard_map.43.near, bf16[128,1536]{1,0:T(8,128)(2,1)S(1)} %copy-done.5, bf16[128,1536]{1,0:T(8,128)(2,1)S(1)} %collective-permute-done.1.first1, ...), custom_call_target="tpu_custom_call" | custom-call | flops 402653184 | bytes 4718592 | tf_op jit(solution)/shard_map/pallas_call | solution.py:137
  66.9 5.0 %collective-permute-start.10 = (bf16[128,1536]{1,0:T(8,128)(2,1)S(1)}, bf16[128,1536]{1,0:T(8,128)(2,1)S(1)}, u32[]{:S(2)}, u32[]{:S(2)}) collective-permute-start(bf16[128,1536]{1,0:T(8,128)(2,1)S(1)} %copy-done.9), channel_id=1, source_target_pairs={{8,16},{24,32},{40,48},{56,64},{72,80},{88,96},{104,112},{120,128}... | collective-permute-start | bytes 1179656 | tf_op jit(solution)/shard_map/ppermute | solution.py:31
  72.0 2.6 %shard_map.45 = (bf16[256,1536]{1,0:T(8,128)(2,1)S(1)}, bf16[256,1536]{1,0:T(8,128)(2,1)S(1)}, f32[512,256]{1,0:T(8,128)S(1)}, f32[128,256]{1,0:T(8,128)S(1)}, f...) custom-call(bf16[512,3072]{1,0:T(8,128)(2,1)S(1)} %shard_map.43.near, bf16[128,3072]{1,0:T(8,128)(2,1)S(1)} %get-tuple-element.71.ahead0, ...), custom_call_target="tpu_custom_call" | custom-call | flops 805306368 | bytes 6291456 | tf_op jit(solution)/shard_map/pallas_call | solution.py:137
  74.6 3.2 %shard_map.46 = (f32[4,672,128]{2,1,0:T(8,128)S(1)}, bf16[4,672,128]{2,1,0:T(8,128)(2,1)S(1)}, bf16[256,1536]{1,0:T(8,128)(2,1)S(1)}, bf16[256,1536]{1,0:T(8,128)(2,1)S(1)}) custom-call(bf16[512,3072]{1,0:T(8,128)(2,1)S(1)} %shard_map.43.near, bf16[128,3072]{1,0:T(8,128)(2,1)S(1)} %get-tuple-element.71.ahead0, ...), custom_call_target="tpu_custom_call" | custom-call | flops 603979776 | bytes 6979584 | tf_op jit(solution)/shard_map/pallas_call | solution.py:137
  78.0 4.3 %collective-permute-start.12 = (bf16[128,1536]{1,0:T(8,128)(2,1)S(1)}, bf16[128,1536]{1,0:T(8,128)(2,1)S(1)}, u32[]{:S(2)}, u32[]{:S(2)}) collective-permute-start(bf16[128,1536]{1,0:T(8,128)(2,1)S(1)} %copy-done.7), channel_id=1, source_target_pairs={{8,16},{24,32},{40,48},{56,64},{72,80},{88,96},{104,112},{120,128}... | collective-permute-start | bytes 1179656 | tf_op jit(solution)/shard_map/ppermute | solution.py:31
  83.7 5.7 %collective-permute-done.11.first = bf16[128,1536]{1,0:T(8,128)(2,1)S(1)} collective-permute-done((bf16[128,1536]{1,0:T(8,128)(2,1)S(1)}, bf16[128,1536]{1,0:T(8,128)(2,1)S(1)}, u32[]{:S(2)}, u32[]{:S(2)}) %collective-permute-start.11) | collective-permute-done | bytes 393248 | tf_op jit(solution)/shard_map/ppermute | solution.py:31
  89.4 5.2 %collective-permute-done.12.second = bf16[128,1536]{1,0:T(8,128)(2,1)S(1)} collective-permute-done((bf16[128,1536]{1,0:T(8,128)(2,1)S(1)}, bf16[128,1536]{1,0:T(8,128)(2,1)S(1)}, u32[]{:S(2)}, u32[]{:S(2)}) %collective-permute-start.12) | collective-permute-done | bytes 393248 | tf_op jit(solution)/shard_map/ppermute | solution.py:31
  98.1 2.9 %collective-permute-start.15 = (bf16[672,128]{1,0:T(8,128)(2,1)S(1)}, bf16[672,128]{1,0:T(8,128)(2,1)S(1)}, u32[]{:S(2)}, u32[]{:S(2)}) collective-permute-start(bf16[672,128]{1,0:T(8,128)(2,1)S(1)} %get-tuple-element.101), channel_id=1, source_target_pairs={{0,4},{1,5},{2,6},{3,7},{4,0},{5,1},{6,2},{7,3},{8,12},{9,13},{10,... | collective-permute-start | bytes 516104 | tf_op jit(solution)/shard_map/ppermute | solution.py:40
  104.5 2.2 %collective-permute-start.19 = (bf16[352,128]{1,0:T(8,128)(2,1)S(1)}, bf16[352,128]{1,0:T(8,128)(2,1)S(1)}, u32[]{:S(2)}, u32[]{:S(2)}) collective-permute-start(bf16[352,128]{1,0:T(8,128)(2,1)S(1)} %get-tuple-element.98), channel_id=1, source_target_pairs={{0,6},{1,7},{2,0},{3,1},{4,2},{5,3},{6,4},{7,5},{8,14},{9,15},{10,... | collective-permute-start | bytes 270344 | tf_op jit(solution)/shard_map/ppermute | solution.py:40
  106.8 3.2 %collective-permute-done.15.two = bf16[672,128]{1,0:T(8,128)(2,1)S(1)} collective-permute-done((bf16[672,128]{1,0:T(8,128)(2,1)S(1)}, bf16[672,128]{1,0:T(8,128)(2,1)S(1)}, u32[]{:S(2)}, u32[]{:S(2)}) %collective-permute-start.15) | collective-permute-done | bytes 172064 | tf_op jit(solution)/shard_map/ppermute | solution.py:40
  113.5 4.1 %collective-permute-start.21 = (bf16[512,128]{1,0:T(8,128)(2,1)S(1)}, bf16[512,128]{1,0:T(8,128)(2,1)S(1)}, u32[]{:S(2)}, u32[]{:S(2)}) collective-permute-start(bf16[512,128]{1,0:T(8,128)(2,1)S(1)} %get-tuple-element.108), channel_id=1, source_target_pairs={{8,16},{24,32},{40,48},{56,64},{72,80},{88,96},{104,112},{120,128}... | collective-permute-start | bytes 393224 | tf_op jit(solution)/shard_map/ppermute | solution.py:31
  118.5 5.2 %collective-permute-done.21.second = bf16[512,128]{1,0:T(8,128)(2,1)S(1)} collective-permute-done((bf16[512,128]{1,0:T(8,128)(2,1)S(1)}, bf16[512,128]{1,0:T(8,128)(2,1)S(1)}, u32[]{:S(2)}, u32[]{:S(2)}) %collective-permute-start.21) | collective-permute-done | bytes 131104 | tf_op jit(solution)/shard_map/ppermute | solution.py:31
  (64 shorter events, 20.4 us)
Async XLA Ops:
  4.9 18.8 %collective-permute-start.1 = (bf16[128,1536]{1,0:T(8,128)(2,1)}, bf16[128,1536]{1,0:T(8,128)(2,1)S(1)}, u32[]{:S(2)}, u32[]{:S(2)}) collective-permute-start(bf16[128,1536]{1,0:T(8,128)(2,1)} %get-tuple-element.59), channel_id=1, source_target_pairs={{0,8},{16,24},{32,40},{48,56},{64,72},{80,88},{96,104},{112,120},{... | collective-permute-start | bytes 1179656 | tf_op jit(solution)/shard_map/ppermute | solution.py:31
  6.4 17.3 %collective-permute-start.3 = (bf16[128,1536]{1,0:T(8,128)(2,1)}, bf16[128,1536]{1,0:T(8,128)(2,1)S(1)}, u32[]{:S(2)}, u32[]{:S(2)}) collective-permute-start(bf16[128,1536]{1,0:T(8,128)(2,1)} %get-tuple-element.70), channel_id=1, source_target_pairs={{8,16},{24,32},{40,48},{56,64},{72,80},{88,96},{104,112},{120,128}... | collective-permute-start | bytes 1179656 | tf_op jit(solution)/shard_map/ppermute | solution.py:31
  10.0 18.2 %collective-permute-start = (bf16[128,1536]{1,0:T(8,128)(2,1)S(1)}, bf16[128,1536]{1,0:T(8,128)(2,1)S(1)}, u32[]{:S(2)}, u32[]{:S(2)}) collective-permute-start(bf16[128,1536]{1,0:T(8,128)(2,1)S(1)} %copy-done.11), channel_id=1, source_target_pairs={{0,8},{16,24},{32,40},{48,56},{64,72},{80,88},{96,104},{112,120},{... | collective-permute-start | bytes 1179656 | tf_op jit(solution)/shard_map/ppermute | solution.py:31
  14.1 52.7 %collective-permute-start.4 = (bf16[256,1536]{1,0:T(8,128)(2,1)}, bf16[256,1536]{1,0:T(8,128)(2,1)}, u32[]{:S(2)}, u32[]{:S(2)}) collective-permute-start(bf16[256,1536]{1,0:T(8,128)(2,1)} %get-tuple-element.61), channel_id=1, source_target_pairs={{0,8},{16,24},{32,40},{48,56},{64,72},{80,88},{96,104},{112,120},{... | collective-permute-start | bytes 2359304 | tf_op jit(solution)/shard_map/ppermute | solution.py:31
  15.1 56.8 %collective-permute-start.5 = (bf16[256,1536]{1,0:T(8,128)(2,1)}, bf16[256,1536]{1,0:T(8,128)(2,1)}, u32[]{:S(2)}, u32[]{:S(2)}) collective-permute-start(bf16[256,1536]{1,0:T(8,128)(2,1)} %get-tuple-element.75), channel_id=1, source_target_pairs={{8,16},{24,32},{40,48},{56,64},{72,80},{88,96},{104,112},{120,128}... | collective-permute-start | bytes 2359304 | tf_op jit(solution)/shard_map/ppermute | solution.py:31
  23.8 50.8 %collective-permute-start.6 = (bf16[256,1536]{1,0:T(8,128)(2,1)}, bf16[256,1536]{1,0:T(8,128)(2,1)}, u32[]{:S(2)}, u32[]{:S(2)}) collective-permute-start(bf16[256,1536]{1,0:T(8,128)(2,1)} %get-tuple-element.63), channel_id=1, source_target_pairs={{0,8},{16,24},{32,40},{48,56},{64,72},{80,88},{96,104},{112,120},{... | collective-permute-start | bytes 2359304 | tf_op jit(solution)/shard_map/ppermute | solution.py:31
  24.6 50.0 %collective-permute-start.7 = (bf16[256,1536]{1,0:T(8,128)(2,1)}, bf16[256,1536]{1,0:T(8,128)(2,1)}, u32[]{:S(2)}, u32[]{:S(2)}) collective-permute-start(bf16[256,1536]{1,0:T(8,128)(2,1)} %get-tuple-element.80), channel_id=1, source_target_pairs={{8,16},{24,32},{40,48},{56,64},{72,80},{88,96},{104,112},{120,128}... | collective-permute-start | bytes 2359304 | tf_op jit(solution)/shard_map/ppermute | solution.py:31
  28.9 35.8 %collective-permute-start.2 = (bf16[128,1536]{1,0:T(8,128)(2,1)}, bf16[128,1536]{1,0:T(8,128)(2,1)}, u32[]{:S(2)}, u32[]{:S(2)}) collective-permute-start(bf16[128,1536]{1,0:T(8,128)(2,1)} %get-tuple-element.69), channel_id=1, source_target_pairs={{8,16},{24,32},{40,48},{56,64},{72,80},{88,96},{104,112},{120,128}... | collective-permute-start | bytes 1179656 | tf_op jit(solution)/shard_map/ppermute | solution.py:31
  40.8 23.8 %copy-start.3 = (bf16[128,1536]{1,0:T(8,128)(2,1)S(1)}, bf16[128,1536]{1,0:T(8,128)(2,1)}, u32[]{:S(2)}) copy-start(bf16[128,1536]{1,0:T(8,128)(2,1)} %copy-done.2) | copy-start | bytes 1179652
  40.9 23.8 %copy-start.5 = (bf16[128,1536]{1,0:T(8,128)(2,1)S(1)}, bf16[128,1536]{1,0:T(8,128)(2,1)}, u32[]{:S(2)}) copy-start(bf16[128,1536]{1,0:T(8,128)(2,1)} %copy-done.4) | copy-start | bytes 1179652
  64.7 17.7 %collective-permute-start.9 = (bf16[128,1536]{1,0:T(8,128)(2,1)S(1)}, bf16[128,1536]{1,0:T(8,128)(2,1)S(1)}, u32[]{:S(2)}, u32[]{:S(2)}) collective-permute-start(bf16[128,1536]{1,0:T(8,128)(2,1)S(1)} %copy-done.10), channel_id=1, source_target_pairs={{0,8},{16,24},{32,40},{48,56},{64,72},{80,88},{96,104},{112,120},{... | collective-permute-start | bytes 1179656 | tf_op jit(solution)/shard_map/ppermute | solution.py:31
  66.9 15.4 %collective-permute-start.10 = (bf16[128,1536]{1,0:T(8,128)(2,1)S(1)}, bf16[128,1536]{1,0:T(8,128)(2,1)S(1)}, u32[]{:S(2)}, u32[]{:S(2)}) collective-permute-start(bf16[128,1536]{1,0:T(8,128)(2,1)S(1)} %copy-done.9), channel_id=1, source_target_pairs={{8,16},{24,32},{40,48},{56,64},{72,80},{88,96},{104,112},{120,128}... | collective-permute-start | bytes 1179656 | tf_op jit(solution)/shard_map/ppermute | solution.py:31
  77.8 18.5 %collective-permute-start.8 = (bf16[4,672,128]{2,1,0:T(8,128)(2,1)S(1)}, bf16[4,672,128]{2,1,0:T(8,128)(2,1)S(1)}, u32[]{:S(2)}, u32[]{:S(2)}) collective-permute-start(bf16[4,672,128]{2,1,0:T(8,128)(2,1)S(1)} %get-tuple-element.82), channel_id=1, source_target_pairs={{0,1},{1,0},{2,3},{3,2},{4,5},{5,4},{6,7},{7,6},{8,9},{9,8},{10,11... | collective-permute-start | bytes 2064392 | tf_op jit(solution)/shard_map/ppermute | solution.py:35
  77.9 11.5 %collective-permute-start.11 = (bf16[128,1536]{1,0:T(8,128)(2,1)S(1)}, bf16[128,1536]{1,0:T(8,128)(2,1)S(1)}, u32[]{:S(2)}, u32[]{:S(2)}) collective-permute-start(bf16[128,1536]{1,0:T(8,128)(2,1)S(1)} %copy-done.8), channel_id=1, source_target_pairs={{0,8},{16,24},{32,40},{48,56},{64,72},{80,88},{96,104},{112,120},{... | collective-permute-start | bytes 1179656 | tf_op jit(solution)/shard_map/ppermute | solution.py:31
  78.0 16.6 %collective-permute-start.12 = (bf16[128,1536]{1,0:T(8,128)(2,1)S(1)}, bf16[128,1536]{1,0:T(8,128)(2,1)S(1)}, u32[]{:S(2)}, u32[]{:S(2)}) collective-permute-start(bf16[128,1536]{1,0:T(8,128)(2,1)S(1)} %copy-done.7), channel_id=1, source_target_pairs={{8,16},{24,32},{40,48},{56,64},{72,80},{88,96},{104,112},{120,128}... | collective-permute-start | bytes 1179656 | tf_op jit(solution)/shard_map/ppermute | solution.py:31
  96.2 6.2 %collective-permute-start.13 = (bf16[4,352,128]{2,1,0:T(8,128)(2,1)S(1)}, bf16[4,352,128]{2,1,0:T(8,128)(2,1)S(1)}, u32[]{:S(2)}, u32[]{:S(2)}) collective-permute-start(bf16[4,352,128]{2,1,0:T(8,128)(2,1)S(1)} %get-tuple-element.95), channel_id=1, source_target_pairs={{0,1},{1,0},{2,3},{3,2},{4,5},{5,4},{6,7},{7,6},{8,9},{9,8},{10,11... | collective-permute-start | bytes 1081352 | tf_op jit(solution)/shard_map/ppermute | solution.py:35
  96.4 8.1 %collective-permute-start.14 = (bf16[672,128]{1,0:T(8,128)(2,1)S(1)}, bf16[672,128]{1,0:T(8,128)(2,1)S(1)}, u32[]{:S(2)}, u32[]{:S(2)}) collective-permute-start(bf16[672,128]{1,0:T(8,128)(2,1)S(1)} %get-tuple-element.100), channel_id=1, source_target_pairs={{0,2},{1,3},{2,4},{3,5},{4,6},{5,7},{6,0},{7,1},{8,10},{9,11},{10,... | collective-permute-start | bytes 516104 | tf_op jit(solution)/shard_map/ppermute | solution.py:40
  98.1 11.9 %collective-permute-start.15 = (bf16[672,128]{1,0:T(8,128)(2,1)S(1)}, bf16[672,128]{1,0:T(8,128)(2,1)S(1)}, u32[]{:S(2)}, u32[]{:S(2)}) collective-permute-start(bf16[672,128]{1,0:T(8,128)(2,1)S(1)} %get-tuple-element.101), channel_id=1, source_target_pairs={{0,4},{1,5},{2,6},{3,7},{4,0},{5,1},{6,2},{7,3},{8,12},{9,13},{10,... | collective-permute-start | bytes 516104 | tf_op jit(solution)/shard_map/ppermute | solution.py:40
  101.0 9.0 %collective-permute-start.16 = (bf16[672,128]{1,0:T(8,128)(2,1)S(1)}, bf16[672,128]{1,0:T(8,128)(2,1)S(1)}, u32[]{:S(2)}, u32[]{:S(2)}) collective-permute-start(bf16[672,128]{1,0:T(8,128)(2,1)S(1)} %get-tuple-element.102), channel_id=1, source_target_pairs={{0,6},{1,7},{2,0},{3,1},{4,2},{5,3},{6,4},{7,5},{8,14},{9,15},{10,... | collective-permute-start | bytes 516104 | tf_op jit(solution)/shard_map/ppermute | solution.py:40
  102.4 9.1 %collective-permute-start.17 = (bf16[352,128]{1,0:T(8,128)(2,1)S(1)}, bf16[352,128]{1,0:T(8,128)(2,1)S(1)}, u32[]{:S(2)}, u32[]{:S(2)}) collective-permute-start(bf16[352,128]{1,0:T(8,128)(2,1)S(1)} %get-tuple-element.96), channel_id=1, source_target_pairs={{0,2},{1,3},{2,4},{3,5},{4,6},{5,7},{6,0},{7,1},{8,10},{9,11},{10,... | collective-permute-start | bytes 270344 | tf_op jit(solution)/shard_map/ppermute | solution.py:40
  103.2 10.1 %collective-permute-start.18 = (bf16[352,128]{1,0:T(8,128)(2,1)S(1)}, bf16[352,128]{1,0:T(8,128)(2,1)S(1)}, u32[]{:S(2)}, u32[]{:S(2)}) collective-permute-start(bf16[352,128]{1,0:T(8,128)(2,1)S(1)} %get-tuple-element.97), channel_id=1, source_target_pairs={{0,4},{1,5},{2,6},{3,7},{4,0},{5,1},{6,2},{7,3},{8,12},{9,13},{10,... | collective-permute-start | bytes 270344 | tf_op jit(solution)/shard_map/ppermute | solution.py:40
  104.5 8.8 %collective-permute-start.19 = (bf16[352,128]{1,0:T(8,128)(2,1)S(1)}, bf16[352,128]{1,0:T(8,128)(2,1)S(1)}, u32[]{:S(2)}, u32[]{:S(2)}) collective-permute-start(bf16[352,128]{1,0:T(8,128)(2,1)S(1)} %get-tuple-element.98), channel_id=1, source_target_pairs={{0,6},{1,7},{2,0},{3,1},{4,2},{5,3},{6,4},{7,5},{8,14},{9,15},{10,... | collective-permute-start | bytes 270344 | tf_op jit(solution)/shard_map/ppermute | solution.py:40
  113.4 5.1 %collective-permute-start.20 = (bf16[512,128]{1,0:T(8,128)(2,1)S(1)}, bf16[512,128]{1,0:T(8,128)(2,1)S(1)}, u32[]{:S(2)}, u32[]{:S(2)}) collective-permute-start(bf16[512,128]{1,0:T(8,128)(2,1)S(1)} %get-tuple-element.107), channel_id=1, source_target_pairs={{0,8},{16,24},{32,40},{48,56},{64,72},{80,88},{96,104},{112,120},{... | collective-permute-start | bytes 393224 | tf_op jit(solution)/shard_map/ppermute | solution.py:31
  113.5 10.2 %collective-permute-start.21 = (bf16[512,128]{1,0:T(8,128)(2,1)S(1)}, bf16[512,128]{1,0:T(8,128)(2,1)S(1)}, u32[]{:S(2)}, u32[]{:S(2)}) collective-permute-start(bf16[512,128]{1,0:T(8,128)(2,1)S(1)} %get-tuple-element.108), channel_id=1, source_target_pairs={{8,16},{24,32},{40,48},{56,64},{72,80},{88,96},{104,112},{120,128}... | collective-permute-start | bytes 393224 | tf_op jit(solution)/shard_map/ppermute | solution.py:31
  (10 other events, 69.4 us)

commit v5 on v4

--- a/solution.py
+++ b/solution.py
@@ -312,62 +312,47 @@
     return value
 
 
-def join_early(total, received):
+def write_pair(even, first, second, lower, upper_far):
+    def write(low, far):
+        low[pl.ds(0, lower.shape[0]), :] = lower
+        far[pl.ds(0, upper_far.shape[0]), :] = upper_far
+        rest = lower.shape[0] - upper_far.shape[0]
+        far[pl.ds(upper_far.shape[0], rest), :] = jnp.zeros((rest, lower.shape[1]), BF16)
+
+    pl.when(even)(lambda: write(first, second))
+    pl.when(jnp.logical_not(even))(lambda: write(second, first))
+
+
+def join_group(total, received, first_rows, second_rows):
     rows, width = total.shape
-
-    def kernel(total, one, two, three, upper, rest):
+    height = rows - first_rows - second_rows
+
+    def kernel(total, one, two, three, upper, first, second):
         refs = (total, one, two, three)
-        upper[...] = gather(refs, pl.ds(0, EARLY_U1))
-        rest[...] = gather(refs, pl.ds(EARLY_U1, rows - EARLY_U1)).astype(BF16)
-
-    return pl.pallas_call(
-        kernel,
-        in_specs=[VMEM] * 4,
-        out_specs=[VMEM] * 2,
-        out_shape=[
-            jax.ShapeDtypeStruct((EARLY_U1, width), F32),
-            jax.ShapeDtypeStruct((rows - EARLY_U1, width), BF16),
-        ],
-        compiler_params=params(),
-        cost_estimate=cost(total.size * 3, 12 * total.size),
-    )(total, *received)
-
-
-def join_late(rest, total, received):
+        upper[...] = gather(refs, pl.ds(0, first_rows))
+        far = gather(refs, pl.ds(first_rows, second_rows)).astype(BF16)
+        low = gather(refs, pl.ds(first_rows + second_rows, height)).astype(BF16)
+        write_pair(on_even(), first, second, low, far)
+
+    outputs = [((first_rows, width), F32), ((height, width), BF16), ((height, width), BF16)]
+    return products(kernel, (total, *received), outputs, 3 * total.size)
+
+
+def join_late(prior, total, received):
     rows, width = total.shape
-    far = EARLY_U2 + LATE_U2
-    low = rest.shape[0] - EARLY_U2
-    height = low + rows - LATE_U1 - LATE_U2
-
-    def kernel(rest, total, one, two, three, upper, first, second):
+    height = rows - LATE_U1 - LATE_U2
+    before = prior.shape[0]
+
+    def kernel(prior, total, one, two, three, upper, first, second):
         refs = (total, one, two, three)
-        even = on_even()
         upper[...] = gather(refs, pl.ds(0, LATE_U1))
-        late_far = gather(refs, pl.ds(LATE_U1, LATE_U2)).astype(BF16)
-        late_low = gather(refs, pl.ds(LATE_U1 + LATE_U2, rows - LATE_U1 - LATE_U2)).astype(BF16)
-
-        def write(lower, upper_far):
-            lower[pl.ds(0, low), :] = rest[pl.ds(EARLY_U2, low), :]
-            lower[pl.ds(low, late_low.shape[0]), :] = late_low
-            upper_far[pl.ds(0, EARLY_U2), :] = rest[pl.ds(0, EARLY_U2), :]
-            upper_far[pl.ds(EARLY_U2, LATE_U2), :] = late_far
-            upper_far[pl.ds(far, height - far), :] = jnp.zeros((height - far, width), BF16)
-
-        pl.when(even)(lambda: write(first, second))
-        pl.when(jnp.logical_not(even))(lambda: write(second, first))
-
-    return pl.pallas_call(
-        kernel,
-        in_specs=[VMEM] * 5,
-        out_specs=[VMEM] * 3,
-        out_shape=[
-            jax.ShapeDtypeStruct((LATE_U1, width), F32),
-            jax.ShapeDtypeStruct((height, width), BF16),
-            jax.ShapeDtypeStruct((height, width), BF16),
-        ],
-        compiler_params=params(),
-        cost_estimate=cost(total.size * 3, 12 * total.size),
-    )(rest, total, *received)
+        far = gather(refs, pl.ds(LATE_U1, LATE_U2)).astype(BF16)
+        low = gather(refs, pl.ds(LATE_U1 + LATE_U2, height)).astype(BF16)
+        second[pl.ds(0, before), :] = prior[...]
+        write_pair(on_even(), first, second.at[pl.ds(before, height), :], low, far)
+
+    outputs = [((LATE_U1, width), F32), ((height, width), BF16), ((before + height, width), BF16)]
+    return products(kernel, (prior, total, *received), outputs, 3 * total.size)
 
 
 def restore(order, early, late):
@@ -389,41 +374,36 @@
     )(order, early, late)
 
 
-def assemble(order, upper, first, second):
+def assemble(order, upper, early, late, second):
     width = order.shape[0]
-    late_low = 3 * 144 - 96
-
-    def rows(ref, base, late):
+    before = early.shape[0]
+
+    def rows(early, late, base, late_base):
         body = jnp.concatenate(
-            [ref[pl.ds(base + 48 * t, 48), :] for t in range(3)] + [ref[pl.ds(late, 48), :]], axis=1
+            [early[pl.ds(base + 48 * t, 48), :] for t in range(3)] + [late[pl.ds(late_base, 48), :]], axis=1
         )
-        last = jnp.concatenate([ref[pl.ds(late + 48 + 16 * t, 16), :] for t in range(4)], axis=1)
+        last = jnp.concatenate([late[pl.ds(late_base + 48 + 16 * t, 16), :] for t in range(4)], axis=1)
         return jnp.concatenate([body[:16], last, body[16:]], axis=0)
 
-    def kernel(order, upper, first, second, out):
+    def kernel(order, upper, early, late, second, out):
         even = on_even()
         out[0, 0] = upper[...]
-
-        def write(far, low):
+        tail = second.at[pl.ds(before, late.shape[0]), :]
+
+        def write(far, far_late, low, low_late):
             exact = order[...]
-            out[0, 1] = jnp.dot(rows(far, 0, EARLY_U2), exact, preferred_element_type=F32)
+            out[0, 1] = jnp.dot(rows(far, far_late, 0, 0), exact, preferred_element_type=F32)
             for t in range(4):
                 out[0, 2, pl.ds(0, 16), lanes(t)] = low[pl.ds(48 * t, 16), :].astype(F32)
-                out[0, 2, pl.ds(16, 16), lanes(t)] = low[pl.ds(late_low + 16 * t, 16), :].astype(F32)
+                out[0, 2, pl.ds(16, 16), lanes(t)] = low_late[pl.ds(16 * t, 16), :].astype(F32)
                 out[0, 2, pl.ds(32, 32), lanes(t)] = low[pl.ds(48 * t + 16, 32), :].astype(F32)
-            out[0, 3] = jnp.dot(rows(low, 192, late_low + 64), exact, preferred_element_type=F32)
-
-        pl.when(even)(lambda: write(first, second))
-        pl.when(jnp.logical_not(even))(lambda: write(second, first))
-
-    return pl.pallas_call(
-        kernel,
-        in_specs=[VMEM] * 4,
-        out_specs=VMEM,
-        out_shape=jax.ShapeDtypeStruct((1, 4, ROWS, width), F32),
-        compiler_params=params(),
-        cost_estimate=cost(2 * 2 * ROWS * width**2, 4 * ROWS * width * 8),
-    )(order, upper, first, second)
+            out[0, 3] = jnp.dot(rows(low, low_late, 192, 64), exact, preferred_element_type=F32)
+
+        pl.when(even)(lambda: write(early, late, second, tail))
+        pl.when(jnp.logical_not(even))(lambda: write(second, tail, early, late))
+
+    outputs = [((1, 4, ROWS, width), F32)]
+    return products(kernel, (order, upper, early, late, second), outputs, 4 * ROWS * width**2)[0]
 
 
 def natural_order(width):
@@ -455,13 +435,14 @@
     kept, sent = pack_late(near, *start[:2], ahead, behind, middle, first[5], second[5])
     late_total, *late_pieces = join_core(kept, swap_core(sent))
     late_received = send_places(late_pieces)
-    upper, rest = join_early(after(total, *late_pieces), received)
-    late_upper, one, two = join_late(rest, late_total, late_received)
+    upper, early_first, early_second = join_group(after(total, *late_pieces), received, EARLY_U1, EARLY_U2)
+    early_first = swap_atoms(early_first, 0)
+    late_upper, one, two = join_late(early_second, late_total, late_received)
     two = swap_atoms(two, 1)
     one = swap_atoms(one, 0)
     order = natural_order(width)
     upper = restore(order, upper, late_upper)
-    return assemble(order, upper, one, two)
+    return assemble(order, upper, early_first, one, two)
 
 
 def solution(mesh):

time: 125 us -> 126 us (level)
  the two profiles are of different devices: /device:TPU:128 before, /device:TPU:100 now
where the time goes in v5:
time: 126 us; the launch traced here: 125 us
  starting transfers between devices  49.2 us (39%)
  waiting for transfers between devices  41 us (33%)
  Pallas kernels  31.8 us (25%)
  local copies, waits for them, and re-layouts  2.79 us (2%)
    ppermute x15, starting transfers between devices, swap_atoms(): return lax.ppermute(value, 'atoms', pairs + [(j, i) for i, j in pairs])  39.3 us
    ppermute x15, waiting for transfers between devices, swap_atoms(): return lax.ppermute(value, 'atoms', pairs + [(j, i) for i, j in pairs])  34 us
    pallas_call x6, Pallas kernels, split(): pl.pallas_call(kernel, grid=(count // STEP,), in_specs=[SMEM, pl.BlockSpe...  16.1 us
    pallas_call x8, Pallas kernels, products(): pl.pallas_call(kernel, in_specs=[VMEM] * len(inputs), out_specs=[VMEM] *...  12.1 us
    ppermute x6, starting transfers between devices, shift_y(): lax.ppermute(value, 'aux', [(i, (i + 2 * steps) % count) for i in range(c...  9.67 us
    ppermute x6, waiting for transfers between devices, shift_y(): lax.ppermute(value, 'aux', [(i, (i + 2 * steps) % count) for i in range(c...  7 us
    unnamed x24, local copies, waits for them, and re-layouts  2.79 us
    pallas_call x1, Pallas kernels, transform(): pl.pallas_call(kernel, grid=(count // STEP,), in_specs=[SMEM, pl.BlockSpe...  2.74 us
  transfers between devices with their start and end apart: 23, of which 9 were waited for; matrix products, arithmetic and copies ran while one was open for 0% of the time, Pallas kernels for 21%

profile of v5, /device:TPU:100, one launch (start us, length us, event | category | flops | bytes accessed | tf_op | source)
XLA Modules:
  0.0 125.2 jit_solution(2819670571012118967)
XLA Ops:
  0.0 2.4 %shard_map.37 = (bf16[128,1536]{1,0:T(8,128)(2,1)}, bf16[128,1536]{1,0:T(8,128)(2,1)}) custom-call(s32[1,2]{1,0:T(1,128)} %flag.13, bf16[6,8,64,512]{3,2,1,0:T(8,128)(2,1)} %bitcast.2, bf16[2,512,512]{2,1,0:T(8,128)(2,1)} %bitcast.9), custom_call_target="tpu_custom_call" | custom-call | flops 201326592 | bytes 1179648 | tf_op jit(solution)/shard_map/pallas_call | solution.py:66
  2.4 2.5 %shard_map.38 = (bf16[128,1536]{1,0:T(8,128)(2,1)}, bf16[128,1536]{1,0:T(8,128)(2,1)}) custom-call(s32[1,2]{1,0:T(1,128)} %flag.13, bf16[6,8,64,512]{3,2,1,0:T(8,128)(2,1)} %bitcast.3, bf16[2,512,512]{2,1,0:T(8,128)(2,1)} %bitcast.10), custom_call_target="tpu_custom_call" | custom-call | flops 201326592 | bytes 1179648 | tf_op jit(solution)/shard_map/pallas_call | solution.py:66
  8.1 4.6 %collective-permute-start = (bf16[128,1536]{1,0:T(8,128)(2,1)S(1)}, bf16[128,1536]{1,0:T(8,128)(2,1)S(1)}, u32[]{:S(2)}, u32[]{:S(2)}) collective-permute-start(bf16[128,1536]{1,0:T(8,128)(2,1)S(1)} %copy-done.11), channel_id=1, source_target_pairs={{0,8},{16,24},{32,40},{48,56},{64,72},{80,88},{96,104},{112,120},{... | collective-permute-start | bytes 1179656 | tf_op jit(solution)/shard_map/ppermute | solution.py:31
  12.7 3.0 %shard_map.39 = (bf16[256,1536]{1,0:T(8,128)(2,1)}, bf16[256,1536]{1,0:T(8,128)(2,1)}) custom-call(s32[1,2]{1,0:T(1,128)} %flag.13, bf16[6,8,64,512]{3,2,1,0:T(8,128)(2,1)} %bitcast.4, bf16[2,512,512]{2,1,0:T(8,128)(2,1)} %bitcast.11), custom_call_target="tpu_custom_call" | custom-call | flops 402653184 | bytes 2359296 | tf_op jit(solution)/shard_map/pallas_call | solution.py:66
  17.6 3.0 %shard_map.40 = (bf16[256,1536]{1,0:T(8,128)(2,1)}, bf16[256,1536]{1,0:T(8,128)(2,1)}) custom-call(s32[1,2]{1,0:T(1,128)} %flag.13, bf16[6,8,64,512]{3,2,1,0:T(8,128)(2,1)} %bitcast.5, bf16[2,512,512]{2,1,0:T(8,128)(2,1)} %bitcast.12), custom_call_target="tpu_custom_call" | custom-call | flops 402653184 | bytes 2359296 | tf_op jit(solution)/shard_map/pallas_call | solution.py:66
  20.7 3.6 %collective-permute-start.6 = (bf16[256,1536]{1,0:T(8,128)(2,1)}, bf16[256,1536]{1,0:T(8,128)(2,1)}, u32[]{:S(2)}, u32[]{:S(2)}) collective-permute-start(bf16[256,1536]{1,0:T(8,128)(2,1)} %get-tuple-element.64), channel_id=1, source_target_pairs={{0,8},{16,24},{32,40},{48,56},{64,72},{80,88},{96,104},{112,120},{... | collective-permute-start | bytes 2359304 | tf_op jit(solution)/shard_map/ppermute | solution.py:31
  27.8 3.9 %collective-permute-start.2 = (bf16[128,1536]{1,0:T(8,128)(2,1)}, bf16[128,1536]{1,0:T(8,128)(2,1)}, u32[]{:S(2)}, u32[]{:S(2)}) collective-permute-start(bf16[128,1536]{1,0:T(8,128)(2,1)} %get-tuple-element.70), channel_id=1, source_target_pairs={{8,16},{24,32},{40,48},{56,64},{72,80},{88,96},{104,112},{120,128}... | collective-permute-start | bytes 1179656 | tf_op jit(solution)/shard_map/ppermute | solution.py:31
  31.7 2.5 %shard_map.41 = (bf16[128,1536]{1,0:T(8,128)(2,1)}, bf16[128,1536]{1,0:T(8,128)(2,1)}) custom-call(s32[1,2]{1,0:T(1,128)} %flag.13, bf16[6,8,64,512]{3,2,1,0:T(8,128)(2,1)} %bitcast.6, bf16[2,512,512]{2,1,0:T(8,128)(2,1)} %bitcast.13), custom_call_target="tpu_custom_call" | custom-call | flops 201326592 | bytes 1179648 | tf_op jit(solution)/shard_map/pallas_call | solution.py:66
  34.2 2.6 %shard_map.42 = (bf16[128,1536]{1,0:T(8,128)(2,1)}, bf16[128,1536]{1,0:T(8,128)(2,1)}) custom-call(s32[1,2]{1,0:T(1,128)} %flag.13, bf16[6,8,64,512]{3,2,1,0:T(8,128)(2,1)} %bitcast.7, bf16[2,512,512]{2,1,0:T(8,128)(2,1)} %bitcast.14), custom_call_target="tpu_custom_call" | custom-call | flops 201326592 | bytes 1179648 | tf_op jit(solution)/shard_map/pallas_call | solution.py:66
  38.0 2.7 %shard_map.43.near = bf16[512,3072]{1,0:T(8,128)(2,1)S(1)} custom-call(s32[1,2]{1,0:T(1,128)S(1)} %copy-done.6, bf16[6,8,64,512]{3,2,1,0:T(8,128)(2,1)S(1)} %bitcast.8, bf16[2,512,512]{2,1,0:T(8,128)(2,1)S(1)} %bitcast.15), custom_call_target="tpu_custom_call" | custom-call | flops 1610612736 | bytes 6291456 | tf_op jit(solution)/shard_map/pallas_call | solution.py:90
  40.8 20.8 %collective-permute-done.2.second0 = bf16[128,1536]{1,0:T(8,128)(2,1)} collective-permute-done((bf16[128,1536]{1,0:T(8,128)(2,1)}, bf16[128,1536]{1,0:T(8,128)(2,1)}, u32[]{:S(2)}, u32[]{:S(2)}) %collective-permute-start.2) | collective-permute-done | bytes 393248 | tf_op jit(solution)/shard_map/ppermute | solution.py:31
  61.6 5.0 %collective-permute-start.9 = (bf16[128,1536]{1,0:T(8,128)(2,1)S(1)}, bf16[128,1536]{1,0:T(8,128)(2,1)S(1)}, u32[]{:S(2)}, u32[]{:S(2)}) collective-permute-start(bf16[128,1536]{1,0:T(8,128)(2,1)S(1)} %copy-done.10), channel_id=1, source_target_pairs={{0,8},{16,24},{32,40},{48,56},{64,72},{80,88},{96,104},{112,120},{... | collective-permute-start | bytes 1179656 | tf_op jit(solution)/shard_map/ppermute | solution.py:31
  66.7 2.2 %shard_map.44 = (bf16[128,3072]{1,0:T(8,128)(2,1)S(1)}, bf16[128,3072]{1,0:T(8,128)(2,1)S(1)}, f32[512,128]{1,0:T(8,128)S(1)}, f32[128,128]{1,0:T(8,128)S(1)}) custom-call(bf16[512,3072]{1,0:T(8,128)(2,1)S(1)} %shard_map.43.near, bf16[128,1536]{1,0:T(8,128)(2,1)S(1)} %copy-done.5, bf16[128,1536]{1,0:T(8,128)(2,1)S(1)} %collective-permute-done.1.first1, ...), custom_call_target="tpu_custom_call" | custom-call | flops 402653184 | bytes 4718592 | tf_op jit(solution)/shard_map/pallas_call | solution.py:137
  70.8 2.6 %shard_map.45 = (bf16[256,1536]{1,0:T(8,128)(2,1)S(1)}, bf16[256,1536]{1,0:T(8,128)(2,1)S(1)}, f32[512,256]{1,0:T(8,128)S(1)}, f32[128,256]{1,0:T(8,128)S(1)}, f...) custom-call(bf16[512,3072]{1,0:T(8,128)(2,1)S(1)} %shard_map.43.near, bf16[128,3072]{1,0:T(8,128)(2,1)S(1)} %get-tuple-element.72.ahead0, ...), custom_call_target="tpu_custom_call" | custom-call | flops 805306368 | bytes 6291456 | tf_op jit(solution)/shard_map/pallas_call | solution.py:137
  73.5 3.2 %shard_map.46 = (f32[4,672,128]{2,1,0:T(8,128)S(1)}, bf16[4,672,128]{2,1,0:T(8,128)(2,1)S(1)}, bf16[256,1536]{1,0:T(8,128)(2,1)S(1)}, bf16[256,1536]{1,0:T(8,128)(2,1)S(1)}) custom-call(bf16[512,3072]{1,0:T(8,128)(2,1)S(1)} %shard_map.43.near, bf16[128,3072]{1,0:T(8,128)(2,1)S(1)} %get-tuple-element.72.ahead0, ...), custom_call_target="tpu_custom_call" | custom-call | flops 603979776 | bytes 6979584 | tf_op jit(solution)/shard_map/pallas_call | solution.py:137
  76.8 2.3 %collective-permute-start.11 = (bf16[128,1536]{1,0:T(8,128)(2,1)S(1)}, bf16[128,1536]{1,0:T(8,128)(2,1)S(1)}, u32[]{:S(2)}, u32[]{:S(2)}) collective-permute-start(bf16[128,1536]{1,0:T(8,128)(2,1)S(1)} %copy-done.8), channel_id=1, source_target_pairs={{0,8},{16,24},{32,40},{48,56},{64,72},{80,88},{96,104},{112,120},{... | collective-permute-start | bytes 1179656 | tf_op jit(solution)/shard_map/ppermute | solution.py:31
  82.5 6.3 %collective-permute-done.11.first = bf16[128,1536]{1,0:T(8,128)(2,1)S(1)} collective-permute-done((bf16[128,1536]{1,0:T(8,128)(2,1)S(1)}, bf16[128,1536]{1,0:T(8,128)(2,1)S(1)}, u32[]{:S(2)}, u32[]{:S(2)}) %collective-permute-start.11) | collective-permute-done | bytes 393248 | tf_op jit(solution)/shard_map/ppermute | solution.py:31
  88.8 3.3 %collective-permute-done.12.second = bf16[128,1536]{1,0:T(8,128)(2,1)S(1)} collective-permute-done((bf16[128,1536]{1,0:T(8,128)(2,1)S(1)}, bf16[128,1536]{1,0:T(8,128)(2,1)S(1)}, u32[]{:S(2)}, u32[]{:S(2)}) %collective-permute-start.12) | collective-permute-done | bytes 393248 | tf_op jit(solution)/shard_map/ppermute | solution.py:31
  95.6 2.9 %collective-permute-start.15 = (bf16[672,128]{1,0:T(8,128)(2,1)S(1)}, bf16[672,128]{1,0:T(8,128)(2,1)S(1)}, u32[]{:S(2)}, u32[]{:S(2)}) collective-permute-start(bf16[672,128]{1,0:T(8,128)(2,1)S(1)} %get-tuple-element.102), channel_id=1, source_target_pairs={{0,4},{1,5},{2,6},{3,7},{4,0},{5,1},{6,2},{7,3},{8,12},{9,13},{10,... | collective-permute-start | bytes 516104 | tf_op jit(solution)/shard_map/ppermute | solution.py:40
  102.0 2.2 %collective-permute-start.19 = (bf16[352,128]{1,0:T(8,128)(2,1)S(1)}, bf16[352,128]{1,0:T(8,128)(2,1)S(1)}, u32[]{:S(2)}, u32[]{:S(2)}) collective-permute-start(bf16[352,128]{1,0:T(8,128)(2,1)S(1)} %get-tuple-element.99), channel_id=1, source_target_pairs={{0,6},{1,7},{2,0},{3,1},{4,2},{5,3},{6,4},{7,5},{8,14},{9,15},{10,... | collective-permute-start | bytes 270344 | tf_op jit(solution)/shard_map/ppermute | solution.py:40
  104.3 3.2 %collective-permute-done.15.two = bf16[672,128]{1,0:T(8,128)(2,1)S(1)} collective-permute-done((bf16[672,128]{1,0:T(8,128)(2,1)S(1)}, bf16[672,128]{1,0:T(8,128)(2,1)S(1)}, u32[]{:S(2)}, u32[]{:S(2)}) %collective-permute-start.15) | collective-permute-done | bytes 172064 | tf_op jit(solution)/shard_map/ppermute | solution.py:40
  110.9 2.2 %collective-permute-start.22 = (bf16[512,128]{1,0:T(8,128)(2,1)S(1)}, bf16[512,128]{1,0:T(8,128)(2,1)S(1)}, u32[]{:S(2)}, u32[]{:S(2)}) collective-permute-start(bf16[512,128]{1,0:T(8,128)(2,1)S(1)} %get-tuple-element.110), channel_id=1, source_target_pairs={{8,16},{24,32},{40,48},{56,64},{72,80},{88,96},{104,112},{120,128}... | collective-permute-start | bytes 393224 | tf_op jit(solution)/shard_map/ppermute | solution.py:31
  113.1 6.5 %collective-permute-start.21 = (bf16[176,128]{1,0:T(8,128)(2,1)S(1)}, bf16[176,128]{1,0:T(8,128)(2,1)S(1)}, u32[]{:S(2)}, u32[]{:S(2)}) collective-permute-start(bf16[176,128]{1,0:T(8,128)(2,1)S(1)} %get-tuple-element.109), channel_id=1, source_target_pairs={{0,8},{16,24},{32,40},{48,56},{64,72},{80,88},{96,104},{112,120},{... | collective-permute-start | bytes 135176 | tf_op jit(solution)/shard_map/ppermute | solution.py:31
  122.0 2.1 %collective-permute-done.20.early = bf16[336,128]{1,0:T(8,128)(2,1)S(1)} collective-permute-done((bf16[336,128]{1,0:T(8,128)(2,1)S(1)}, bf16[336,128]{1,0:T(8,128)(2,1)S(1)}, u32[]{:S(2)}, u32[]{:S(2)}) %collective-permute-start.20) | collective-permute-done | bytes 86048 | tf_op jit(solution)/shard_map/ppermute | solution.py:31
  (66 shorter events, 29.1 us)
Async XLA Ops:
  4.9 15.7 %collective-permute-start.1 = (bf16[128,1536]{1,0:T(8,128)(2,1)}, bf16[128,1536]{1,0:T(8,128)(2,1)S(1)}, u32[]{:S(2)}, u32[]{:S(2)}) collective-permute-start(bf16[128,1536]{1,0:T(8,128)(2,1)} %get-tuple-element.60), channel_id=1, source_target_pairs={{0,8},{16,24},{32,40},{48,56},{64,72},{80,88},{96,104},{112,120},{... | collective-permute-start | bytes 1179656 | tf_op jit(solution)/shard_map/ppermute | solution.py:31
  6.1 18.1 %collective-permute-start.3 = (bf16[128,1536]{1,0:T(8,128)(2,1)}, bf16[128,1536]{1,0:T(8,128)(2,1)S(1)}, u32[]{:S(2)}, u32[]{:S(2)}) collective-permute-start(bf16[128,1536]{1,0:T(8,128)(2,1)} %get-tuple-element.71), channel_id=1, source_target_pairs={{8,16},{24,32},{40,48},{56,64},{72,80},{88,96},{104,112},{120,128}... | collective-permute-start | bytes 1179656 | tf_op jit(solution)/shard_map/ppermute | solution.py:31
  8.1 18.9 %collective-permute-start = (bf16[128,1536]{1,0:T(8,128)(2,1)S(1)}, bf16[128,1536]{1,0:T(8,128)(2,1)S(1)}, u32[]{:S(2)}, u32[]{:S(2)}) collective-permute-start(bf16[128,1536]{1,0:T(8,128)(2,1)S(1)} %copy-done.11), channel_id=1, source_target_pairs={{0,8},{16,24},{32,40},{48,56},{64,72},{80,88},{96,104},{112,120},{... | collective-permute-start | bytes 1179656 | tf_op jit(solution)/shard_map/ppermute | solution.py:31
  15.7 53.2 %collective-permute-start.4 = (bf16[256,1536]{1,0:T(8,128)(2,1)}, bf16[256,1536]{1,0:T(8,128)(2,1)}, u32[]{:S(2)}, u32[]{:S(2)}) collective-permute-start(bf16[256,1536]{1,0:T(8,128)(2,1)} %get-tuple-element.62), channel_id=1, source_target_pairs={{0,8},{16,24},{32,40},{48,56},{64,72},{80,88},{96,104},{112,120},{... | collective-permute-start | bytes 2359304 | tf_op jit(solution)/shard_map/ppermute | solution.py:31
  15.7 55.1 %collective-permute-start.5 = (bf16[256,1536]{1,0:T(8,128)(2,1)}, bf16[256,1536]{1,0:T(8,128)(2,1)}, u32[]{:S(2)}, u32[]{:S(2)}) collective-permute-start(bf16[256,1536]{1,0:T(8,128)(2,1)} %get-tuple-element.76), channel_id=1, source_target_pairs={{8,16},{24,32},{40,48},{56,64},{72,80},{88,96},{104,112},{120,128}... | collective-permute-start | bytes 2359304 | tf_op jit(solution)/shard_map/ppermute | solution.py:31
  20.7 52.8 %collective-permute-start.6 = (bf16[256,1536]{1,0:T(8,128)(2,1)}, bf16[256,1536]{1,0:T(8,128)(2,1)}, u32[]{:S(2)}, u32[]{:S(2)}) collective-permute-start(bf16[256,1536]{1,0:T(8,128)(2,1)} %get-tuple-element.64), channel_id=1, source_target_pairs={{0,8},{16,24},{32,40},{48,56},{64,72},{80,88},{96,104},{112,120},{... | collective-permute-start | bytes 2359304 | tf_op jit(solution)/shard_map/ppermute | solution.py:31
  25.1 48.4 %collective-permute-start.7 = (bf16[256,1536]{1,0:T(8,128)(2,1)}, bf16[256,1536]{1,0:T(8,128)(2,1)}, u32[]{:S(2)}, u32[]{:S(2)}) collective-permute-start(bf16[256,1536]{1,0:T(8,128)(2,1)} %get-tuple-element.81), channel_id=1, source_target_pairs={{8,16},{24,32},{40,48},{56,64},{72,80},{88,96},{104,112},{120,128}... | collective-permute-start | bytes 2359304 | tf_op jit(solution)/shard_map/ppermute | solution.py:31
  27.8 33.9 %collective-permute-start.2 = (bf16[128,1536]{1,0:T(8,128)(2,1)}, bf16[128,1536]{1,0:T(8,128)(2,1)}, u32[]{:S(2)}, u32[]{:S(2)}) collective-permute-start(bf16[128,1536]{1,0:T(8,128)(2,1)} %get-tuple-element.70), channel_id=1, source_target_pairs={{8,16},{24,32},{40,48},{56,64},{72,80},{88,96},{104,112},{120,128}... | collective-permute-start | bytes 1179656 | tf_op jit(solution)/shard_map/ppermute | solution.py:31
  38.0 28.7 %copy-start.5 = (bf16[128,1536]{1,0:T(8,128)(2,1)S(1)}, bf16[128,1536]{1,0:T(8,128)(2,1)}, u32[]{:S(2)}) copy-start(bf16[128,1536]{1,0:T(8,128)(2,1)} %copy-done.4) | copy-start | bytes 1179652
  61.6 19.6 %collective-permute-start.9 = (bf16[128,1536]{1,0:T(8,128)(2,1)S(1)}, bf16[128,1536]{1,0:T(8,128)(2,1)S(1)}, u32[]{:S(2)}, u32[]{:S(2)}) collective-permute-start(bf16[128,1536]{1,0:T(8,128)(2,1)S(1)} %copy-done.10), channel_id=1, source_target_pairs={{0,8},{16,24},{32,40},{48,56},{64,72},{80,88},{96,104},{112,120},{... | collective-permute-start | bytes 1179656 | tf_op jit(solution)/shard_map/ppermute | solution.py:31
  68.9 12.3 %collective-permute-start.10 = (bf16[128,1536]{1,0:T(8,128)(2,1)S(1)}, bf16[128,1536]{1,0:T(8,128)(2,1)S(1)}, u32[]{:S(2)}, u32[]{:S(2)}) collective-permute-start(bf16[128,1536]{1,0:T(8,128)(2,1)S(1)} %copy-done.9), channel_id=1, source_target_pairs={{8,16},{24,32},{40,48},{56,64},{72,80},{88,96},{104,112},{120,128}... | collective-permute-start | bytes 1179656 | tf_op jit(solution)/shard_map/ppermute | solution.py:31
  76.7 17.1 %collective-permute-start.8 = (bf16[4,672,128]{2,1,0:T(8,128)(2,1)S(1)}, bf16[4,672,128]{2,1,0:T(8,128)(2,1)S(1)}, u32[]{:S(2)}, u32[]{:S(2)}) collective-permute-start(bf16[4,672,128]{2,1,0:T(8,128)(2,1)S(1)} %get-tuple-element.83), channel_id=1, source_target_pairs={{0,1},{1,0},{2,3},{3,2},{4,5},{5,4},{6,7},{7,6},{8,9},{9,8},{10,11... | collective-permute-start | bytes 2064392 | tf_op jit(solution)/shard_map/ppermute | solution.py:35
  76.8 12.0 %collective-permute-start.11 = (bf16[128,1536]{1,0:T(8,128)(2,1)S(1)}, bf16[128,1536]{1,0:T(8,128)(2,1)S(1)}, u32[]{:S(2)}, u32[]{:S(2)}) collective-permute-start(bf16[128,1536]{1,0:T(8,128)(2,1)S(1)} %copy-done.8), channel_id=1, source_target_pairs={{0,8},{16,24},{32,40},{48,56},{64,72},{80,88},{96,104},{112,120},{... | collective-permute-start | bytes 1179656 | tf_op jit(solution)/shard_map/ppermute | solution.py:31
  79.1 13.0 %collective-permute-start.12 = (bf16[128,1536]{1,0:T(8,128)(2,1)S(1)}, bf16[128,1536]{1,0:T(8,128)(2,1)S(1)}, u32[]{:S(2)}, u32[]{:S(2)}) collective-permute-start(bf16[128,1536]{1,0:T(8,128)(2,1)S(1)} %copy-done.7), channel_id=1, source_target_pairs={{8,16},{24,32},{40,48},{56,64},{72,80},{88,96},{104,112},{120,128}... | collective-permute-start | bytes 1179656 | tf_op jit(solution)/shard_map/ppermute | solution.py:31
  93.7 6.2 %collective-permute-start.13 = (bf16[4,352,128]{2,1,0:T(8,128)(2,1)S(1)}, bf16[4,352,128]{2,1,0:T(8,128)(2,1)S(1)}, u32[]{:S(2)}, u32[]{:S(2)}) collective-permute-start(bf16[4,352,128]{2,1,0:T(8,128)(2,1)S(1)} %get-tuple-element.96), channel_id=1, source_target_pairs={{0,1},{1,0},{2,3},{3,2},{4,5},{5,4},{6,7},{7,6},{8,9},{9,8},{10,11... | collective-permute-start | bytes 1081352 | tf_op jit(solution)/shard_map/ppermute | solution.py:35
  93.9 8.1 %collective-permute-start.14 = (bf16[672,128]{1,0:T(8,128)(2,1)S(1)}, bf16[672,128]{1,0:T(8,128)(2,1)S(1)}, u32[]{:S(2)}, u32[]{:S(2)}) collective-permute-start(bf16[672,128]{1,0:T(8,128)(2,1)S(1)} %get-tuple-element.101), channel_id=1, source_target_pairs={{0,2},{1,3},{2,4},{3,5},{4,6},{5,7},{6,0},{7,1},{8,10},{9,11},{10,... | collective-permute-start | bytes 516104 | tf_op jit(solution)/shard_map/ppermute | solution.py:40
  95.6 11.9 %collective-permute-start.15 = (bf16[672,128]{1,0:T(8,128)(2,1)S(1)}, bf16[672,128]{1,0:T(8,128)(2,1)S(1)}, u32[]{:S(2)}, u32[]{:S(2)}) collective-permute-start(bf16[672,128]{1,0:T(8,128)(2,1)S(1)} %get-tuple-element.102), channel_id=1, source_target_pairs={{0,4},{1,5},{2,6},{3,7},{4,0},{5,1},{6,2},{7,3},{8,12},{9,13},{10,... | collective-permute-start | bytes 516104 | tf_op jit(solution)/shard_map/ppermute | solution.py:40
  98.5 9.0 %collective-permute-start.16 = (bf16[672,128]{1,0:T(8,128)(2,1)S(1)}, bf16[672,128]{1,0:T(8,128)(2,1)S(1)}, u32[]{:S(2)}, u32[]{:S(2)}) collective-permute-start(bf16[672,128]{1,0:T(8,128)(2,1)S(1)} %get-tuple-element.103), channel_id=1, source_target_pairs={{0,6},{1,7},{2,0},{3,1},{4,2},{5,3},{6,4},{7,5},{8,14},{9,15},{10,... | collective-permute-start | bytes 516104 | tf_op jit(solution)/shard_map/ppermute | solution.py:40
  99.9 9.1 %collective-permute-start.17 = (bf16[352,128]{1,0:T(8,128)(2,1)S(1)}, bf16[352,128]{1,0:T(8,128)(2,1)S(1)}, u32[]{:S(2)}, u32[]{:S(2)}) collective-permute-start(bf16[352,128]{1,0:T(8,128)(2,1)S(1)} %get-tuple-element.97), channel_id=1, source_target_pairs={{0,2},{1,3},{2,4},{3,5},{4,6},{5,7},{6,0},{7,1},{8,10},{9,11},{10,... | collective-permute-start | bytes 270344 | tf_op jit(solution)/shard_map/ppermute | solution.py:40
  100.7 10.1 %collective-permute-start.18 = (bf16[352,128]{1,0:T(8,128)(2,1)S(1)}, bf16[352,128]{1,0:T(8,128)(2,1)S(1)}, u32[]{:S(2)}, u32[]{:S(2)}) collective-permute-start(bf16[352,128]{1,0:T(8,128)(2,1)S(1)} %get-tuple-element.98), channel_id=1, source_target_pairs={{0,4},{1,5},{2,6},{3,7},{4,0},{5,1},{6,2},{7,3},{8,12},{9,13},{10,... | collective-permute-start | bytes 270344 | tf_op jit(solution)/shard_map/ppermute | solution.py:40
  102.0 8.8 %collective-permute-start.19 = (bf16[352,128]{1,0:T(8,128)(2,1)S(1)}, bf16[352,128]{1,0:T(8,128)(2,1)S(1)}, u32[]{:S(2)}, u32[]{:S(2)}) collective-permute-start(bf16[352,128]{1,0:T(8,128)(2,1)S(1)} %get-tuple-element.99), channel_id=1, source_target_pairs={{0,6},{1,7},{2,0},{3,1},{4,2},{5,3},{6,4},{7,5},{8,14},{9,15},{10,... | collective-permute-start | bytes 270344 | tf_op jit(solution)/shard_map/ppermute | solution.py:40
  110.9 13.2 %collective-permute-start.22 = (bf16[512,128]{1,0:T(8,128)(2,1)S(1)}, bf16[512,128]{1,0:T(8,128)(2,1)S(1)}, u32[]{:S(2)}, u32[]{:S(2)}) collective-permute-start(bf16[512,128]{1,0:T(8,128)(2,1)S(1)} %get-tuple-element.110), channel_id=1, source_target_pairs={{8,16},{24,32},{40,48},{56,64},{72,80},{88,96},{104,112},{120,128}... | collective-permute-start | bytes 393224 | tf_op jit(solution)/shard_map/ppermute | solution.py:31
  113.1 8.9 %collective-permute-start.21 = (bf16[176,128]{1,0:T(8,128)(2,1)S(1)}, bf16[176,128]{1,0:T(8,128)(2,1)S(1)}, u32[]{:S(2)}, u32[]{:S(2)}) collective-permute-start(bf16[176,128]{1,0:T(8,128)(2,1)S(1)} %get-tuple-element.109), channel_id=1, source_target_pairs={{0,8},{16,24},{32,40},{48,56},{64,72},{80,88},{96,104},{112,120},{... | collective-permute-start | bytes 135176 | tf_op jit(solution)/shard_map/ppermute | solution.py:31
  119.6 4.5 %collective-permute-start.20 = (bf16[336,128]{1,0:T(8,128)(2,1)S(1)}, bf16[336,128]{1,0:T(8,128)(2,1)S(1)}, u32[]{:S(2)}, u32[]{:S(2)}) collective-permute-start(bf16[336,128]{1,0:T(8,128)(2,1)S(1)} %get-tuple-element.108), channel_id=1, source_target_pairs={{0,8},{16,24},{32,40},{48,56},{64,72},{80,88},{96,104},{112,120},{... | collective-permute-start | bytes 258056 | tf_op jit(solution)/shard_map/ppermute | solution.py:31
  (11 other events, 102.9 us)
